TPU v7x, 32 devices: a whole 2x2x4 slice. The times are simulated.
32 devices in a mesh: groups: 2 (over x), expert: 16 (over z, y, core).
Axes of the slice: x: 2, y: 2, z: 4, core: 2. Of those that a mesh axis runs over, the one named last changes fastest.
Arguments:
- tokens: bfloat16 [2048, 2048], P(('groups', 'expert')), parts along dimension 0, may hold values from -6 to 6
- grad_out: bfloat16 [2048, 2048], P(('groups', 'expert')), parts along dimension 0, may hold values from -3 to 3
- expert_ids: int32 [2048, 4], P(('groups', 'expert')), parts along dimension 0, may hold values from 0 to 7, as said below
- router_weight: bfloat16 [2048, 8], replicated, may hold values from -0.125 to 0.125
- gate_weight: bfloat16 [16, 2048, 384], P('expert'), may hold values from -0.125 to 0.125
- up_weight: bfloat16 [16, 2048, 384], P('expert'), may hold values from -0.125 to 0.125
- down_weight: bfloat16 [16, 384, 2048], P('expert'), may hold values from -0.21875 to 0.21875
Outputs:
- mixed: bfloat16 [2048, 2048], P(('groups', 'expert')), parts along dimension 0
- token_grad: bfloat16 [2048, 2048], P(('groups', 'expert')), parts along dimension 0
- gate_grad: bfloat16 [32, 2048, 384], P(('groups', 'expert')), parts along dimension 0
- up_grad: bfloat16 [32, 2048, 384], P(('groups', 'expert')), parts along dimension 0
- down_grad: bfloat16 [32, 384, 2048], P(('groups', 'expert')), parts along dimension 0
- router_grad: float32 [4096, 8], P(('groups', 'expert')), parts along dimension 0
There are 2 independent parts, one for each index of `groups`. A program takes and returns all parts, laid end to end along the dimension named above; an argument that names none is the same for every part. Nothing has to cross between parts.
Inputs may be any that keep to these rules, and one draw needn't show every extreme that they name: `expert_ids`: each token names 4 different experts. In each aligned block of 32 tokens (either half of one device's tokens) no expert is named by more than 32 tokens, and some expert by exactly 32 in every block.
All inputs are finite; a program needn't handle non-finite values.
Results may differ from a plain program's by a relative error of at most 0.009.
Values may be sent and summed in bfloat16 or wider, within the bound.
No kernel may reach another device: no remote copies, remote signals or barrier semaphores. Data moves between devices by JAX's collectives and lax.ppermute only.
A program may use at most 128 MiB of HBM per device.

v0:
```python
import jax
import jax.numpy as jnp
from jax import lax
from jax.sharding import PartitionSpec as P


def from_partner(value, axis, distance):
    mask = 2**distance
    pairs = [(source, source ^ mask) for source in range(lax.axis_size(axis))]
    return lax.ppermute(value, axis, pairs)


def expert_pass(rows, grads, gate_full, up_full, down_full):
    pre_gate = jnp.dot(rows, gate_full, preferred_element_type=jnp.float32)
    pre_up = jnp.dot(rows, up_full, preferred_element_type=jnp.float32)
    squash = jax.nn.sigmoid(pre_gate)
    activated = pre_gate * squash
    hidden = (activated * pre_up).astype(jnp.bfloat16)
    partial_out = jnp.dot(hidden, down_full, preferred_element_type=jnp.float32)
    back_hidden = jnp.dot(grads, down_full.T, preferred_element_type=jnp.float32)
    gate_delta = (back_hidden * pre_up * squash * (1.0 + pre_gate * (1.0 - squash))).astype(
        jnp.bfloat16
    )
    up_delta = (back_hidden * activated).astype(jnp.bfloat16)
    partial_back = jnp.dot(gate_delta, gate_full.T, preferred_element_type=jnp.float32)
    partial_back = partial_back + jnp.dot(up_delta, up_full.T, preferred_element_type=jnp.float32)
    return (partial_out, partial_back, hidden, gate_delta, up_delta)


def rounded_term(left, right):
    return (
        jnp.dot(left.T, right, preferred_element_type=jnp.float32)
        .astype(jnp.bfloat16)
        .astype(jnp.float32)
    )


def on_device(tokens, grad_out, expert_ids, router_weight, gate_weight, up_weight, down_weight):
    devices = lax.axis_size("expert")
    token_count, model_width = tokens.shape
    per_token = expert_ids.shape[1]
    experts = router_weight.shape[1]
    halfway = token_count // 2
    capacity = 2 * token_count * per_token // devices
    slot_total = devices * capacity
    pair_count = token_count * per_token
    onehot = expert_ids[:, :, None] == jnp.arange(experts, dtype=jnp.int32)[None, None, :]
    logits = jnp.dot(tokens, router_weight, preferred_element_type=jnp.float32)
    chosen = jnp.sum(jnp.where(onehot, logits[:, None, :], 0.0), axis=2)
    probability = jax.nn.sigmoid(chosen)
    summed = jnp.sum(probability, axis=1, keepdims=True)
    gate_share = probability / summed
    scaled = (gate_share[:, :, None] * grad_out[:, None, :].astype(jnp.float32)).astype(
        jnp.bfloat16
    )
    scaled = scaled.reshape(pair_count, model_width)
    matches = onehot.astype(jnp.int32).reshape(2, halfway * per_token, experts)
    before = jnp.cumsum(matches, axis=1) - matches
    position = jnp.sum(before * matches, axis=2).reshape(token_count, per_token)
    parity = (jnp.arange(token_count, dtype=jnp.int32) // halfway)[:, None]
    target = ((2 * expert_ids + parity) * capacity + position).reshape(pair_count)
    source = (
        jnp.full((slot_total,), pair_count, jnp.int32)
        .at[target]
        .set(jnp.arange(pair_count, dtype=jnp.int32))
    )
    filled = (source < pair_count)[:, None]
    clipped = jnp.minimum(source, pair_count - 1)
    row_buffer = jnp.where(filled, jnp.take(tokens, clipped // per_token, axis=0), 0.0)
    grad_buffer = jnp.where(filled, jnp.take(scaled, clipped, axis=0), 0.0)
    row_buffer = row_buffer.reshape(devices, capacity, model_width)
    grad_buffer = grad_buffer.reshape(devices, capacity, model_width)
    rows_in, grads_in = (
        lax.all_to_all(row_buffer, "expert", split_axis=0, concat_axis=0, tiled=True),
        lax.all_to_all(grad_buffer, "expert", split_axis=0, concat_axis=0, tiled=True),
    )
    rows_in = rows_in.reshape(slot_total, model_width)
    grads_in = grads_in.reshape(slot_total, model_width)
    gate_own, up_own, down_own = (gate_weight[0], up_weight[0], down_weight[0])
    other_rows, other_grads = from_partner((rows_in, grads_in), "expert", 0)
    both_rows = jnp.concatenate([rows_in, other_rows], axis=0)
    both_grads = jnp.concatenate([grads_in, other_grads], axis=0)
    partial_out, partial_back, hidden, gate_delta, up_delta = expert_pass(
        both_rows, both_grads, gate_own, up_own, down_own
    )
    got_out, got_back = (
        from_partner(partial_out[slot_total:].astype(jnp.bfloat16), "expert", 0).astype(
            jnp.float32
        ),
        from_partner(partial_back[slot_total:].astype(jnp.bfloat16), "expert", 0).astype(
            jnp.float32
        ),
    )
    out_rows = (partial_out[:slot_total] + got_out).astype(jnp.bfloat16)
    back_rows = (partial_back[:slot_total] + got_back).astype(jnp.bfloat16)
    gate_sum = rounded_term(rows_in, gate_delta[:slot_total]) + rounded_term(
        other_rows, gate_delta[slot_total:]
    )
    up_sum = rounded_term(rows_in, up_delta[:slot_total]) + rounded_term(
        other_rows, up_delta[slot_total:]
    )
    down_sum = rounded_term(hidden[:slot_total], grads_in) + rounded_term(
        hidden[slot_total:], other_grads
    )
    gate_grad = gate_sum.astype(jnp.bfloat16)[None]
    up_grad = up_sum.astype(jnp.bfloat16)[None]
    down_grad = down_sum.astype(jnp.bfloat16)[None]
    out_back, grad_back = (
        lax.all_to_all(
            out_rows.reshape(devices, capacity, model_width),
            "expert",
            split_axis=0,
            concat_axis=0,
            tiled=True,
        ),
        lax.all_to_all(
            back_rows.reshape(devices, capacity, model_width),
            "expert",
            split_axis=0,
            concat_axis=0,
            tiled=True,
        ),
    )
    expert_out = jnp.take(out_back.reshape(slot_total, model_width), target, axis=0)
    expert_out = expert_out.reshape(token_count, per_token, model_width).astype(jnp.float32)
    expert_back = jnp.take(grad_back.reshape(slot_total, model_width), target, axis=0)
    expert_back = expert_back.reshape(token_count, per_token, model_width).astype(jnp.float32)
    mixed = jnp.sum(gate_share[:, :, None] * expert_out, axis=1).astype(jnp.bfloat16)
    gate_slope = jnp.sum(grad_out[:, None, :].astype(jnp.float32) * expert_out, axis=2)
    prob_slope = (gate_slope - jnp.sum(gate_share * gate_slope, axis=1, keepdims=True)) / summed
    logit_slope = prob_slope * probability * (1.0 - probability)
    router_delta = jnp.sum(jnp.where(onehot, logit_slope[:, :, None], 0.0), axis=1).astype(
        jnp.bfloat16
    )
    token_grad = jnp.sum(expert_back, axis=1) + jnp.dot(
        router_delta, router_weight.T, preferred_element_type=jnp.float32
    )
    token_grad = token_grad.astype(jnp.bfloat16)
    router_grad = lax.psum_scatter(
        lax.dot_general(
            tokens, router_delta, (((0,), (0,)), ((), ())), preferred_element_type=jnp.float32
        ),
        "expert",
        scatter_dimension=0,
        tiled=True,
    )
    return (mixed, token_grad, gate_grad, up_grad, down_grad, router_grad)


def solution(mesh):
    return jax.shard_map(
        on_device,
        mesh=mesh,
        in_specs=(
            P(("groups", "expert"), None),
            P(("groups", "expert"), None),
            P(("groups", "expert"), None),
            P(),
            P("expert", None, None),
            P("expert", None, None),
            P("expert", None, None),
        ),
        out_specs=(
            P(("groups", "expert"), None),
            P(("groups", "expert"), None),
            P(("groups", "expert"), None, None),
            P(("groups", "expert"), None, None),
            P(("groups", "expert"), None, None),
            P(("groups", "expert"), None),
        ),
        check_vma=False,
    )
```

profile of v0, /device:TPU:13, one launch (start us, length us, event | category | flops | bytes accessed | tf_op | source)
XLA Modules:
  0.0 308.7 jit_solution(7346292753936989190)
XLA Ops:
  7.2 0.9 copy.32
  8.9 0.7 multiply_add_fusion
  9.8 1.4 scatter_custom_fusion
  11.4 3.3 %gather_fusion = bf16[512,2048]{1,0:T(8,128)(2,1)} fusion(bf16[64,2048]{1,0:T(8,128)(2,1)S(1)} %copy-done.2, s32[1024]{0:T(1024)S(1)} %pad_clamp_fusion.2), kind=kCustom, calls=%fused_computation.2 | custom fusion | bytes 4196352 | tf_op jit(solution)/shard_map/jit(_take)/gather | solution.py:69
  14.8 1.9 select_select_fusion.1
  16.7 53.8 %all_to_all.20 = bf16[16,32,2048]{2,1,0:T(8,128)(2,1)S(1)} all-to-all(bf16[16,32,2048]{2,1,0:T(8,128)(2,1)S(1)} %select_select_fusion.1), channel_id=1, replica_groups=mesh['groups'=2,'expert'=16] {'expert'}, dimensions={0} | all-to-all | bytes 4194304 | tf_op jit(solution)/shard_map/all_to_all | solution.py:74
  70.7 3.9 %collective-permute-done = bf16[512,2048]{1,0:T(8,128)(2,1)S(1)} collective-permute-done((bf16[512,2048]{1,0:T(8,128)(2,1)S(1)}, bf16[512,2048]{1,0:T(8,128)(2,1)S(1)}, u32[]{:S(2)}, u32[]{:S(2)}) %collective-permute-start) | collective-permute-done | bytes 2097184 | tf_op jit(solution)/shard_map/ppermute | solution.py:10
  74.7 2.3 fusion.7
  77.0 3.5 %multiply_convert_fusion.3 = (bf16[1024,384]{1,0:T(8,128)(2,1)S(1)}, f32[1024,384]{1,0:T(8,128)}) fusion(f32[1024,384]{1,0:T(8,128)S(1)} %fusion.7, bf16[1,2048,384]{2,1,0:T(8,128)(2,1)S(1)} %copy-done.10, bf16[512,2048]{1,0:T(8,128)(2,1)S(1)} %collective-permute-done, bf16[512,2048]{1,0:T(8,128)(2,1)S(1)} %bitcast.57), kind=kOutput, calls=%fused_computation.49 | convolution fusion | flops 1621360640 | bytes 9699328 | tf_op jit(solution)/shard_map/dot_general | solution.py:15
  80.5 2.3 fusion.13
  82.9 0.3 slice.81
  83.2 0.3 collective-permute-start.1
  83.5 3.9 %collective-permute-done.1 = bf16[512,2048]{1,0:T(8,128)(2,1)S(1)} collective-permute-done((bf16[512,2048]{1,0:T(8,128)(2,1)S(1)}, bf16[512,2048]{1,0:T(8,128)(2,1)S(1)}, u32[]{:S(2)}, u32[]{:S(2)}) %collective-permute-start.1) | collective-permute-done | bytes 2097184 | tf_op jit(solution)/shard_map/ppermute | solution.py:10
  87.4 2.1 fusion.1
  89.5 5.3 %all-to-all-start.1 = ((bf16[16,32,2048]{2,1,0:T(8,128)(2,1)}), bf16[16,32,2048]{2,1,0:T(8,128)(2,1)}, u32[]{:S(2)}, u32[]{:S(2)}) async-start(bf16[16,32,2048]{2,1,0:T(8,128)(2,1)} %bitcast.54), calls=%async_computation.1 | async-start | bytes 4194304 | tf_op jit(solution)/shard_map/all_to_all | solution.py:109
  94.9 1.8 mul.94
  96.7 3.0 mul.95
  100.1 42.2 %all-to-all-done.1 = bf16[16,32,2048]{2,1,0:T(8,128)(2,1)} async-done(((bf16[16,32,2048]{2,1,0:T(8,128)(2,1)}), bf16[16,32,2048]{2,1,0:T(8,128)(2,1)}, u32[]{:S(2)}, u32[]{:S(2)}) %all-to-all-start.1) | async-done | bytes 2097184 | tf_op jit(solution)/shard_map/all_to_all | solution.py:109
  142.3 4.2 %gather_fusion.2 = bf16[256,2048]{1,0:T(8,128)(2,1)S(1)} fusion(bf16[512,2048]{1,0:T(8,128)(2,1)} %bitcast.7, s32[1024]{0:T(1024)S(1)} %pad_clamp_fusion.1), kind=kCustom, calls=%fused_computation.clone | custom fusion | bytes 2098176 | tf_op jit(solution)/shard_map/jit(_take)/gather | solution.py:124
  146.6 2.4 multiply_reduce_fusion
  149.4 1.8 multiply_convert_fusion
  151.2 3.3 %gather_fusion.1 = bf16[512,2048]{1,0:T(8,128)(2,1)} fusion(bf16[256,2048]{1,0:T(8,128)(2,1)S(1)} %multiply_convert_fusion, s32[1024]{0:T(1024)S(1)} %pad_clamp_fusion), kind=kCustom, calls=%fused_computation.3 | custom fusion | bytes 4196352 | tf_op jit(solution)/shard_map/jit(_take)/gather | solution.py:70
  154.5 1.9 select_select_fusion
  156.4 52.3 %all_to_all.21 = bf16[16,32,2048]{2,1,0:T(8,128)(2,1)S(1)} all-to-all(bf16[16,32,2048]{2,1,0:T(8,128)(2,1)S(1)} %select_select_fusion), channel_id=1, replica_groups=mesh['groups'=2,'expert'=16] {'expert'}, dimensions={0} | all-to-all | bytes 4194304 | tf_op jit(solution)/shard_map/all_to_all | solution.py:75
  208.9 3.9 %collective-permute-done.2 = bf16[512,2048]{1,0:T(8,128)(2,1)S(1)} collective-permute-done((bf16[512,2048]{1,0:T(8,128)(2,1)S(1)}, bf16[512,2048]{1,0:T(8,128)(2,1)S(1)}, u32[]{:S(2)}, u32[]{:S(2)}) %collective-permute-start.2) | collective-permute-done | bytes 2097184 | tf_op jit(solution)/shard_map/ppermute | solution.py:10
  212.9 4.2 %multiply_convert_fusion.1 = (bf16[1024,384]{1,0:T(8,128)(2,1)S(1)}, bf16[1024,384]{1,0:T(8,128)(2,1)S(1)}) fusion(f32[1024,384]{1,0:T(8,128)S(1)} %copy-done.22, f32[1024,384]{1,0:T(8,128)S(1)} %copy-done.23, bf16[1,384,2048]{2,1,0:T(8,128)(2,1)S(1)} %copy-done, bf16[512,2048]{1,0:T(8,128)(2,1)S(1)} %collective-permute-done.2, ...), kind=kOutput, calls=%fused_computation.47 | convolution fusion | flops 1624113152 | bytes 10485760 | tf_op jit(solution)/shard_map/dot_general | solution.py:20
  217.1 2.4 fusion.17
  219.5 2.5 convolution_add_fusion
  221.9 0.3 slice.80
  222.2 0.3 collective-permute-start.3
  222.5 3.9 %collective-permute-done.3 = bf16[512,2048]{1,0:T(8,128)(2,1)S(1)} collective-permute-done((bf16[512,2048]{1,0:T(8,128)(2,1)S(1)}, bf16[512,2048]{1,0:T(8,128)(2,1)S(1)}, u32[]{:S(2)}, u32[]{:S(2)}) %collective-permute-start.3) | collective-permute-done | bytes 2097184 | tf_op jit(solution)/shard_map/ppermute | solution.py:10
  226.5 2.1 fusion
  228.6 5.3 %all-to-all-start.3 = ((bf16[16,32,2048]{2,1,0:T(8,128)(2,1)}), bf16[16,32,2048]{2,1,0:T(8,128)(2,1)}, u32[]{:S(2)}, u32[]{:S(2)}) async-start(bf16[16,32,2048]{2,1,0:T(8,128)(2,1)} %bitcast.53), calls=%async_computation.3 | async-start | bytes 4194304 | tf_op jit(solution)/shard_map/all_to_all | solution.py:116
  233.9 0.8 convolution_bitcast_fusion
  234.7 2.7 convolution_convert_fusion.1
  237.5 1.3 convolution_convert_fusion.3
  238.8 1.3 convolution_convert_fusion.5
  240.4 2.2 fusion.10
  242.6 2.5 fusion.9
  245.1 2.5 fusion.8
  247.5 34.1 %all-to-all-done.3 = bf16[16,32,2048]{2,1,0:T(8,128)(2,1)} async-done(((bf16[16,32,2048]{2,1,0:T(8,128)(2,1)}), bf16[16,32,2048]{2,1,0:T(8,128)(2,1)}, u32[]{:S(2)}, u32[]{:S(2)}) %all-to-all-start.3) | async-done | bytes 2097184 | tf_op jit(solution)/shard_map/all_to_all | solution.py:116
  281.6 4.3 %gather_fusion.3 = bf16[256,2048]{1,0:T(8,128)(2,1)S(1)} fusion(bf16[512,2048]{1,0:T(8,128)(2,1)} %bitcast.11, s32[1024]{0:T(1024)S(1)} %pad_clamp_fusion.1), kind=kCustom, calls=%fused_computation.1.clone | custom fusion | bytes 2098176 | tf_op jit(solution)/shard_map/jit(_take)/gather | solution.py:126
  285.9 2.3 select_convert_fusion
  288.3 2.9 reshape.221
  291.1 2.9 reduce_sum.78
  294.1 1.0 fusion.11
  295.0 3.0 reshape.218
  298.0 3.9 %multiply_reduce_fusion.1 = bf16[64,2048]{1,0:T(8,128)(2,1)} fusion(f32[64,4,2048]{2,1,0:T(4,128)} %reshape.218, f32[64,4]{1,0:T(8,128)S(1)} %copy.31), kind=kLoop, calls=%fused_computation.37 | loop fusion | flops 917504 | bytes 2360320 | tf_op jit(solution)/shard_map/reduce_sum | solution.py:128
  (85 shorter events, 2.9 us)
Async XLA Ops:
  7.2 73.4 %copy-start = (bf16[1,384,2048]{2,1,0:T(8,128)(2,1)S(1)}, bf16[1,384,2048]{2,1,0:T(8,128)(2,1)}, u32[]{:S(2)}) copy-start(bf16[1,384,2048]{2,1,0:T(8,128)(2,1)} %param.15) | copy-start | bytes 4718596
  7.2 4.2 %copy-start.2 = (bf16[64,2048]{1,0:T(8,128)(2,1)S(1)}, bf16[64,2048]{1,0:T(8,128)(2,1)}, u32[]{:S(2)}) copy-start(bf16[64,2048]{1,0:T(8,128)(2,1)} %param.9) | copy-start | bytes 786436
  16.7 58.0 %copy-start.8 = (bf16[1,2048,384]{2,1,0:T(8,128)(2,1)S(1)}, bf16[1,2048,384]{2,1,0:T(8,128)(2,1)}, u32[]{:S(2)}) copy-start(bf16[1,2048,384]{2,1,0:T(8,128)(2,1)} %param.13) | copy-start | bytes 4718596
  70.5 6.5 %copy-start.5 = (bf16[16,32,2048]{2,1,0:T(8,128)(2,1)}, bf16[16,32,2048]{2,1,0:T(8,128)(2,1)S(1)}, u32[]{:S(2)}) copy-start(bf16[16,32,2048]{2,1,0:T(8,128)(2,1)S(1)} %all_to_all.20) | copy-start | bytes 6291460
  70.5 6.5 %copy-start.10 = (bf16[1,2048,384]{2,1,0:T(8,128)(2,1)S(1)}, bf16[1,2048,384]{2,1,0:T(8,128)(2,1)}, u32[]{:S(2)}) copy-start(bf16[1,2048,384]{2,1,0:T(8,128)(2,1)} %param.14) | copy-start | bytes 4718596
  70.5 4.2 %collective-permute-start = (bf16[512,2048]{1,0:T(8,128)(2,1)S(1)}, bf16[512,2048]{1,0:T(8,128)(2,1)S(1)}, u32[]{:S(2)}, u32[]{:S(2)}) collective-permute-start(bf16[512,2048]{1,0:T(8,128)(2,1)S(1)} %bitcast.55), channel_id=1, source_target_pairs={{0,1},{1,0},{2,3},{3,2},{4,5},{5,4},{6,7},{7,6},{8,9},{9,8},{10,11... | collective-permute-start | bytes 6291464 | tf_op jit(solution)/shard_map/ppermute | solution.py:10
  74.7 2.3 copy-start.17
  77.0 3.5 %copy-start.21 = (f32[1024,384]{1,0:T(8,128)}, f32[1024,384]{1,0:T(8,128)S(1)}, u32[]{:S(2)}) copy-start(f32[1024,384]{1,0:T(8,128)S(1)} %fusion.7) | copy-start | bytes 4718596
  80.5 2.3 copy-start.12
  83.2 4.2 %collective-permute-start.1 = (bf16[512,2048]{1,0:T(8,128)(2,1)S(1)}, bf16[512,2048]{1,0:T(8,128)(2,1)S(1)}, u32[]{:S(2)}, u32[]{:S(2)}) collective-permute-start(bf16[512,2048]{1,0:T(8,128)(2,1)S(1)} %slice.81), channel_id=1, source_target_pairs={{0,1},{1,0},{2,3},{3,2},{4,5},{5,4},{6,7},{7,6},{8,9},{9,8},{10,11... | collective-permute-start | bytes 6291464 | tf_op jit(solution)/shard_map/ppermute | solution.py:10
  89.5 5.4 %copy-start.14 = (bf16[64,2048]{1,0:T(8,128)(2,1)S(1)}, bf16[64,2048]{1,0:T(8,128)(2,1)}, u32[]{:S(2)}) copy-start(bf16[64,2048]{1,0:T(8,128)(2,1)} %param.10) | copy-start | bytes 786436
  89.5 52.8 %all-to-all-start.1 = ((bf16[16,32,2048]{2,1,0:T(8,128)(2,1)}), bf16[16,32,2048]{2,1,0:T(8,128)(2,1)}, u32[]{:S(2)}, u32[]{:S(2)}) async-start(bf16[16,32,2048]{2,1,0:T(8,128)(2,1)} %bitcast.54), calls=%async_computation.1 | async-start | bytes 4194304 | tf_op jit(solution)/shard_map/all_to_all | solution.py:109
  96.7 3.1 %copy-start.15 = (bf16[2048,8]{0,1:T(8,128)(2,1)S(1)}, bf16[2048,8]{0,1:T(8,128)(2,1)}, u32[]{:S(2)}) copy-start(bf16[2048,8]{0,1:T(8,128)(2,1)} %param.12) | copy-start | bytes 98308
  96.7 3.3 %copy-start.16 = (s32[64,4]{0,1:T(4,128)S(1)}, s32[64,4]{0,1:T(4,128)}, u32[]{:S(2)}) copy-start(s32[64,4]{0,1:T(4,128)} %param.11) | copy-start | bytes 3076
  146.5 2.7 copy-start.3
  156.4 56.5 %copy-start.22 = (f32[1024,384]{1,0:T(8,128)S(1)}, f32[1024,384]{1,0:T(8,128)}, u32[]{:S(2)}) copy-start(f32[1024,384]{1,0:T(8,128)} %copy-done.21) | copy-start | bytes 4718596
  156.4 56.5 %copy-start.23 = (f32[1024,384]{1,0:T(8,128)S(1)}, f32[1024,384]{1,0:T(8,128)}, u32[]{:S(2)}) copy-start(f32[1024,384]{1,0:T(8,128)} %get-tuple-element.18) | copy-start | bytes 4718596
  208.7 8.3 %copy-start.7 = (bf16[16,32,2048]{2,1,0:T(8,128)(2,1)}, bf16[16,32,2048]{2,1,0:T(8,128)(2,1)S(1)}, u32[]{:S(2)}) copy-start(bf16[16,32,2048]{2,1,0:T(8,128)(2,1)S(1)} %all_to_all.21) | copy-start | bytes 6291460
  208.7 4.2 %collective-permute-start.2 = (bf16[512,2048]{1,0:T(8,128)(2,1)S(1)}, bf16[512,2048]{1,0:T(8,128)(2,1)S(1)}, u32[]{:S(2)}, u32[]{:S(2)}) collective-permute-start(bf16[512,2048]{1,0:T(8,128)(2,1)S(1)} %bitcast.60), channel_id=1, source_target_pairs={{0,1},{1,0},{2,3},{3,2},{4,5},{5,4},{6,7},{7,6},{8,9},{9,8},{10,11... | collective-permute-start | bytes 6291464 | tf_op jit(solution)/shard_map/ppermute | solution.py:10
  212.9 4.2 %copy-start.19 = (bf16[512,2048]{1,0:T(8,128)(2,1)}, bf16[512,2048]{1,0:T(8,128)(2,1)S(1)}, u32[]{:S(2)}) copy-start(bf16[512,2048]{1,0:T(8,128)(2,1)S(1)} %collective-permute-done.2) | copy-start | bytes 6291460
  212.9 4.2 %copy-start.9 = (bf16[1,2048,384]{2,1,0:T(8,128)(2,1)S(1)}, bf16[1,2048,384]{2,1,0:T(8,128)(2,1)}, u32[]{:S(2)}) copy-start(bf16[1,2048,384]{2,1,0:T(8,128)(2,1)} %param.13) | copy-start | bytes 4718596
  217.1 2.4 copy-start.11
  222.2 4.2 %collective-permute-start.3 = (bf16[512,2048]{1,0:T(8,128)(2,1)S(1)}, bf16[512,2048]{1,0:T(8,128)(2,1)S(1)}, u32[]{:S(2)}, u32[]{:S(2)}) collective-permute-start(bf16[512,2048]{1,0:T(8,128)(2,1)S(1)} %slice.80), channel_id=1, source_target_pairs={{0,1},{1,0},{2,3},{3,2},{4,5},{5,4},{6,7},{7,6},{8,9},{9,8},{10,11... | collective-permute-start | bytes 6291464 | tf_op jit(solution)/shard_map/ppermute | solution.py:10
  228.6 6.1 %copy-start.13 = (bf16[1024,384]{1,0:T(8,128)(2,1)S(1)}, bf16[1024,384]{1,0:T(8,128)(2,1)}, u32[]{:S(2)}) copy-start(bf16[1024,384]{1,0:T(8,128)(2,1)} %copy-done.12) | copy-start | bytes 2359300
  228.6 53.0 %all-to-all-start.3 = ((bf16[16,32,2048]{2,1,0:T(8,128)(2,1)}), bf16[16,32,2048]{2,1,0:T(8,128)(2,1)}, u32[]{:S(2)}, u32[]{:S(2)}) async-start(bf16[16,32,2048]{2,1,0:T(8,128)(2,1)} %bitcast.53), calls=%async_computation.3 | async-start | bytes 4194304 | tf_op jit(solution)/shard_map/all_to_all | solution.py:116
  233.8 68.0 %reduce-scatter.2.cloned.1.call-start = ((), (), s32[]{:S(2)}) async-start(), calls=%async_computation.5 | async-start | bytes 69632 | tf_op jit(solution)/shard_map/reduce_scatter | solution.py:139
  234.7 2.8 copy-start.6
  238.8 1.6 copy-start.20
  240.4 2.2 copy-start.18
  281.6 4.3 %copy-start.4 = (bf16[256,2048]{1,0:T(8,128)(2,1)S(1)}, bf16[256,2048]{1,0:T(8,128)(2,1)}, u32[]{:S(2)}) copy-start(bf16[256,2048]{1,0:T(8,128)(2,1)} %copy-done.3) | copy-start | bytes 3145732
  295.0 6.8 %copy-start.1 = (bf16[1,384,2048]{2,1,0:T(8,128)(2,1)S(1)}, bf16[1,384,2048]{2,1,0:T(8,128)(2,1)}, u32[]{:S(2)}) copy-start(bf16[1,384,2048]{2,1,0:T(8,128)(2,1)} %param.15) | copy-start | bytes 4718596
Sparse Core Ops, SparseCore 0:
  238.6 52.5 reduce-scatter.1
where the time goes:
time: 309 us
  blocking collectives  106 us (34%)
  waiting for transfers between devices  92.1 us (30%)
  matrix products  31.6 us (10%)
  local copies, waits for them, and re-layouts  30.3 us (10%)
  other arithmetic  22.7 us (7%)
  between operations  14.5 us (5%)
  starting transfers between devices  11.5 us (4%)
    all_to_all x1, blocking collectives, on_device(): lax.all_to_all(row_buffer, 'expert', split_axis=0, concat_axis=0, tiled=T...  53.8 us
    all_to_all x1, blocking collectives, on_device(): lax.all_to_all(grad_buffer, 'expert', split_axis=0, concat_axis=0, tiled=...  52.3 us
    all_to_all x1, waiting for transfers between devices, on_device(): lax.all_to_all(out_rows.reshape(devices, capacity, model_width), 'expert'...  42.2 us
    all_to_all x1, waiting for transfers between devices, on_device(): lax.all_to_all(back_rows.reshape(devices, capacity, model_width), 'expert...  34.1 us
    ppermute x4, waiting for transfers between devices, from_partner(): return lax.ppermute(value, axis, pairs)  15.8 us
    dot_general x6, matrix products, rounded_term(): jnp.dot(left.T, right, preferred_element_type=jnp.float32)  12.5 us
  transfers between devices with their start and end apart: 7, of which 6 were waited for; matrix products, arithmetic and copies ran while one was open for 13% of the time, Pallas kernels for 0%

commit v1 on v0

v1 whole, which is shorter than its diff:
```python
import jax
import jax.numpy as jnp
from jax import lax
from jax.sharding import PartitionSpec as P

F32 = jnp.float32
BF16 = jnp.bfloat16


def from_partner(value, axis, distance):
    mask = 2**distance
    pairs = [(source, source ^ mask) for source in range(lax.axis_size(axis))]
    return lax.ppermute(value, axis, pairs)


def dot(left, right):
    return jnp.dot(left, right, preferred_element_type=F32)


def dot_nt(left, right):
    return lax.dot_general(left, right, (((1,), (1,)), ((), ())), preferred_element_type=F32)


def dot_tn(left, right):
    return lax.dot_general(left, right, (((0,), (0,)), ((), ())), preferred_element_type=F32)


def ring_chips(chips):
    return list(range(0, chips, 2)) + list(range(chips - 1, 0, -2))


def ring_send(value, step):
    chips = lax.axis_size("expert") // 2
    ring = ring_chips(chips)
    pairs = [
        (2 * ring[place] + core, 2 * ring[(place + step) % chips] + core)
        for place in range(chips)
        for core in range(2)
    ]
    return lax.ppermute(value, "expert", pairs)


def ring_gather(block, chips):
    far = chips // 2
    half = block.shape[0] // 2
    behind, ahead = [block], [block]
    for _ in range(far - 1):
        behind.append(ring_send(behind[-1], 1))
        ahead.append(ring_send(ahead[-1], -1))
    upper = ring_send(behind[-1][:half], 1)
    lower = ring_send(ahead[-1][half:], -1)
    return behind + [upper, lower] + ahead[:0:-1]


def ring_scatter(terms, chips):
    far = chips // 2
    half = terms(0).shape[0] // 2
    total = terms(0).astype(F32)
    for step, span in ((1, slice(0, half)), (-1, slice(half, 2 * half))):
        moving = ring_send(terms(far)[span], step)
        for distance in range(far - 1, 0, -1):
            own = terms((-step * distance) % chips).astype(F32)
            if distance == far - 1:
                joined = own[span] + moving.astype(F32)
                own = jnp.concatenate([joined, own[half:]] if step == 1 else [own[:half], joined])
            else:
                own = own + moving.astype(F32)
            moving = ring_send(own.astype(BF16), step)
        total = total + moving.astype(F32)
    return total


def all_tokens_pass(
    tokens, grad_out, expert_ids, router_weight, gate_weight, up_weight, down_weight
):
    chips = lax.axis_size("expert") // 2
    rows_own, model_width = tokens.shape
    experts = router_weight.shape[1]
    width = gate_weight.shape[2]
    device = lax.axis_index("expert")
    chip, core = device // 2, device % 2
    place = jnp.where(chip % 2 == 0, chip // 2, chips - 1 - chip // 2)

    def around(array, axis):
        turned = jnp.concatenate(
            [lax.slice_in_dim(array, 0, 1, axis=axis)]
            + [lax.slice_in_dim(array, c, c + 1, axis=axis) for c in range(chips - 1, 0, -1)],
            axis=axis,
        )
        twice = jnp.concatenate([turned, turned], axis=axis)
        return lax.dynamic_slice_in_dim(twice, chips - place, chips, axis=axis)

    token_blocks = ring_gather(tokens, chips)
    grad_blocks = ring_gather(grad_out, chips)

    onehot = (
        expert_ids[:, :, None] == jnp.arange(experts, dtype=jnp.int32)[None, None, :]
    ).astype(F32)
    named = jnp.sum(onehot, axis=1)
    probability = named * jax.nn.sigmoid(dot(tokens, router_weight))
    summed = jnp.sum(probability, axis=1, keepdims=True)
    shares = jnp.concatenate(
        [probability / summed, probability * (1.0 - probability) / summed], axis=1
    )
    shares_all = lax.all_gather(shares, "expert").reshape(chips, 2, rows_own, 2 * experts)
    shares_all = lax.dynamic_index_in_dim(shares_all, core, 1, keepdims=False)
    shares_all = jnp.stack([shares_all[c] for c in ring_chips(chips)])
    shares_all = around(shares_all, 0).reshape(chips * rows_own, 2 * experts)
    gates_all, slope_all = shares_all[:, :experts], shares_all[:, experts:]
    gate_mine = lax.dynamic_slice_in_dim(gates_all, chip, 1, axis=1)

    gate_own, up_own, down_own = gate_weight[0], up_weight[0], down_weight[0]
    gate_other, up_other, down_other = from_partner((gate_own, up_own, down_own), "expert", 0)
    weight_in = jnp.concatenate([gate_own, up_own, gate_other, up_other], axis=1)
    weight_out = jnp.concatenate([down_own, down_other], axis=0)

    rows = jnp.concatenate(token_blocks, axis=0)
    before = dot(rows, weight_in)
    pre_gate = jnp.concatenate([before[:, :width], before[:, 2 * width : 3 * width]], axis=1)
    pre_up = jnp.concatenate([before[:, width : 2 * width], before[:, 3 * width :]], axis=1)
    squash = jax.nn.sigmoid(pre_gate)
    activated = pre_gate * squash
    hidden = activated * pre_up
    hidden_gated = (gate_mine * hidden).astype(BF16)
    out = dot(hidden_gated, weight_out).astype(BF16)

    def block_of(array):
        return lambda j: array[j * rows_own : (j + 1) * rows_own]

    mixed = ring_scatter(block_of(out), chips).astype(BF16)

    grads = jnp.concatenate(grad_blocks, axis=0)
    back_hidden = dot_nt(grads, weight_out)
    gate_slope = jnp.sum(hidden * back_hidden, axis=1)
    back_gated = gate_mine * back_hidden
    gate_delta = (back_gated * pre_up * squash * (1.0 + pre_gate * (1.0 - squash))).astype(BF16)
    up_delta = (back_gated * activated).astype(BF16)
    delta_own = jnp.concatenate([gate_delta[:, :width], up_delta[:, :width]], axis=1)
    delta_other = jnp.concatenate([gate_delta[:, width:], up_delta[:, width:]], axis=1)
    back = dot_nt(jnp.concatenate([delta_own, delta_other], axis=1), weight_in).astype(BF16)
    back_sum = ring_scatter(block_of(back), chips)

    in_other = from_partner(dot_tn(rows, delta_other).astype(BF16), "expert", 0).astype(F32)
    down_other_part = from_partner(
        dot_tn(hidden_gated[:, width:], grads).astype(BF16), "expert", 0
    ).astype(F32)
    in_own = dot_tn(rows, delta_own)
    gate_grad = (in_own[:, :width] + in_other[:, :width]).astype(BF16)[None]
    up_grad = (in_own[:, width:] + in_other[:, width:]).astype(BF16)[None]
    down_grad = (dot_tn(hidden_gated[:, :width], grads) + down_other_part).astype(BF16)[None]

    gate_slope = around(gate_slope.reshape(chips, rows_own), 0)
    slopes = lax.all_gather(gate_slope, "expert").reshape(chips, 2, chips, rows_own)
    slopes = lax.dynamic_index_in_dim(slopes, core, 1, keepdims=False)
    slopes = around(slopes, 1).reshape(chips, chips * rows_own).T
    router_delta = (
        slope_all * (slopes - jnp.sum(gates_all * slopes, axis=1, keepdims=True))
    ).astype(BF16)
    token_grad = (back_sum + dot_nt(router_delta[:rows_own], router_weight)).astype(BF16)
    part = model_width // (2 * chips)
    columns = lax.dynamic_slice_in_dim(rows, chip * 2 * part, 2 * part, axis=1)
    router_part = dot_tn(columns, router_delta).reshape(2, part, experts)
    router_grad = lax.dynamic_index_in_dim(
        router_part, core, 0, keepdims=False
    ) + from_partner(
        lax.dynamic_index_in_dim(router_part, 1 - core, 0, keepdims=False), "expert", 0
    )
    return (mixed, token_grad, gate_grad, up_grad, down_grad, router_grad)


def expert_pass(rows, grads, gate_full, up_full, down_full):
    pre_gate = dot(rows, gate_full)
    pre_up = dot(rows, up_full)
    squash = jax.nn.sigmoid(pre_gate)
    activated = pre_gate * squash
    hidden = (activated * pre_up).astype(BF16)
    partial_out = dot(hidden, down_full)
    back_hidden = dot_nt(grads, down_full)
    gate_delta = (back_hidden * pre_up * squash * (1.0 + pre_gate * (1.0 - squash))).astype(BF16)
    up_delta = (back_hidden * activated).astype(BF16)
    partial_back = dot_nt(gate_delta, gate_full) + dot_nt(up_delta, up_full)
    return (partial_out, partial_back, hidden, gate_delta, up_delta)


def rounded_term(left, right):
    return dot_tn(left, right).astype(BF16).astype(F32)


def slots_pass(tokens, grad_out, expert_ids, router_weight, gate_weight, up_weight, down_weight):
    devices = lax.axis_size("expert")
    token_count, model_width = tokens.shape
    per_token = expert_ids.shape[1]
    experts = router_weight.shape[1]
    halfway = token_count // 2
    capacity = 2 * token_count * per_token // devices
    slot_total = devices * capacity
    pair_count = token_count * per_token
    onehot = expert_ids[:, :, None] == jnp.arange(experts, dtype=jnp.int32)[None, None, :]
    logits = dot(tokens, router_weight)
    chosen = jnp.sum(jnp.where(onehot, logits[:, None, :], 0.0), axis=2)
    probability = jax.nn.sigmoid(chosen)
    summed = jnp.sum(probability, axis=1, keepdims=True)
    gate_share = probability / summed
    scaled = (gate_share[:, :, None] * grad_out[:, None, :].astype(F32)).astype(BF16)
    scaled = scaled.reshape(pair_count, model_width)
    named = jnp.sum(onehot.astype(BF16), axis=1).reshape(2, halfway, experts)
    order = jnp.arange(halfway, dtype=jnp.int32)
    earlier = (order[None, :] < order[:, None]).astype(BF16)
    before = jnp.einsum("st,pte->pse", earlier, named, preferred_element_type=F32)
    before = before.reshape(token_count, 1, experts)
    position = jnp.sum(jnp.where(onehot, before, 0.0), axis=2).astype(jnp.int32)
    parity = (jnp.arange(token_count, dtype=jnp.int32) // halfway)[:, None]
    target = ((2 * expert_ids + parity) * capacity + position).reshape(pair_count)
    source = (
        jnp.full((slot_total,), pair_count, jnp.int32)
        .at[target]
        .set(jnp.arange(pair_count, dtype=jnp.int32))
    )
    filled = (source < pair_count)[:, None]
    clipped = jnp.minimum(source, pair_count - 1)
    row_buffer = jnp.where(filled, jnp.take(tokens, clipped // per_token, axis=0), 0.0)
    grad_buffer = jnp.where(filled, jnp.take(scaled, clipped, axis=0), 0.0)
    row_buffer = row_buffer.reshape(devices, capacity, model_width)
    grad_buffer = grad_buffer.reshape(devices, capacity, model_width)

    def exchange(value):
        return lax.all_to_all(value, "expert", split_axis=0, concat_axis=0, tiled=True)

    rows_in = exchange(row_buffer).reshape(slot_total, model_width)
    grads_in = exchange(grad_buffer).reshape(slot_total, model_width)
    other_rows, other_grads = from_partner((rows_in, grads_in), "expert", 0)
    both_rows = jnp.concatenate([rows_in, other_rows], axis=0)
    both_grads = jnp.concatenate([grads_in, other_grads], axis=0)
    partial_out, partial_back, hidden, gate_delta, up_delta = expert_pass(
        both_rows, both_grads, gate_weight[0], up_weight[0], down_weight[0]
    )
    got_out = from_partner(partial_out[slot_total:].astype(BF16), "expert", 0).astype(F32)
    got_back = from_partner(partial_back[slot_total:].astype(BF16), "expert", 0).astype(F32)
    out_rows = (partial_out[:slot_total] + got_out).astype(BF16)
    back_rows = (partial_back[:slot_total] + got_back).astype(BF16)
    gate_sum = rounded_term(rows_in, gate_delta[:slot_total]) + rounded_term(
        other_rows, gate_delta[slot_total:]
    )
    up_sum = rounded_term(rows_in, up_delta[:slot_total]) + rounded_term(
        other_rows, up_delta[slot_total:]
    )
    down_sum = rounded_term(hidden[:slot_total], grads_in) + rounded_term(
        hidden[slot_total:], other_grads
    )
    gate_grad = gate_sum.astype(BF16)[None]
    up_grad = up_sum.astype(BF16)[None]
    down_grad = down_sum.astype(BF16)[None]
    out_back = exchange(out_rows.reshape(devices, capacity, model_width))
    grad_back = exchange(back_rows.reshape(devices, capacity, model_width))
    expert_out = jnp.take(out_back.reshape(slot_total, model_width), target, axis=0)
    expert_out = expert_out.reshape(token_count, per_token, model_width).astype(F32)
    expert_back = jnp.take(grad_back.reshape(slot_total, model_width), target, axis=0)
    expert_back = expert_back.reshape(token_count, per_token, model_width).astype(F32)
    mixed = jnp.sum(gate_share[:, :, None] * expert_out, axis=1).astype(BF16)
    gate_slope = jnp.sum(grad_out[:, None, :].astype(F32) * expert_out, axis=2)
    prob_slope = (gate_slope - jnp.sum(gate_share * gate_slope, axis=1, keepdims=True)) / summed
    logit_slope = prob_slope * probability * (1.0 - probability)
    router_delta = jnp.sum(jnp.where(onehot, logit_slope[:, :, None], 0.0), axis=1).astype(BF16)
    token_grad = jnp.sum(expert_back, axis=1) + dot_nt(router_delta, router_weight)
    token_grad = token_grad.astype(BF16)
    router_grad = lax.psum_scatter(
        dot_tn(tokens, router_delta), "expert", scatter_dimension=0, tiled=True
    )
    return (mixed, token_grad, gate_grad, up_grad, down_grad, router_grad)


def on_device(tokens, grad_out, expert_ids, router_weight, gate_weight, up_weight, down_weight):
    token_count = tokens.shape[0]
    capacity = 2 * token_count * expert_ids.shape[1] // lax.axis_size("expert")
    step = all_tokens_pass if 2 * capacity >= token_count else slots_pass
    return step(tokens, grad_out, expert_ids, router_weight, gate_weight, up_weight, down_weight)


def solution(mesh):
    return jax.shard_map(
        on_device,
        mesh=mesh,
        in_specs=(
            P(("groups", "expert"), None),
            P(("groups", "expert"), None),
            P(("groups", "expert"), None),
            P(),
            P("expert", None, None),
            P("expert", None, None),
            P("expert", None, None),
        ),
        out_specs=(
            P(("groups", "expert"), None),
            P(("groups", "expert"), None),
            P(("groups", "expert"), None, None),
            P(("groups", "expert"), None, None),
            P(("groups", "expert"), None, None),
            P(("groups", "expert"), None),
        ),
        check_vma=False,
    )
```

time: 309 us -> 180 us (0.58)
  the two profiles are of different devices: /device:TPU:13 before, /device:TPU:0 now
where the time goes in v1:
time: 180 us
  waiting for transfers between devices  58 us (32%)
  blocking collectives  41.2 us (23%)
  starting transfers between devices  35.4 us (20%)
  matrix products  25.5 us (14%)
  local copies, waits for them, and re-layouts  12 us (7%)
  other arithmetic  6.43 us (4%)
    ppermute x32, waiting for transfers between devices, ring_send(): return lax.ppermute(value, 'expert', pairs)  58 us
    ppermute x32, starting transfers between devices, ring_send(): return lax.ppermute(value, 'expert', pairs)  34 us
    all_gather x1, blocking collectives, all_tokens_pass(): lax.all_gather(shares, 'expert').reshape(chips, 2, rows_own, 2 * experts)  22.4 us
    all_gather x1, blocking collectives, all_tokens_pass(): lax.all_gather(gate_slope, 'expert').reshape(chips, 2, chips, rows_own)  18.8 us
    unnamed x48, local copies, waits for them, and re-layouts  10.1 us
    dot_general x3, matrix products, dot_nt(): lax.dot_general(left, right, (((1,), (1,)), ((), ())), preferred_element_...  9.1 us
    dot_general x5, matrix products, dot_tn(): lax.dot_general(left, right, (((0,), (0,)), ((), ())), preferred_element_...  8.87 us
    dot_general x3, matrix products, dot(): return jnp.dot(left, right, preferred_element_type=F32)  7.55 us
  transfers between devices with their start and end apart: 38, of which 17 were waited for; matrix products, arithmetic and copies ran while one was open for 19% of the time, Pallas kernels for 0%

profile of v1, /device:TPU:0, one launch (start us, length us, event | category | flops | bytes accessed | tf_op | source)
XLA Modules:
  0.0 179.8 jit_solution(4086779322855561884)
XLA Ops:
  0.6 3.1 %collective-permute-start.19 = (bf16[64,2048]{1,0:T(8,128)(2,1)}, bf16[64,2048]{1,0:T(8,128)(2,1)S(1)}, u32[]{:S(2)}, u32[]{:S(2)}) collective-permute-start(bf16[64,2048]{1,0:T(8,128)(2,1)} %param.8), channel_id=1, source_target_pairs={{0,4},{1,5},{4,8},{5,9},{8,12},{9,13},{12,14},{13,15},{14,10},{15,... | collective-permute-start | bytes 786440 | tf_op jit(solution)/shard_map/ppermute | solution.py:40
  3.7 2.0 %collective-permute-start = (bf16[64,2048]{1,0:T(8,128)(2,1)}, bf16[64,2048]{1,0:T(8,128)(2,1)S(1)}, u32[]{:S(2)}, u32[]{:S(2)}) collective-permute-start(bf16[64,2048]{1,0:T(8,128)(2,1)} %param.7), channel_id=1, source_target_pairs={{0,4},{1,5},{4,8},{5,9},{8,12},{9,13},{12,14},{13,15},{14,10},{15,... | collective-permute-start | bytes 786440 | tf_op jit(solution)/shard_map/ppermute | solution.py:40
  5.8 1.7 constant_dynamic-update-slice_fusion.17
  8.1 1.1 fusion.48
  9.3 22.4 %all-gather.2 = f32[16,64,16]{1,2,0:T(8,128)S(1)} all-gather(f32[1,64,16]{1,2,0:T(8,128)S(1)} %maximum_bitcast_fusion), channel_id=2, replica_groups=mesh['groups'=2,'expert'=16] {'expert'}, dimensions={0}, use_global_device_ids=true | all-gather | bytes 69632 | tf_op jit(solution)/shard_map/all_gather | solution.py:105
  32.1 1.0 constant_dynamic-update-slice_fusion.8
  33.1 2.0 %collective-permute-start.24 = (bf16[64,2048]{1,0:T(8,128)(2,1)S(1)}, bf16[64,2048]{1,0:T(8,128)(2,1)S(1)}, u32[]{:S(2)}, u32[]{:S(2)}) collective-permute-start(bf16[64,2048]{1,0:T(8,128)(2,1)S(1)} %collective-permute-done.23), channel_id=1, source_target_pairs={{0,2},{1,3},{4,0},{5,1},{8,4},{9,5},{12,8},{13,9},{14,12},{15,13},... | collective-permute-start | bytes 786440 | tf_op jit(solution)/shard_map/ppermute | solution.py:40
  35.2 2.0 %collective-permute-start.5 = (bf16[64,2048]{1,0:T(8,128)(2,1)S(1)}, bf16[64,2048]{1,0:T(8,128)(2,1)S(1)}, u32[]{:S(2)}, u32[]{:S(2)}) collective-permute-start(bf16[64,2048]{1,0:T(8,128)(2,1)S(1)} %collective-permute-done.4), channel_id=1, source_target_pairs={{0,2},{1,3},{4,0},{5,1},{8,4},{9,5},{12,8},{13,9},{14,12},{15,13},... | collective-permute-start | bytes 786440 | tf_op jit(solution)/shard_map/ppermute | solution.py:40
  37.9 4.3 %collective-permute-done.20 = bf16[64,2048]{1,0:T(8,128)(2,1)S(1)} collective-permute-done((bf16[64,2048]{1,0:T(8,128)(2,1)S(1)}, bf16[64,2048]{1,0:T(8,128)(2,1)S(1)}, u32[]{:S(2)}, u32[]{:S(2)}) %collective-permute-start.20) | collective-permute-done | bytes 262176 | tf_op jit(solution)/shard_map/ppermute | solution.py:40
  42.3 2.0 %collective-permute-start.25 = (bf16[64,2048]{1,0:T(8,128)(2,1)S(1)}, bf16[64,2048]{1,0:T(8,128)(2,1)S(1)}, u32[]{:S(2)}, u32[]{:S(2)}) collective-permute-start(bf16[64,2048]{1,0:T(8,128)(2,1)S(1)} %collective-permute-done.24), channel_id=1, source_target_pairs={{0,2},{1,3},{4,0},{5,1},{8,4},{9,5},{12,8},{13,9},{14,12},{15,13},... | collective-permute-start | bytes 786440 | tf_op jit(solution)/shard_map/ppermute | solution.py:40
  44.3 3.5 %collective-permute-done.1 = bf16[64,2048]{1,0:T(8,128)(2,1)S(1)} collective-permute-done((bf16[64,2048]{1,0:T(8,128)(2,1)S(1)}, bf16[64,2048]{1,0:T(8,128)(2,1)S(1)}, u32[]{:S(2)}, u32[]{:S(2)}) %collective-permute-start.1) | collective-permute-done | bytes 262176 | tf_op jit(solution)/shard_map/ppermute | solution.py:40
  47.9 2.0 %collective-permute-start.6 = (bf16[64,2048]{1,0:T(8,128)(2,1)S(1)}, bf16[64,2048]{1,0:T(8,128)(2,1)S(1)}, u32[]{:S(2)}, u32[]{:S(2)}) collective-permute-start(bf16[64,2048]{1,0:T(8,128)(2,1)S(1)} %collective-permute-done.5), channel_id=1, source_target_pairs={{0,2},{1,3},{4,0},{5,1},{8,4},{9,5},{12,8},{13,9},{14,12},{15,13},... | collective-permute-start | bytes 786440 | tf_op jit(solution)/shard_map/ppermute | solution.py:40
  50.7 2.8 %collective-permute-done.21 = bf16[64,2048]{1,0:T(8,128)(2,1)S(1)} collective-permute-done((bf16[64,2048]{1,0:T(8,128)(2,1)S(1)}, bf16[64,2048]{1,0:T(8,128)(2,1)S(1)}, u32[]{:S(2)}, u32[]{:S(2)}) %collective-permute-start.21) | collective-permute-done | bytes 262176 | tf_op jit(solution)/shard_map/ppermute | solution.py:40
  54.1 4.4 %collective-permute-done.2 = bf16[64,2048]{1,0:T(8,128)(2,1)S(1)} collective-permute-done((bf16[64,2048]{1,0:T(8,128)(2,1)S(1)}, bf16[64,2048]{1,0:T(8,128)(2,1)S(1)}, u32[]{:S(2)}, u32[]{:S(2)}) %collective-permute-start.2) | collective-permute-done | bytes 262176 | tf_op jit(solution)/shard_map/ppermute | solution.py:40
  58.8 1.8 collective-permute-start.26
  61.4 2.1 %collective-permute-done.22 = bf16[32,2048]{1,0:T(8,128)(2,1)S(1)} collective-permute-done((bf16[32,2048]{1,0:T(8,128)(2,1)S(1)}, bf16[32,2048]{1,0:T(8,128)(2,1)S(1)}, u32[]{:S(2)}, u32[]{:S(2)}) %collective-permute-start.22) | collective-permute-done | bytes 131104 | tf_op jit(solution)/shard_map/ppermute | solution.py:40
  64.6 1.5 collective-permute-start.7
  66.9 1.6 collective-permute-done.3
  68.5 1.1 collective-permute-done.7
  71.9 4.6 %fusion.19 = f32[512,1536]{1,0:T(8,128)S(1)} fusion(bf16[512,2048]{1,0:T(8,128)(2,1)S(1)} %constant_dynamic-update-slice_fusion, bf16[2048,384]{1,0:T(8,128)(2,1)S(1)} %collective-permute-done.9, bf16[2048,384]{1,0:T(8,128)(2,1)} %collective-permute-done.8, bf16[2048,384]{1,0:T(8,128)(2,1)S(1)} %bitcast.110, bf16[2048,384]{1,0:T(8,128)(2,1)S(1)} %bitcast.113), kind=kOutput, calls=%fused_computation.37 | convolution fusion | flops 3246391296 | bytes 11534336 | tf_op jit(solution)/shard_map/dot_general | solution.py:17
  76.8 1.9 %copy-done.3 = bf16[512,2048]{1,0:T(8,128)(2,1)S(1)} copy-done((bf16[512,2048]{1,0:T(8,128)(2,1)S(1)}, bf16[512,2048]{1,0:T(8,128)(2,1)}, u32[]{:S(2)}) %copy-start.3) | copy-done | bytes 2097176
  79.2 3.8 %multiply_convert_fusion.1 = (bf16[512,768]{1,0:T(8,128)(2,1)S(1)}, f32[512]{0:T(512)S(1)}, bf16[512,768]{1,0:T(8,128)(2,1)}, bf16[512,768]{1,0:T(8,128)(2,1)}) fusion(f32[512,384]{1,0:T(8,128)S(1)} %get-tuple-element.13, f32[512,384]{1,0:T(8,128)S(1)} %get-tuple-element.14, f32[512,384]{1,0:T(8,128)S(1)} %get-tuple-element.15, ...), kind=kOutput, calls=%fused_computation.26 | convolution fusion | flops 1625161216 | bytes 10752000 | tf_op jit(solution)/shard_map/dot_general | solution.py:21
  83.1 18.8 %all-gather.1 = f32[128,64]{1,0:T(8,128)S(1)} all-gather(f32[8,64]{1,0:T(8,128)S(1)} %constant_dynamic-slice_fusion.8), channel_id=3, replica_groups=mesh['groups'=2,'expert'=16] {'expert'}, dimensions={0}, use_global_device_ids=true | all-gather | bytes 34816 | tf_op jit(solution)/shard_map/all_gather | solution.py:153
  102.9 2.9 %convolution_convert_fusion.3 = bf16[384,2048]{1,0:T(8,128)(2,1)S(1)} fusion(bf16[512,2048]{1,0:T(8,128)(2,1)} %constant_dynamic-update-slice_fusion.9, bf16[512,768]{1,0:T(8,128)(2,1)} %get-tuple-element.10), kind=kOutput, calls=%fused_computation.10 | convolution fusion | flops 806092800 | bytes 4063232 | tf_op jit(solution)/shard_map/dot_general | solution.py:25
  105.8 1.8 convolution_convert_fusion.2
  107.8 2.0 %collective-permute-start.15 = (bf16[32,2048]{1,0:T(8,128)(2,1)S(1)}, bf16[32,2048]{1,0:T(8,128)(2,1)S(1)}, u32[]{:S(2)}, u32[]{:S(2)}) collective-permute-start(bf16[32,2048]{1,0:T(8,128)(2,1)S(1)} %get-tuple-element.29), channel_id=1, source_target_pairs={{0,2},{1,3},{4,0},{5,1},{8,4},{9,5},{12,8},{13,9},{14,12},{15,13},... | collective-permute-start | bytes 393224 | tf_op jit(solution)/shard_map/ppermute | solution.py:40
  109.9 1.8 %convolution_convert_fusion = bf16[2048,768]{1,0:T(8,128)(2,1)S(1)} fusion(bf16[512,2048]{1,0:T(8,128)(2,1)S(1)} %constant_dynamic-update-slice_fusion, bf16[512,384]{1,0:T(8,128)(2,1)S(1)} %get-tuple-element.64, bf16[512,384]{1,0:T(8,128)(2,1)S(1)} %get-tuple-element.33), kind=kOutput, calls=%fused_computation.1 | convolution fusion | flops 1613758464 | bytes 6029312 | tf_op jit(solution)/shard_map/dot_general | solution.py:25
  111.8 1.8 %fusion.20 = f32[2048,768]{1,0:T(8,128)S(1)} fusion(bf16[512,2048]{1,0:T(8,128)(2,1)S(1)} %constant_dynamic-update-slice_fusion, bf16[512,384]{1,0:T(8,128)(2,1)S(1)} %get-tuple-element.65, bf16[512,384]{1,0:T(8,128)(2,1)S(1)} %get-tuple-element.32), kind=kOutput, calls=%fused_computation.38 | convolution fusion | flops 1612185600 | bytes 9175040 | tf_op jit(solution)/shard_map/dot_general | solution.py:25
  113.7 5.1 %convolution_convert_fusion.1 = bf16[512,2048]{1,0:T(8,128)(2,1)S(1)} fusion(bf16[512,384]{1,0:T(8,128)(2,1)S(1)} %get-tuple-element.64, bf16[512,384]{1,0:T(8,128)(2,1)S(1)} %get-tuple-element.33, bf16[512,384]{1,0:T(8,128)(2,1)S(1)} %get-tuple-element.65, bf16[512,384]{1,0:T(8,128)(2,1)S(1)} %get-tuple-element.32, bf16[2048,384]{1,0:T(8,128)(2,1)} %copy-done.11, ...), kind=kOutput, calls=%fused_computation.8 | convolution fusion | flops 3253731328 | bytes 9961472 | tf_op jit(solution)/shard_map/dot_general | solution.py:21
  119.1 1.8 collective-permute-start.31
  122.7 1.2 collective-permute-done.27
  124.5 2.1 %collective-permute-start.32 = (bf16[64,2048]{1,0:T(8,128)(2,1)S(1)}, bf16[64,2048]{1,0:T(8,128)(2,1)S(1)}, u32[]{:S(2)}, u32[]{:S(2)}) collective-permute-start(bf16[64,2048]{1,0:T(8,128)(2,1)S(1)} %pad_maximum_fusion.11), channel_id=1, source_target_pairs={{0,2},{1,3},{4,0},{5,1},{8,4},{9,5},{12,8},{13,9},{14,12},{15,13},... | collective-permute-start | bytes 786440 | tf_op jit(solution)/shard_map/ppermute | solution.py:40
  126.7 4.0 %collective-permute-done.12 = bf16[64,2048]{1,0:T(8,128)(2,1)S(1)} collective-permute-done((bf16[64,2048]{1,0:T(8,128)(2,1)S(1)}, bf16[64,2048]{1,0:T(8,128)(2,1)S(1)}, u32[]{:S(2)}, u32[]{:S(2)}) %collective-permute-start.12) | collective-permute-done | bytes 262176 | tf_op jit(solution)/shard_map/ppermute | solution.py:40
  130.7 1.5 collective-permute-start.28
  132.3 4.8 %collective-permute-done.28 = bf16[64,2048]{1,0:T(8,128)(2,1)S(1)} collective-permute-done((bf16[64,2048]{1,0:T(8,128)(2,1)S(1)}, bf16[64,2048]{1,0:T(8,128)(2,1)S(1)}, u32[]{:S(2)}, u32[]{:S(2)}) %collective-permute-start.28) | collective-permute-done | bytes 262176 | tf_op jit(solution)/shard_map/ppermute | solution.py:40
  137.0 2.1 %collective-permute-start.13 = (bf16[64,2048]{1,0:T(8,128)(2,1)S(1)}, bf16[64,2048]{1,0:T(8,128)(2,1)S(1)}, u32[]{:S(2)}, u32[]{:S(2)}) collective-permute-start(bf16[64,2048]{1,0:T(8,128)(2,1)S(1)} %add_convert_fusion.10), channel_id=1, source_target_pairs={{0,4},{1,5},{4,8},{5,9},{8,12},{9,13},{12,14},{13,15},{14,10},{15,... | collective-permute-start | bytes 786440 | tf_op jit(solution)/shard_map/ppermute | solution.py:40
  139.5 6.8 %collective-permute-done.13 = bf16[64,2048]{1,0:T(8,128)(2,1)S(1)} collective-permute-done((bf16[64,2048]{1,0:T(8,128)(2,1)S(1)}, bf16[64,2048]{1,0:T(8,128)(2,1)S(1)}, u32[]{:S(2)}, u32[]{:S(2)}) %collective-permute-start.13) | collective-permute-done | bytes 262176 | tf_op jit(solution)/shard_map/ppermute | solution.py:40
  146.4 2.1 %collective-permute-start.14 = (bf16[64,2048]{1,0:T(8,128)(2,1)S(1)}, bf16[64,2048]{1,0:T(8,128)(2,1)S(1)}, u32[]{:S(2)}, u32[]{:S(2)}) collective-permute-start(bf16[64,2048]{1,0:T(8,128)(2,1)S(1)} %get-tuple-element.24), channel_id=1, source_target_pairs={{0,4},{1,5},{4,8},{5,9},{8,12},{9,13},{12,14},{13,15},{14,10},{15,... | collective-permute-start | bytes 786440 | tf_op jit(solution)/shard_map/ppermute | solution.py:40
  148.5 3.4 %collective-permute-done.29 = bf16[64,2048]{1,0:T(8,128)(2,1)S(1)} collective-permute-done((bf16[64,2048]{1,0:T(8,128)(2,1)S(1)}, bf16[64,2048]{1,0:T(8,128)(2,1)S(1)}, u32[]{:S(2)}, u32[]{:S(2)}) %collective-permute-start.29) | collective-permute-done | bytes 262176 | tf_op jit(solution)/shard_map/ppermute | solution.py:40
  152.0 2.1 %collective-permute-start.30 = (bf16[64,2048]{1,0:T(8,128)(2,1)S(1)}, bf16[64,2048]{1,0:T(8,128)(2,1)S(1)}, u32[]{:S(2)}, u32[]{:S(2)}) collective-permute-start(bf16[64,2048]{1,0:T(8,128)(2,1)S(1)} %get-tuple-element.16), channel_id=1, source_target_pairs={{0,4},{1,5},{4,8},{5,9},{8,12},{9,13},{12,14},{13,15},{14,10},{15,... | collective-permute-start | bytes 786440 | tf_op jit(solution)/shard_map/ppermute | solution.py:40
  154.1 1.6 collective-permute-done.17
  156.1 8.7 %collective-permute-done.33 = bf16[64,2048]{1,0:T(8,128)(2,1)S(1)} collective-permute-done((bf16[64,2048]{1,0:T(8,128)(2,1)S(1)}, bf16[64,2048]{1,0:T(8,128)(2,1)S(1)}, u32[]{:S(2)}, u32[]{:S(2)}) %collective-permute-start.33) | collective-permute-done | bytes 262176 | tf_op jit(solution)/shard_map/ppermute | solution.py:40
  165.7 5.5 %collective-permute-done.18 = bf16[64,2048]{1,0:T(8,128)(2,1)S(1)} collective-permute-done((bf16[64,2048]{1,0:T(8,128)(2,1)S(1)}, bf16[64,2048]{1,0:T(8,128)(2,1)S(1)}, u32[]{:S(2)}, u32[]{:S(2)}) %collective-permute-start.18) | collective-permute-done | bytes 262176 | tf_op jit(solution)/shard_map/ppermute | solution.py:40
  171.2 0.8 add_convert_fusion.6
  172.0 2.0 %collective-permute-done.34 = bf16[64,2048]{1,0:T(8,128)(2,1)S(1)} collective-permute-done((bf16[64,2048]{1,0:T(8,128)(2,1)S(1)}, bf16[64,2048]{1,0:T(8,128)(2,1)S(1)}, u32[]{:S(2)}, u32[]{:S(2)}) %collective-permute-start.34) | collective-permute-done | bytes 262176 | tf_op jit(solution)/shard_map/ppermute | solution.py:40
  174.0 0.8 add_convert_fusion.1
  174.8 2.2 %fusion.2 = bf16[1,384,2048]{2,1,0:T(8,128)(2,1)} fusion(bf16[384,2048]{1,0:T(8,128)(2,1)S(1)} %collective-permute-done.36, bf16[512,2048]{1,0:T(8,128)(2,1)S(1)} %copy-done.4, bf16[512,768]{1,0:T(8,128)(2,1)S(1)} %copy-done.15), kind=kOutput, calls=%fused_computation.11 | convolution fusion | flops 807665664 | bytes 5636096 | tf_op jit(solution)/shard_map/dot_general | solution.py:25
  177.5 2.3 %fusion.5 = (bf16[1,2048,384]{2,1,0:T(8,128)(2,1)}, bf16[1,2048,384]{2,1,0:T(8,128)(2,1)}) fusion(f32[2048,768]{1,0:T(8,128)S(1)} %convert_element_type.202, f32[2048,768]{1,0:T(8,128)S(1)} %fusion.20), kind=kLoop, calls=%fused_computation.14 | loop fusion | flops 3145728 | bytes 15728640 | tf_op jit(solution)/shard_map/broadcast_in_dim | solution.py:149
  (136 shorter events, 15.8 us)
Async XLA Ops:
  0.6 7.5 %copy-start = (bf16[2048,8]{0,1:T(8,128)(2,1)S(1)}, bf16[2048,8]{0,1:T(8,128)(2,1)}, u32[]{:S(2)}) copy-start(bf16[2048,8]{0,1:T(8,128)(2,1)} %param.10) | copy-start | bytes 98308
  0.6 32.4 %collective-permute-start.19 = (bf16[64,2048]{1,0:T(8,128)(2,1)}, bf16[64,2048]{1,0:T(8,128)(2,1)S(1)}, u32[]{:S(2)}, u32[]{:S(2)}) collective-permute-start(bf16[64,2048]{1,0:T(8,128)(2,1)} %param.8), channel_id=1, source_target_pairs={{0,4},{1,5},{4,8},{5,9},{8,12},{9,13},{12,14},{13,15},{14,10},{15,... | collective-permute-start | bytes 786440 | tf_op jit(solution)/shard_map/ppermute | solution.py:40
  3.7 29.4 %collective-permute-start.23 = (bf16[64,2048]{1,0:T(8,128)(2,1)}, bf16[64,2048]{1,0:T(8,128)(2,1)S(1)}, u32[]{:S(2)}, u32[]{:S(2)}) collective-permute-start(bf16[64,2048]{1,0:T(8,128)(2,1)} %param.8), channel_id=1, source_target_pairs={{0,2},{1,3},{4,0},{5,1},{8,4},{9,5},{12,8},{13,9},{14,12},{15,13},... | collective-permute-start | bytes 786440 | tf_op jit(solution)/shard_map/ppermute | solution.py:40
  3.7 31.4 %collective-permute-start = (bf16[64,2048]{1,0:T(8,128)(2,1)}, bf16[64,2048]{1,0:T(8,128)(2,1)S(1)}, u32[]{:S(2)}, u32[]{:S(2)}) collective-permute-start(bf16[64,2048]{1,0:T(8,128)(2,1)} %param.7), channel_id=1, source_target_pairs={{0,4},{1,5},{4,8},{5,9},{8,12},{9,13},{12,14},{13,15},{14,10},{15,... | collective-permute-start | bytes 786440 | tf_op jit(solution)/shard_map/ppermute | solution.py:40
  5.8 29.5 %collective-permute-start.4 = (bf16[64,2048]{1,0:T(8,128)(2,1)}, bf16[64,2048]{1,0:T(8,128)(2,1)S(1)}, u32[]{:S(2)}, u32[]{:S(2)}) collective-permute-start(bf16[64,2048]{1,0:T(8,128)(2,1)} %param.7), channel_id=1, source_target_pairs={{0,2},{1,3},{4,0},{5,1},{8,4},{9,5},{12,8},{13,9},{14,12},{15,13},... | collective-permute-start | bytes 786440 | tf_op jit(solution)/shard_map/ppermute | solution.py:40
  5.8 66.1 %collective-permute-start.8 = (bf16[2048,384]{1,0:T(8,128)(2,1)}, bf16[2048,384]{1,0:T(8,128)(2,1)}, u32[]{:S(2)}, u32[]{:S(2)}) collective-permute-start(bf16[2048,384]{1,0:T(8,128)(2,1)} %bitcast.112), channel_id=1, source_target_pairs={{0,1},{1,0},{2,3},{3,2},{4,5},{5,4},{6,7},{7,6},{8,9},{9,8},{10,11... | collective-permute-start | bytes 4718600 | tf_op jit(solution)/shard_map/ppermute | solution.py:13
  33.1 9.2 %collective-permute-start.20 = (bf16[64,2048]{1,0:T(8,128)(2,1)S(1)}, bf16[64,2048]{1,0:T(8,128)(2,1)S(1)}, u32[]{:S(2)}, u32[]{:S(2)}) collective-permute-start(bf16[64,2048]{1,0:T(8,128)(2,1)S(1)} %collective-permute-done.19), channel_id=1, source_target_pairs={{0,4},{1,5},{4,8},{5,9},{8,12},{9,13},{12,14},{13,15},{14,10},{15,... | collective-permute-start | bytes 786440 | tf_op jit(solution)/shard_map/ppermute | solution.py:40
  33.1 9.2 %collective-permute-start.24 = (bf16[64,2048]{1,0:T(8,128)(2,1)S(1)}, bf16[64,2048]{1,0:T(8,128)(2,1)S(1)}, u32[]{:S(2)}, u32[]{:S(2)}) collective-permute-start(bf16[64,2048]{1,0:T(8,128)(2,1)S(1)} %collective-permute-done.23), channel_id=1, source_target_pairs={{0,2},{1,3},{4,0},{5,1},{8,4},{9,5},{12,8},{13,9},{14,12},{15,13},... | collective-permute-start | bytes 786440 | tf_op jit(solution)/shard_map/ppermute | solution.py:40
  35.2 12.7 %collective-permute-start.1 = (bf16[64,2048]{1,0:T(8,128)(2,1)S(1)}, bf16[64,2048]{1,0:T(8,128)(2,1)S(1)}, u32[]{:S(2)}, u32[]{:S(2)}) collective-permute-start(bf16[64,2048]{1,0:T(8,128)(2,1)S(1)} %collective-permute-done), channel_id=1, source_target_pairs={{0,4},{1,5},{4,8},{5,9},{8,12},{9,13},{12,14},{13,15},{14,10},{15,... | collective-permute-start | bytes 786440 | tf_op jit(solution)/shard_map/ppermute | solution.py:40
  35.2 12.7 %collective-permute-start.5 = (bf16[64,2048]{1,0:T(8,128)(2,1)S(1)}, bf16[64,2048]{1,0:T(8,128)(2,1)S(1)}, u32[]{:S(2)}, u32[]{:S(2)}) collective-permute-start(bf16[64,2048]{1,0:T(8,128)(2,1)S(1)} %collective-permute-done.4), channel_id=1, source_target_pairs={{0,2},{1,3},{4,0},{5,1},{8,4},{9,5},{12,8},{13,9},{14,12},{15,13},... | collective-permute-start | bytes 786440 | tf_op jit(solution)/shard_map/ppermute | solution.py:40
  42.2 11.2 %collective-permute-start.21 = (bf16[64,2048]{1,0:T(8,128)(2,1)S(1)}, bf16[64,2048]{1,0:T(8,128)(2,1)S(1)}, u32[]{:S(2)}, u32[]{:S(2)}) collective-permute-start(bf16[64,2048]{1,0:T(8,128)(2,1)S(1)} %collective-permute-done.20), channel_id=1, source_target_pairs={{0,4},{1,5},{4,8},{5,9},{8,12},{9,13},{12,14},{13,15},{14,10},{15,... | collective-permute-start | bytes 786440 | tf_op jit(solution)/shard_map/ppermute | solution.py:40
  42.3 11.2 %collective-permute-start.25 = (bf16[64,2048]{1,0:T(8,128)(2,1)S(1)}, bf16[64,2048]{1,0:T(8,128)(2,1)S(1)}, u32[]{:S(2)}, u32[]{:S(2)}) collective-permute-start(bf16[64,2048]{1,0:T(8,128)(2,1)S(1)} %collective-permute-done.24), channel_id=1, source_target_pairs={{0,2},{1,3},{4,0},{5,1},{8,4},{9,5},{12,8},{13,9},{14,12},{15,13},... | collective-permute-start | bytes 786440 | tf_op jit(solution)/shard_map/ppermute | solution.py:40
  47.9 10.7 %collective-permute-start.2 = (bf16[64,2048]{1,0:T(8,128)(2,1)S(1)}, bf16[64,2048]{1,0:T(8,128)(2,1)S(1)}, u32[]{:S(2)}, u32[]{:S(2)}) collective-permute-start(bf16[64,2048]{1,0:T(8,128)(2,1)S(1)} %collective-permute-done.1), channel_id=1, source_target_pairs={{0,4},{1,5},{4,8},{5,9},{8,12},{9,13},{12,14},{13,15},{14,10},{15,... | collective-permute-start | bytes 786440 | tf_op jit(solution)/shard_map/ppermute | solution.py:40
  47.9 10.9 %collective-permute-start.6 = (bf16[64,2048]{1,0:T(8,128)(2,1)S(1)}, bf16[64,2048]{1,0:T(8,128)(2,1)S(1)}, u32[]{:S(2)}, u32[]{:S(2)}) collective-permute-start(bf16[64,2048]{1,0:T(8,128)(2,1)S(1)} %collective-permute-done.5), channel_id=1, source_target_pairs={{0,2},{1,3},{4,0},{5,1},{8,4},{9,5},{12,8},{13,9},{14,12},{15,13},... | collective-permute-start | bytes 786440 | tf_op jit(solution)/shard_map/ppermute | solution.py:40
  53.5 18.4 %collective-permute-start.9 = (bf16[2048,384]{1,0:T(8,128)(2,1)}, bf16[2048,384]{1,0:T(8,128)(2,1)S(1)}, u32[]{:S(2)}, u32[]{:S(2)}) collective-permute-start(bf16[2048,384]{1,0:T(8,128)(2,1)} %bitcast.109), channel_id=1, source_target_pairs={{0,1},{1,0},{2,3},{3,2},{4,5},{5,4},{6,7},{7,6},{8,9},{9,8},{10,11... | collective-permute-start | bytes 4718600 | tf_op jit(solution)/shard_map/ppermute | solution.py:13
  53.6 23.2 %collective-permute-start.10 = (bf16[384,2048]{1,0:T(8,128)(2,1)}, bf16[384,2048]{1,0:T(8,128)(2,1)S(1)}, u32[]{:S(2)}, u32[]{:S(2)}) collective-permute-start(bf16[384,2048]{1,0:T(8,128)(2,1)} %bitcast.106), channel_id=1, source_target_pairs={{0,1},{1,0},{2,3},{3,2},{4,5},{5,4},{6,7},{7,6},{8,9},{9,8},{10,11... | collective-permute-start | bytes 4718600 | tf_op jit(solution)/shard_map/ppermute | solution.py:13
  58.5 5.0 %collective-permute-start.22 = (bf16[32,2048]{1,0:T(8,128)(2,1)S(1)}, bf16[32,2048]{1,0:T(8,128)(2,1)S(1)}, u32[]{:S(2)}, u32[]{:S(2)}) collective-permute-start(bf16[32,2048]{1,0:T(8,128)(2,1)S(1)} %slice.390), channel_id=1, source_target_pairs={{0,4},{1,5},{4,8},{5,9},{8,12},{9,13},{12,14},{13,15},{14,10},{15,... | collective-permute-start | bytes 393224 | tf_op jit(solution)/shard_map/ppermute | solution.py:40
  58.8 5.8 %collective-permute-start.26 = (bf16[32,2048]{1,0:T(8,128)(2,1)S(1)}, bf16[32,2048]{1,0:T(8,128)(2,1)S(1)}, u32[]{:S(2)}, u32[]{:S(2)}) collective-permute-start(bf16[32,2048]{1,0:T(8,128)(2,1)S(1)} %slice.391), channel_id=1, source_target_pairs={{0,2},{1,3},{4,0},{5,1},{8,4},{9,5},{12,8},{13,9},{14,12},{15,13},... | collective-permute-start | bytes 393224 | tf_op jit(solution)/shard_map/ppermute | solution.py:40
  61.4 10.5 %copy-start.7 = (bf16[1,2048,384]{2,1,0:T(8,128)(2,1)S(1)}, bf16[1,2048,384]{2,1,0:T(8,128)(2,1)}, u32[]{:S(2)}) copy-start(bf16[1,2048,384]{2,1,0:T(8,128)(2,1)} %param.12) | copy-start | bytes 4718596
  61.4 10.5 %copy-start.9 = (bf16[1,2048,384]{2,1,0:T(8,128)(2,1)S(1)}, bf16[1,2048,384]{2,1,0:T(8,128)(2,1)}, u32[]{:S(2)}) copy-start(bf16[1,2048,384]{2,1,0:T(8,128)(2,1)} %param.11) | copy-start | bytes 4718596
  63.5 5.0 %collective-permute-start.3 = (bf16[32,2048]{1,0:T(8,128)(2,1)S(1)}, bf16[32,2048]{1,0:T(8,128)(2,1)S(1)}, u32[]{:S(2)}, u32[]{:S(2)}) collective-permute-start(bf16[32,2048]{1,0:T(8,128)(2,1)S(1)} %slice.373), channel_id=1, source_target_pairs={{0,4},{1,5},{4,8},{5,9},{8,12},{9,13},{12,14},{13,15},{14,10},{15,... | collective-permute-start | bytes 393224 | tf_op jit(solution)/shard_map/ppermute | solution.py:40
  64.6 5.0 %collective-permute-start.7 = (bf16[32,2048]{1,0:T(8,128)(2,1)S(1)}, bf16[32,2048]{1,0:T(8,128)(2,1)S(1)}, u32[]{:S(2)}, u32[]{:S(2)}) collective-permute-start(bf16[32,2048]{1,0:T(8,128)(2,1)S(1)} %slice.374), channel_id=1, source_target_pairs={{0,2},{1,3},{4,0},{5,1},{8,4},{9,5},{12,8},{13,9},{14,12},{15,13},... | collective-permute-start | bytes 393224 | tf_op jit(solution)/shard_map/ppermute | solution.py:40
  71.9 4.6 %copy-start.11 = (bf16[2048,384]{1,0:T(8,128)(2,1)}, bf16[2048,384]{1,0:T(8,128)(2,1)S(1)}, u32[]{:S(2)}) copy-start(bf16[2048,384]{1,0:T(8,128)(2,1)S(1)} %collective-permute-done.9) | copy-start | bytes 4718596
  76.8 6.1 %copy-start.12 = (bf16[384,2048]{1,0:T(8,128)(2,1)}, bf16[384,2048]{1,0:T(8,128)(2,1)S(1)}, u32[]{:S(2)}) copy-start(bf16[384,2048]{1,0:T(8,128)(2,1)S(1)} %collective-permute-done.10) | copy-start | bytes 4718596
  102.6 18.3 %collective-permute-start.37 = (f32[128,8]{0,1:T(8,128)S(1)}, f32[128,8]{0,1:T(8,128)S(1)}, u32[]{:S(2)}, u32[]{:S(2)}) collective-permute-start(f32[128,8]{0,1:T(8,128)S(1)} %dynamic-slice_bitcast_fusion.1), channel_id=1, source_target_pairs={{0,1},{1,0},{2,3},{3,2},{4,5},{5,4},{6,7},{7,6},{8,9},{9,8},{10,11... | collective-permute-start | bytes 12296 | tf_op jit(solution)/shard_map/ppermute | solution.py:13
  102.9 2.9 %copy-start.13 = (bf16[384,2048]{1,0:T(8,128)(2,1)S(1)}, bf16[384,2048]{1,0:T(8,128)(2,1)}, u32[]{:S(2)}) copy-start(bf16[384,2048]{1,0:T(8,128)(2,1)} %copy-done.12) | copy-start | bytes 4718596
  102.9 2.9 %copy-start.14 = (bf16[512,768]{1,0:T(8,128)(2,1)S(1)}, bf16[512,768]{1,0:T(8,128)(2,1)}, u32[]{:S(2)}) copy-start(bf16[512,768]{1,0:T(8,128)(2,1)} %get-tuple-element.10) | copy-start | bytes 2359300
  105.8 3.9 %copy-start.2 = (bf16[512,768]{1,0:T(8,128)(2,1)S(1)}, bf16[512,768]{1,0:T(8,128)(2,1)}, u32[]{:S(2)}) copy-start(bf16[512,768]{1,0:T(8,128)(2,1)} %get-tuple-element.11) | copy-start | bytes 2359300
  107.7 13.8 %collective-permute-start.11 = (bf16[32,2048]{1,0:T(8,128)(2,1)S(1)}, bf16[32,2048]{1,0:T(8,128)(2,1)S(1)}, u32[]{:S(2)}, u32[]{:S(2)}) collective-permute-start(bf16[32,2048]{1,0:T(8,128)(2,1)S(1)} %get-tuple-element.28), channel_id=1, source_target_pairs={{0,4},{1,5},{4,8},{5,9},{8,12},{9,13},{12,14},{13,15},{14,10},{15,... | collective-permute-start | bytes 393224 | tf_op jit(solution)/shard_map/ppermute | solution.py:40
  107.8 14.2 %collective-permute-start.15 = (bf16[32,2048]{1,0:T(8,128)(2,1)S(1)}, bf16[32,2048]{1,0:T(8,128)(2,1)S(1)}, u32[]{:S(2)}, u32[]{:S(2)}) collective-permute-start(bf16[32,2048]{1,0:T(8,128)(2,1)S(1)} %get-tuple-element.29), channel_id=1, source_target_pairs={{0,2},{1,3},{4,0},{5,1},{8,4},{9,5},{12,8},{13,9},{14,12},{15,13},... | collective-permute-start | bytes 393224 | tf_op jit(solution)/shard_map/ppermute | solution.py:40
  118.8 5.1 %collective-permute-start.27 = (bf16[32,2048]{1,0:T(8,128)(2,1)S(1)}, bf16[32,2048]{1,0:T(8,128)(2,1)S(1)}, u32[]{:S(2)}, u32[]{:S(2)}) collective-permute-start(bf16[32,2048]{1,0:T(8,128)(2,1)S(1)} %get-tuple-element.20), channel_id=1, source_target_pairs={{0,4},{1,5},{4,8},{5,9},{8,12},{9,13},{12,14},{13,15},{14,10},{15,... | collective-permute-start | bytes 393224 | tf_op jit(solution)/shard_map/ppermute | solution.py:40
  119.1 5.3 %collective-permute-start.31 = (bf16[32,2048]{1,0:T(8,128)(2,1)S(1)}, bf16[32,2048]{1,0:T(8,128)(2,1)S(1)}, u32[]{:S(2)}, u32[]{:S(2)}) collective-permute-start(bf16[32,2048]{1,0:T(8,128)(2,1)S(1)} %get-tuple-element.21), channel_id=1, source_target_pairs={{0,2},{1,3},{4,0},{5,1},{8,4},{9,5},{12,8},{13,9},{14,12},{15,13},... | collective-permute-start | bytes 393224 | tf_op jit(solution)/shard_map/ppermute | solution.py:40
  120.9 53.9 %collective-permute-start.36 = (bf16[384,2048]{1,0:T(8,128)(2,1)S(1)}, bf16[384,2048]{1,0:T(8,128)(2,1)S(1)}, u32[]{:S(2)}, u32[]{:S(2)}) collective-permute-start(bf16[384,2048]{1,0:T(8,128)(2,1)S(1)} %convolution_convert_fusion.3), channel_id=1, source_target_pairs={{0,1},{1,0},{2,3},{3,2},{4,5},{5,4},{6,7},{7,6},{8,9},{9,8},{10,11... | collective-permute-start | bytes 4718600 | tf_op jit(solution)/shard_map/ppermute | solution.py:13
  121.5 55.5 %collective-permute-start.35 = (bf16[2048,768]{1,0:T(8,128)(2,1)S(1)}, bf16[2048,768]{1,0:T(8,128)(2,1)S(1)}, u32[]{:S(2)}, u32[]{:S(2)}) collective-permute-start(bf16[2048,768]{1,0:T(8,128)(2,1)S(1)} %convolution_convert_fusion), channel_id=1, source_target_pairs={{0,1},{1,0},{2,3},{3,2},{4,5},{5,4},{6,7},{7,6},{8,9},{9,8},{10,11... | collective-permute-start | bytes 9437192 | tf_op jit(solution)/shard_map/ppermute | solution.py:13
  122.1 17.1 %collective-permute-start.16 = (bf16[64,2048]{1,0:T(8,128)(2,1)S(1)}, bf16[64,2048]{1,0:T(8,128)(2,1)S(1)}, u32[]{:S(2)}, u32[]{:S(2)}) collective-permute-start(bf16[64,2048]{1,0:T(8,128)(2,1)S(1)} %pad_maximum_fusion.9), channel_id=1, source_target_pairs={{0,2},{1,3},{4,0},{5,1},{8,4},{9,5},{12,8},{13,9},{14,12},{15,13},... | collective-permute-start | bytes 786440 | tf_op jit(solution)/shard_map/ppermute | solution.py:40
  123.9 6.8 %collective-permute-start.12 = (bf16[64,2048]{1,0:T(8,128)(2,1)S(1)}, bf16[64,2048]{1,0:T(8,128)(2,1)S(1)}, u32[]{:S(2)}, u32[]{:S(2)}) collective-permute-start(bf16[64,2048]{1,0:T(8,128)(2,1)S(1)} %pad_maximum_fusion.8), channel_id=1, source_target_pairs={{0,4},{1,5},{4,8},{5,9},{8,12},{9,13},{12,14},{13,15},{14,10},{15,... | collective-permute-start | bytes 786440 | tf_op jit(solution)/shard_map/ppermute | solution.py:40
  124.5 24.0 %collective-permute-start.32 = (bf16[64,2048]{1,0:T(8,128)(2,1)S(1)}, bf16[64,2048]{1,0:T(8,128)(2,1)S(1)}, u32[]{:S(2)}, u32[]{:S(2)}) collective-permute-start(bf16[64,2048]{1,0:T(8,128)(2,1)S(1)} %pad_maximum_fusion.11), channel_id=1, source_target_pairs={{0,2},{1,3},{4,0},{5,1},{8,4},{9,5},{12,8},{13,9},{14,12},{15,13},... | collective-permute-start | bytes 786440 | tf_op jit(solution)/shard_map/ppermute | solution.py:40
  130.7 6.4 %collective-permute-start.28 = (bf16[64,2048]{1,0:T(8,128)(2,1)S(1)}, bf16[64,2048]{1,0:T(8,128)(2,1)S(1)}, u32[]{:S(2)}, u32[]{:S(2)}) collective-permute-start(bf16[64,2048]{1,0:T(8,128)(2,1)S(1)} %pad_maximum_fusion.10), channel_id=1, source_target_pairs={{0,4},{1,5},{4,8},{5,9},{8,12},{9,13},{12,14},{13,15},{14,10},{15,... | collective-permute-start | bytes 786440 | tf_op jit(solution)/shard_map/ppermute | solution.py:40
  137.0 9.2 %collective-permute-start.13 = (bf16[64,2048]{1,0:T(8,128)(2,1)S(1)}, bf16[64,2048]{1,0:T(8,128)(2,1)S(1)}, u32[]{:S(2)}, u32[]{:S(2)}) collective-permute-start(bf16[64,2048]{1,0:T(8,128)(2,1)S(1)} %add_convert_fusion.10), channel_id=1, source_target_pairs={{0,4},{1,5},{4,8},{5,9},{8,12},{9,13},{12,14},{13,15},{14,10},{15,... | collective-permute-start | bytes 786440 | tf_op jit(solution)/shard_map/ppermute | solution.py:40
  139.2 12.7 %collective-permute-start.29 = (bf16[64,2048]{1,0:T(8,128)(2,1)S(1)}, bf16[64,2048]{1,0:T(8,128)(2,1)S(1)}, u32[]{:S(2)}, u32[]{:S(2)}) collective-permute-start(bf16[64,2048]{1,0:T(8,128)(2,1)S(1)} %add_convert_fusion.5), channel_id=1, source_target_pairs={{0,4},{1,5},{4,8},{5,9},{8,12},{9,13},{12,14},{13,15},{14,10},{15,... | collective-permute-start | bytes 786440 | tf_op jit(solution)/shard_map/ppermute | solution.py:40
  146.4 18.9 %collective-permute-start.14 = (bf16[64,2048]{1,0:T(8,128)(2,1)S(1)}, bf16[64,2048]{1,0:T(8,128)(2,1)S(1)}, u32[]{:S(2)}, u32[]{:S(2)}) collective-permute-start(bf16[64,2048]{1,0:T(8,128)(2,1)S(1)} %get-tuple-element.24), channel_id=1, source_target_pairs={{0,4},{1,5},{4,8},{5,9},{8,12},{9,13},{12,14},{13,15},{14,10},{15,... | collective-permute-start | bytes 786440 | tf_op jit(solution)/shard_map/ppermute | solution.py:40
  148.5 7.2 %collective-permute-start.17 = (bf16[64,2048]{1,0:T(8,128)(2,1)S(1)}, bf16[64,2048]{1,0:T(8,128)(2,1)S(1)}, u32[]{:S(2)}, u32[]{:S(2)}) collective-permute-start(bf16[64,2048]{1,0:T(8,128)(2,1)S(1)} %get-tuple-element.25), channel_id=1, source_target_pairs={{0,2},{1,3},{4,0},{5,1},{8,4},{9,5},{12,8},{13,9},{14,12},{15,13},... | collective-permute-start | bytes 786440 | tf_op jit(solution)/shard_map/ppermute | solution.py:40
  152.0 20.0 %collective-permute-start.30 = (bf16[64,2048]{1,0:T(8,128)(2,1)S(1)}, bf16[64,2048]{1,0:T(8,128)(2,1)S(1)}, u32[]{:S(2)}, u32[]{:S(2)}) collective-permute-start(bf16[64,2048]{1,0:T(8,128)(2,1)S(1)} %get-tuple-element.16), channel_id=1, source_target_pairs={{0,4},{1,5},{4,8},{5,9},{8,12},{9,13},{12,14},{13,15},{14,10},{15,... | collective-permute-start | bytes 786440 | tf_op jit(solution)/shard_map/ppermute | solution.py:40
  155.7 19.1 %copy-start.4 = (bf16[512,2048]{1,0:T(8,128)(2,1)S(1)}, bf16[512,2048]{1,0:T(8,128)(2,1)}, u32[]{:S(2)}) copy-start(bf16[512,2048]{1,0:T(8,128)(2,1)} %constant_dynamic-update-slice_fusion.9) | copy-start | bytes 6291460
  155.7 19.1 %copy-start.15 = (bf16[512,768]{1,0:T(8,128)(2,1)S(1)}, bf16[512,768]{1,0:T(8,128)(2,1)}, u32[]{:S(2)}) copy-start(bf16[512,768]{1,0:T(8,128)(2,1)} %get-tuple-element.10) | copy-start | bytes 2359300
  155.7 9.1 %collective-permute-start.33 = (bf16[64,2048]{1,0:T(8,128)(2,1)S(1)}, bf16[64,2048]{1,0:T(8,128)(2,1)S(1)}, u32[]{:S(2)}, u32[]{:S(2)}) collective-permute-start(bf16[64,2048]{1,0:T(8,128)(2,1)S(1)} %get-tuple-element.17), channel_id=1, source_target_pairs={{0,2},{1,3},{4,0},{5,1},{8,4},{9,5},{12,8},{13,9},{14,12},{15,13},... | collective-permute-start | bytes 786440 | tf_op jit(solution)/shard_map/ppermute | solution.py:40
  164.8 6.4 %collective-permute-start.18 = (bf16[64,2048]{1,0:T(8,128)(2,1)S(1)}, bf16[64,2048]{1,0:T(8,128)(2,1)S(1)}, u32[]{:S(2)}, u32[]{:S(2)}) collective-permute-start(bf16[64,2048]{1,0:T(8,128)(2,1)S(1)} %add_convert_fusion.7), channel_id=1, source_target_pairs={{0,2},{1,3},{4,0},{5,1},{8,4},{9,5},{12,8},{13,9},{14,12},{15,13},... | collective-permute-start | bytes 786440 | tf_op jit(solution)/shard_map/ppermute | solution.py:40
  165.3 8.7 %collective-permute-start.34 = (bf16[64,2048]{1,0:T(8,128)(2,1)S(1)}, bf16[64,2048]{1,0:T(8,128)(2,1)S(1)}, u32[]{:S(2)}, u32[]{:S(2)}) collective-permute-start(bf16[64,2048]{1,0:T(8,128)(2,1)S(1)} %add_convert_fusion.2), channel_id=1, source_target_pairs={{0,2},{1,3},{4,0},{5,1},{8,4},{9,5},{12,8},{13,9},{14,12},{15,13},... | collective-permute-start | bytes 786440 | tf_op jit(solution)/shard_map/ppermute | solution.py:40
  (6 other events, 13.7 us)

commit v2 on v1

--- a/solution.py
+++ b/solution.py
@@ -1,6 +1,8 @@
 import jax
 import jax.numpy as jnp
 from jax import lax
+from jax.experimental import pallas as pl
+from jax.experimental.pallas import tpu as pltpu
 from jax.sharding import PartitionSpec as P
 
 F32 = jnp.float32
@@ -25,13 +27,14 @@
     return lax.dot_general(left, right, (((0,), (0,)), ((), ())), preferred_element_type=F32)
 
 
-def ring_chips(chips):
-    return list(range(0, chips, 2)) + list(range(chips - 1, 0, -2))
+LANES = 128
+PIECES = 3
+MIB = 2**20
 
 
 def ring_send(value, step):
     chips = lax.axis_size("expert") // 2
-    ring = ring_chips(chips)
+    ring = list(range(0, chips, 2)) + list(range(chips - 1, 0, -2))
     pairs = [
         (2 * ring[place] + core, 2 * ring[(place + step) % chips] + core)
         for place in range(chips)
@@ -40,131 +43,516 @@
     return lax.ppermute(value, "expert", pairs)
 
 
-def ring_gather(block, chips):
-    far = chips // 2
-    half = block.shape[0] // 2
-    behind, ahead = [block], [block]
-    for _ in range(far - 1):
-        behind.append(ring_send(behind[-1], 1))
-        ahead.append(ring_send(ahead[-1], -1))
-    upper = ring_send(behind[-1][:half], 1)
-    lower = ring_send(ahead[-1][half:], -1)
-    return behind + [upper, lower] + ahead[:0:-1]
-
-
-def ring_scatter(terms, chips):
-    far = chips // 2
-    half = terms(0).shape[0] // 2
-    total = terms(0).astype(F32)
-    for step, span in ((1, slice(0, half)), (-1, slice(half, 2 * half))):
-        moving = ring_send(terms(far)[span], step)
-        for distance in range(far - 1, 0, -1):
-            own = terms((-step * distance) % chips).astype(F32)
-            if distance == far - 1:
-                joined = own[span] + moving.astype(F32)
-                own = jnp.concatenate([joined, own[half:]] if step == 1 else [own[:half], joined])
-            else:
-                own = own + moving.astype(F32)
-            moving = ring_send(own.astype(BF16), step)
-        total = total + moving.astype(F32)
-    return total
+def after(values, *firsts):
+    return lax.optimization_barrier((values, firsts))[0]
+
+
+def kernel_call(body, name, outs, ins, scratch=(), flops=0, limit=8, **more):
+    moved = sum(a.size * a.dtype.itemsize for a in (*ins, *outs))
+    return pl.pallas_call(
+        body,
+        name=name,
+        out_shape=outs,
+        scratch_shapes=scratch,
+        compiler_params=pltpu.CompilerParams(vmem_limit_bytes=limit * MIB),
+        cost_estimate=pl.CostEstimate(flops=flops, bytes_accessed=moved, transcendentals=0),
+        **more,
+    )(*ins)
+
+
+VMEM = pl.BlockSpec(memory_space=pltpu.VMEM)
+ANY = pl.BlockSpec(memory_space=pl.ANY)
+
+
+def lane_ids(rows):
+    return lax.broadcasted_iota(jnp.int32, (rows, LANES), 1)
+
+
+def pack_block(tokens, grad_out, ids):
+    count, width = tokens.shape
+
+    def body(tokens_ref, grads_ref, ids_ref, block_ref):
+        block_ref[:, :width] = tokens_ref[...]
+        block_ref[:, width : 2 * width] = grads_ref[...]
+        block_ref[:, 2 * width :] = ids_ref[...]
+
+    out = jax.ShapeDtypeStruct((count, 2 * width + LANES), BF16)
+    return kernel_call(body, "pack_block", (out,), (tokens, grad_out, ids))[0]
+
+
+def pack_weights(own, other):
+    depth, width = own[0].shape
+    steps = 4
+    tile = depth // steps
+
+    def body(gate_ref, up_ref, down_ref, gate_other_ref, up_other_ref, down_other_ref, in_ref, out_ref):
+        for i, ref in enumerate((gate_ref, gate_other_ref, up_ref, up_other_ref)):
+            in_ref[:, i * width : (i + 1) * width] = ref[...]
+        out_ref[:width] = down_ref[...]
+        out_ref[width:] = down_other_ref[...]
+
+    in_spec = pl.BlockSpec((tile, width), lambda d: (d, 0))
+    down_spec = pl.BlockSpec((width, tile), lambda d: (0, d))
+    return kernel_call(
+        body,
+        "pack_weights",
+        (
+            jax.ShapeDtypeStruct((depth, 4 * width), BF16),
+            jax.ShapeDtypeStruct((2 * width, depth), BF16),
+        ),
+        (*own, *other),
+        grid=(steps,),
+        in_specs=[in_spec, in_spec, down_spec] * 2,
+        out_specs=[
+            pl.BlockSpec((tile, 4 * width), lambda d: (d, 0)),
+            pl.BlockSpec((2 * width, tile), lambda d: (0, d)),
+        ],
+        limit=16,
+    )
+
+
+def expert_chunk(blocks, weights, router, behind, where, per_token, part):
+    number = len(blocks)
+    stride = blocks[0].shape[1]
+    spans, total = [], 0
+    for block in blocks:
+        spans.append(slice(total, total + block.shape[0]))
+        total += block.shape[0]
+    width, model_width = weights[1].shape[0] // 2, weights[1].shape[1]
+
+    def body(*refs):
+        block_refs, refs = refs[:number], refs[number:]
+        in_ref, down_ref, router_ref, behind_ref, where_ref = refs[:5]
+        made_refs, refs = refs[5 : 5 + number], refs[5 + number :]
+        hidden_refs, delta_refs = refs[:2], refs[2:4]
+        side_ref, column_ref, both_ref, delta_ref = refs[4:]
+        for i in range(number):
+            both_ref[spans[i], :] = block_refs[i][...]
+        rows = both_ref[:, :model_width]
+        grads = both_ref[:, model_width : 2 * model_width]
+        ids = both_ref[:, 2 * model_width :].astype(F32)
+        logits = dot(rows, router_ref[...])
+        named = jnp.zeros((total, LANES), F32)
+        for k in range(per_token):
+            named = named + jnp.where(ids[:, k : k + 1] == behind_ref[...], 1.0, 0.0)
+        probability = named * jax.nn.sigmoid(logits)
+        summed = jnp.sum(probability, axis=1, keepdims=True)
+        gates = probability / summed
+        side_ref[:, :LANES] = gates
+        side_ref[:, LANES : 2 * LANES] = probability * (1.0 - probability) / summed
+        gate = gates[:, :1]
+        first = pl.multiple_of(where_ref[0] * 2 * part, 2 * part)
+        column_ref[...] = both_ref[:, pl.ds(first, 2 * part)]
+        before = dot(rows, in_ref[...])
+        pre_gate, pre_up = before[:, : 2 * width], before[:, 2 * width :]
+        squash = jax.nn.sigmoid(pre_gate)
+        activated = pre_gate * squash
+        hidden = activated * pre_up
+        hidden_gated = (gate * hidden).astype(BF16)
+        back_hidden = dot_nt(grads, down_ref[...])
+        slope = jnp.sum(hidden * back_hidden, axis=1, keepdims=True)
+        side_ref[:, 2 * LANES :] = jnp.broadcast_to(slope, (total, LANES))
+        back_hidden = gate * back_hidden
+        gate_delta = back_hidden * pre_up * squash * (1.0 + pre_gate * (1.0 - squash))
+        gate_delta, up_delta = gate_delta.astype(BF16), (back_hidden * activated).astype(BF16)
+        delta_ref[:, : 2 * width] = gate_delta
+        delta_ref[:, 2 * width :] = up_delta
+        for h in range(2):
+            half = slice(h * width, (h + 1) * width)
+            hidden_refs[h][...] = hidden_gated[:, half]
+            delta_refs[h][:, :width] = gate_delta[:, half]
+            delta_refs[h][:, width:] = up_delta[:, half]
+        out = dot(hidden_gated, down_ref[...]).astype(BF16)
+        back = dot_nt(delta_ref[...], in_ref[...]).astype(BF16)
+        for i in range(number):
+            made_refs[i][:, :model_width] = out[spans[i]]
+            made_refs[i][:, model_width:] = back[spans[i]]
+
+    outs = (
+        *(jax.ShapeDtypeStruct((block.shape[0], 2 * model_width), BF16) for block in blocks),
+        *(jax.ShapeDtypeStruct((total, width), BF16) for _ in range(2)),
+        *(jax.ShapeDtypeStruct((total, 2 * width), BF16) for _ in range(2)),
+        jax.ShapeDtypeStruct((total, 3 * LANES), F32),
+        jax.ShapeDtypeStruct((total, 2 * part), BF16),
+        jax.ShapeDtypeStruct((total, stride), BF16),
+    )
+    made = kernel_call(
+        body,
+        "expert_chunk",
+        outs,
+        (*blocks, *weights, router, behind, where),
+        scratch=[pltpu.VMEM((total, 4 * width), BF16)],
+        limit=24,
+        flops=24 * total * model_width * width,
+        in_specs=[VMEM] * (number + 4) + [pl.BlockSpec(memory_space=pltpu.SMEM)],
+        out_specs=[VMEM] * len(outs),
+    )
+    return made[:number], made[number : number + 2], made[number + 2 : number + 4], made[-3:]
+
+
+def first_messages(upper, lower, sides, layout):
+    half, stride = upper.shape
+    count = 2 * half
+    chips = len(layout)
+
+    def body(upper_ref, lower_ref, *refs):
+        side_refs, (up_ref, down_ref, slopes_ref) = refs[: len(sides)], refs[len(sides) :]
+        table = jnp.zeros((count, LANES), F32)
+        for k, (index, offset) in enumerate(layout):
+            column = side_refs[index][offset : offset + count, :]
+            table = jnp.where(lane_ids(count) == k, column, table)
+        packed = jnp.zeros((count, LANES), F32)
+        for piece in range(PIECES):
+            part = table.astype(BF16).astype(F32)
+            table = table - part
+            packed = packed + (part if piece == 0 else pltpu.roll(part, piece * chips, 1))
+        packed = packed[:half] + pltpu.roll(packed[half:], PIECES * chips, 1)
+        packed = packed.astype(BF16)
+        slopes_ref[...] = packed
+        up_ref[:, :stride] = upper_ref[...]
+        up_ref[:, stride:] = packed
+        down_ref[:, :stride] = lower_ref[...]
+        down_ref[:, stride:] = packed
+
+    outs = (
+        jax.ShapeDtypeStruct((half, stride + LANES), BF16),
+        jax.ShapeDtypeStruct((half, stride + LANES), BF16),
+        jax.ShapeDtypeStruct((half, LANES), BF16),
+    )
+    slope_specs = [pl.BlockSpec((side.shape[0], LANES), lambda i: (0, 2)) for side in sides]
+    return kernel_call(
+        body,
+        "first_messages",
+        outs,
+        (upper, lower, *sides),
+        grid=(1,),
+        in_specs=[pl.BlockSpec(upper.shape, lambda i: (0, 0))] * 2 + slope_specs,
+        out_specs=[pl.BlockSpec(o.shape, lambda i: (0, 0)) for o in outs],
+    )
+
+
+def next_message(got, made, slopes=None, upper=None, wait_for=()):
+    count, stride = made.shape
+    half = count // 2
+    small = got.shape[0] == half
+
+    def body(got_ref, made_ref, *refs):
+        message_ref = refs[-1]
+        if small:
+            near, rest = (slice(0, half), slice(half, count)) if upper else (slice(half, count), slice(0, half))
+            message_ref[near, :stride] = (
+                made_ref[near].astype(F32) + got_ref[:, :stride].astype(F32)
+            ).astype(BF16)
+            message_ref[rest, :stride] = made_ref[rest]
+        else:
+            message_ref[:, :stride] = (
+                made_ref[...].astype(F32) + got_ref[:, :stride].astype(F32)
+            ).astype(BF16)
+        message_ref[:half, stride:] = refs[0][...] if slopes is not None else got_ref[:half, stride:]
+        message_ref[half:, stride:] = jnp.zeros((count - half, LANES), BF16)
+
+    ins = (got, made) if slopes is None else (got, made, slopes)
+    out = jax.ShapeDtypeStruct((count, stride + LANES), BF16)
+    return kernel_call(
+        body,
+        "next_message",
+        (out,),
+        (*ins, *wait_for),
+        flops=count * stride,
+        in_specs=[VMEM] * len(ins) + [ANY] * len(wait_for),
+        out_specs=[VMEM],
+    )[0]
+
+
+def weight_parts(arrived, hidden, delta, half=None, received=None, wait_for=()):
+    number = len(arrived)
+    total = sum(a.shape[0] for a in arrived)
+    model_width = (arrived[0].shape[1] - LANES) // 2
+    width = hidden[0].shape[1]
+    tile = 256 if model_width % 256 == 0 else model_width
+    every = model_width // tile
+    steps, skip = (every, 0) if half is None else (every // 2, half * (every // 2))
+    chunks = len(hidden)
+
+    def body(*refs):
+        token_refs, grad_refs = refs[:number], refs[number : 2 * number]
+        hidden_refs = refs[2 * number : 2 * number + chunks]
+        delta_refs = refs[2 * number + chunks : 2 * number + 2 * chunks]
+        rest = refs[2 * number + 2 * chunks + len(wait_for) : -2]
+        hidden_ref, delta_ref = refs[-2:]
+
+        @pl.when(pl.program_id(0) == 0)
+        def _():
+            first = 0
+            for i in range(chunks):
+                last = first + hidden_refs[i].shape[0]
+                delta_ref[first:last, :] = delta_refs[i][...]
+                first = last
+            hidden_ref[...] = jnp.concatenate([ref[...] for ref in hidden_refs], axis=0).T
+
+        mark_ref = rest[-1]
+        mark_ref[...] = jnp.zeros(mark_ref.shape, F32)
+        rows = jnp.concatenate([ref[...] for ref in token_refs], axis=0)
+        grads = jnp.concatenate([ref[...] for ref in grad_refs], axis=0)
+        into = dot_tn(rows, delta_ref[...])
+        down = dot(hidden_ref[...], grads)
+        if received is None:
+            gate_ref, up_ref, down_ref, _ = rest
+            gate_ref[...] = into[:, :width].astype(BF16)
+            up_ref[...] = into[:, width:].astype(BF16)
+            down_ref[...] = down.astype(BF16)
+        else:
+            gate_ref, up_ref, down_ref, _ = rest[6:]
+            early = pl.program_id(0) < every // 2
+            got_gate, got_up, got_down = (
+                jnp.where(early, rest[i][...], rest[3 + i][...]).astype(F32) for i in range(3)
+            )
+            gate_ref[0] = (into[:, :width] + got_gate).astype(BF16)
+            up_ref[0] = (into[:, width:] + got_up).astype(BF16)
+            down_ref[0] = (down + got_down).astype(BF16)
+
+    def whole(a):
+        return pl.BlockSpec(a.shape, lambda d: (0, 0))
+
+    in_specs = [pl.BlockSpec((a.shape[0], tile), lambda d: (0, skip + d)) for a in arrived]
+    in_specs += [pl.BlockSpec((a.shape[0], tile), lambda d: (0, every + skip + d)) for a in arrived]
+    in_specs += [whole(a) for a in (*hidden, *delta)]
+    in_specs += [ANY] * len(wait_for)
+    ins = (*arrived, *arrived, *hidden, *delta, *wait_for)
+    if received is None:
+        shapes = [(model_width // 2, width)] * 2 + [(width, model_width // 2)]
+        out_specs = [pl.BlockSpec((tile, width), lambda d: (d, 0))] * 2
+        out_specs += [pl.BlockSpec((width, tile), lambda d: (0, d))]
+    else:
+        shapes = [(1, model_width, width)] * 2 + [(1, width, model_width)]
+        out_specs = [pl.BlockSpec((1, tile, width), lambda d: (0, d, 0))] * 2
+        out_specs += [pl.BlockSpec((1, width, tile), lambda d: (0, 0, d))]
+        last = every // 2 - 1
+        in_specs += [pl.BlockSpec((tile, width), lambda d: (jnp.minimum(d, last), 0))] * 2
+        in_specs += [pl.BlockSpec((width, tile), lambda d: (0, jnp.minimum(d, last)))]
+        in_specs += [pl.BlockSpec((tile, width), lambda d: (jnp.maximum(d - last - 1, 0), 0))] * 2
+        in_specs += [pl.BlockSpec((width, tile), lambda d: (0, jnp.maximum(d - last - 1, 0)))]
+        ins += received
+    outs = [jax.ShapeDtypeStruct(shape, BF16) for shape in shapes]
+    outs = (*outs, jax.ShapeDtypeStruct((8, LANES), F32))
+    out_specs.append(pl.BlockSpec((8, LANES), lambda d: (0, 0)))
+    return kernel_call(
+        body,
+        "weight_parts",
+        outs,
+        ins,
+        scratch=[pltpu.VMEM((width, total), BF16), pltpu.VMEM((total, 2 * width), BF16)],
+        flops=6 * total * tile * steps * width,
+        grid=(steps,),
+        in_specs=in_specs,
+        out_specs=out_specs,
+    )
+
+
+def router_parts(where, pieces, passed, slopes, sides, layout, order, experts, mark):
+    chips = len(layout)
+    number = len(pieces)
+    half, stride = passed[0].shape[0] // 2, passed[0].shape[1]
+    count, part = 2 * half, pieces[0].shape[1] // 2
+
+    def body(where_ref, *refs):
+        column_refs, refs = refs[:number], refs[number:]
+        passed_refs, slopes_ref, refs = refs[: chips - 1], refs[chips - 1], refs[chips:]
+        side_refs = refs[: len(sides)]
+        delta_ref, keep_ref, send_ref, total_ref = refs[len(sides) + 1 :]
+        tables = []
+        for k in range(chips):
+            packed = (slopes_ref if k == 0 else passed_refs[k - 1])[...].astype(F32)
+            halves = []
+            for rows in range(2):
+                table = jnp.zeros((half, LANES), F32)
+                for piece in range(PIECES):
+                    first = (PIECES * rows + piece) * chips
+                    table = table + (packed if first == 0 else pltpu.roll(packed, LANES - first, 1))
+                halves.append(table)
+            tables.append(jnp.concatenate(halves, axis=0))
+        sub = lax.broadcasted_iota(jnp.int32, (LANES, LANES), 0)
+        lane = lane_ids(LANES)
+        turn = jnp.zeros((LANES, LANES), F32)
+        for k in range(chips):
+            turn = jnp.where((sub == k) & (lane == where_ref[2 + k]), 1.0, turn)
+        turn = turn.astype(BF16)
+        deltas = []
+        for q in range(chips):
+            slope = jnp.zeros((count, LANES), F32)
+            for k in range(chips):
+                from_lane = (q - k) % chips
+                column = tables[k][:, from_lane : from_lane + 1]
+                slope = jnp.where(lane_ids(count) == k, column, slope)
+            index, offset = layout[q]
+            gates = side_refs[index][offset : offset + count, :LANES]
+            factor = side_refs[index][offset : offset + count, LANES : 2 * LANES]
+            middle = jnp.sum(gates * slope, axis=1, keepdims=True)
+            delta = (factor * (slope - middle)).astype(BF16)
+            deltas.append(dot(delta, turn).astype(BF16))
+        delta_ref[...] = deltas[0]
+        columns = jnp.concatenate([ref[...] for ref in column_refs], axis=0)
+        total_ref[...] = dot_tn(columns, jnp.concatenate([deltas[q] for q in order], axis=0))
+        core = where_ref[1]
+        own, other = pl.multiple_of(core * part, part), pl.multiple_of((1 - core) * part, part)
+        keep_ref[...] = total_ref[pl.ds(own, part), :experts]
+        send_ref[...] = total_ref[pl.ds(other, part), :experts]
+
+    info = stride // LANES - 1
+    in_specs = [pl.BlockSpec(a.shape, lambda i, w: (0, 0)) for a in pieces]
+    in_specs += [pl.BlockSpec((half, LANES), lambda i, w: (0, info)) for _ in range(chips - 1)]
+    in_specs += [pl.BlockSpec(slopes.shape, lambda i, w: (0, 0))]
+    in_specs += [pl.BlockSpec((side.shape[0], 2 * LANES), lambda i, w: (0, 0)) for side in sides]
+    outs = (
+        jax.ShapeDtypeStruct((count, LANES), BF16),
+        jax.ShapeDtypeStruct((part, experts), F32),
+        jax.ShapeDtypeStruct((part, experts), F32),
+    )
+    in_specs += [ANY]
+    ins = (where, *pieces, *passed, slopes, *sides, mark)
+    return pl.pallas_call(
+        body,
+        name="router_parts",
+        out_shape=outs,
+        grid_spec=pltpu.PrefetchScalarGridSpec(
+            num_scalar_prefetch=1,
+            grid=(1,),
+            in_specs=in_specs,
+            out_specs=[pl.BlockSpec(o.shape, lambda i, w: (0, 0)) for o in outs],
+            scratch_shapes=[pltpu.VMEM((2 * part, LANES), F32)],
+        ),
+        compiler_params=pltpu.CompilerParams(vmem_limit_bytes=8 * MIB),
+        cost_estimate=pl.CostEstimate(flops=10**7, bytes_accessed=10**6, transcendentals=0),
+    )(*ins)
+
+
+def last_sums(got_up, got_down, made, delta, router):
+    count, stride = made.shape
+    model_width = stride // 2
+
+    def body(up_ref, down_ref, made_ref, delta_ref, router_ref, mixed_ref, grad_ref):
+        total = (
+            made_ref[...].astype(F32)
+            + up_ref[:, :stride].astype(F32)
+            + down_ref[:, :stride].astype(F32)
+        )
+        mixed_ref[...] = total[:, :model_width].astype(BF16)
+        grad_ref[...] = (
+            total[:, model_width:] + dot_nt(delta_ref[...], router_ref[...])
+        ).astype(BF16)
+
+    out = jax.ShapeDtypeStruct((count, model_width), BF16)
+    return kernel_call(body, "last_sums", (out, out), (got_up, got_down, made, delta, router))
 
 
 def all_tokens_pass(
     tokens, grad_out, expert_ids, router_weight, gate_weight, up_weight, down_weight
 ):
     chips = lax.axis_size("expert") // 2
-    rows_own, model_width = tokens.shape
+    far = chips // 2
+    count = tokens.shape[0]
+    half = count // 2
+    per_token = expert_ids.shape[1]
     experts = router_weight.shape[1]
-    width = gate_weight.shape[2]
     device = lax.axis_index("expert")
     chip, core = device // 2, device % 2
     place = jnp.where(chip % 2 == 0, chip // 2, chips - 1 - chip // 2)
-
-    def around(array, axis):
-        turned = jnp.concatenate(
-            [lax.slice_in_dim(array, 0, 1, axis=axis)]
-            + [lax.slice_in_dim(array, c, c + 1, axis=axis) for c in range(chips - 1, 0, -1)],
-            axis=axis,
+    behind = (place - jnp.arange(chips, dtype=jnp.int32)) % chips
+    behind = jnp.where(behind < far, 2 * behind, 2 * (chips - 1 - behind) + 1)
+    where = jnp.concatenate([jnp.stack([chip, core]).astype(jnp.int32), behind])
+    turn = (jnp.arange(experts, dtype=jnp.int32)[:, None] == behind[None, :]).astype(BF16)
+    turn = jnp.pad(turn, ((0, 0), (0, LANES - chips)))
+    router_turned = dot(router_weight, turn).astype(BF16)
+    router_wide = jnp.pad(router_weight, ((0, 0), (0, LANES - experts)))
+    behind = jnp.pad(behind.astype(F32), (0, LANES - chips), constant_values=-1.0)[None]
+
+    ids = jnp.pad(expert_ids.astype(BF16), ((0, 0), (0, LANES - per_token)))
+    block = pack_block(tokens, grad_out, ids)
+    own = after((gate_weight[0], up_weight[0], down_weight[0]), block)
+    weights = pack_weights(own, from_partner(own, "expert", 0))
+
+    arrived = {0: block}
+    made, layout, order = {}, {}, []
+    hidden, delta, sides, columns, kept = ([], []), ([], []), [], [], []
+    part = tokens.shape[1] // (2 * chips)
+
+    def work(names):
+        terms, hiddens, deltas, (side, column, both) = expert_chunk(
+            [arrived[name] for name in names],
+            weights,
+            router_turned,
+            behind,
+            where,
+            per_token,
+            part,
         )
-        twice = jnp.concatenate([turned, turned], axis=axis)
-        return lax.dynamic_slice_in_dim(twice, chips - place, chips, axis=axis)
-
-    token_blocks = ring_gather(tokens, chips)
-    grad_blocks = ring_gather(grad_out, chips)
-
-    onehot = (
-        expert_ids[:, :, None] == jnp.arange(experts, dtype=jnp.int32)[None, None, :]
-    ).astype(F32)
-    named = jnp.sum(onehot, axis=1)
-    probability = named * jax.nn.sigmoid(dot(tokens, router_weight))
-    summed = jnp.sum(probability, axis=1, keepdims=True)
-    shares = jnp.concatenate(
-        [probability / summed, probability * (1.0 - probability) / summed], axis=1
-    )
-    shares_all = lax.all_gather(shares, "expert").reshape(chips, 2, rows_own, 2 * experts)
-    shares_all = lax.dynamic_index_in_dim(shares_all, core, 1, keepdims=False)
-    shares_all = jnp.stack([shares_all[c] for c in ring_chips(chips)])
-    shares_all = around(shares_all, 0).reshape(chips * rows_own, 2 * experts)
-    gates_all, slope_all = shares_all[:, :experts], shares_all[:, experts:]
-    gate_mine = lax.dynamic_slice_in_dim(gates_all, chip, 1, axis=1)
-
-    gate_own, up_own, down_own = gate_weight[0], up_weight[0], down_weight[0]
-    gate_other, up_other, down_other = from_partner((gate_own, up_own, down_own), "expert", 0)
-    weight_in = jnp.concatenate([gate_own, up_own, gate_other, up_other], axis=1)
-    weight_out = jnp.concatenate([down_own, down_other], axis=0)
-
-    rows = jnp.concatenate(token_blocks, axis=0)
-    before = dot(rows, weight_in)
-    pre_gate = jnp.concatenate([before[:, :width], before[:, 2 * width : 3 * width]], axis=1)
-    pre_up = jnp.concatenate([before[:, width : 2 * width], before[:, 3 * width :]], axis=1)
-    squash = jax.nn.sigmoid(pre_gate)
-    activated = pre_gate * squash
-    hidden = activated * pre_up
-    hidden_gated = (gate_mine * hidden).astype(BF16)
-    out = dot(hidden_gated, weight_out).astype(BF16)
-
-    def block_of(array):
-        return lambda j: array[j * rows_own : (j + 1) * rows_own]
-
-    mixed = ring_scatter(block_of(out), chips).astype(BF16)
-
-    grads = jnp.concatenate(grad_blocks, axis=0)
-    back_hidden = dot_nt(grads, weight_out)
-    gate_slope = jnp.sum(hidden * back_hidden, axis=1)
-    back_gated = gate_mine * back_hidden
-    gate_delta = (back_gated * pre_up * squash * (1.0 + pre_gate * (1.0 - squash))).astype(BF16)
-    up_delta = (back_gated * activated).astype(BF16)
-    delta_own = jnp.concatenate([gate_delta[:, :width], up_delta[:, :width]], axis=1)
-    delta_other = jnp.concatenate([gate_delta[:, width:], up_delta[:, width:]], axis=1)
-    back = dot_nt(jnp.concatenate([delta_own, delta_other], axis=1), weight_in).astype(BF16)
-    back_sum = ring_scatter(block_of(back), chips)
-
-    in_other = from_partner(dot_tn(rows, delta_other).astype(BF16), "expert", 0).astype(F32)
-    down_other_part = from_partner(
-        dot_tn(hidden_gated[:, width:], grads).astype(BF16), "expert", 0
-    ).astype(F32)
-    in_own = dot_tn(rows, delta_own)
-    gate_grad = (in_own[:, :width] + in_other[:, :width]).astype(BF16)[None]
-    up_grad = (in_own[:, width:] + in_other[:, width:]).astype(BF16)[None]
-    down_grad = (dot_tn(hidden_gated[:, :width], grads) + down_other_part).astype(BF16)[None]
-
-    gate_slope = around(gate_slope.reshape(chips, rows_own), 0)
-    slopes = lax.all_gather(gate_slope, "expert").reshape(chips, 2, chips, rows_own)
-    slopes = lax.dynamic_index_in_dim(slopes, core, 1, keepdims=False)
-    slopes = around(slopes, 1).reshape(chips, chips * rows_own).T
-    router_delta = (
-        slope_all * (slopes - jnp.sum(gates_all * slopes, axis=1, keepdims=True))
-    ).astype(BF16)
-    token_grad = (back_sum + dot_nt(router_delta[:rows_own], router_weight)).astype(BF16)
-    part = model_width // (2 * chips)
-    columns = lax.dynamic_slice_in_dim(rows, chip * 2 * part, 2 * part, axis=1)
-    router_part = dot_tn(columns, router_delta).reshape(2, part, experts)
-    router_grad = lax.dynamic_index_in_dim(
-        router_part, core, 0, keepdims=False
-    ) + from_partner(
-        lax.dynamic_index_in_dim(router_part, 1 - core, 0, keepdims=False), "expert", 0
-    )
+        offset = 0
+        for name, term in zip(names, terms):
+            made[name], layout[name] = term, (len(sides), offset)
+            offset += term.shape[0]
+        order.extend(names)
+        for h in range(2):
+            hidden[h].append(hiddens[h])
+            delta[h].append(deltas[h])
+        sides.append(side)
+        columns.append(column)
+        kept.append(both)
+
+    waiting = [0]
+    for k in range(1, far):
+        arrived[k] = ring_send(arrived[k - 1], 1)
+        arrived[chips - k] = ring_send(arrived[(chips - k + 1) % chips], -1)
+        waiting += [k, chips - k]
+        if k < far - 1:
+            work(waiting)
+            waiting = []
+            if k > 1:
+                arrived[k], arrived[chips - k] = after(
+                    (arrived[k], arrived[chips - k]), *sides[: k - 1]
+                )
+    ends = after((arrived[far - 1], arrived[far + 1]), *sides)
+    arrived["upper"] = ring_send(ends[0][:half], 1)
+    arrived["lower"] = ring_send(ends[1][half:], -1)
+    work(waiting + ["upper", "lower"])
+    layout[far] = layout["upper"]
+    layout = [layout[k] for k in range(chips)]
+    order = [far if name == "upper" else name for name in order if name != "lower"]
+
+    up, down, slopes = first_messages(made["upper"], made["lower"], sides, layout)
+    up, down = ring_send(up, 1), ring_send(down, -1)
+    passed = {chips - 1: down}
+    for distance in range(far - 1, 0, -1):
+        hops = far - distance
+        wait_for = tuple(part[-1] for part in parts) if distance == 1 else ()
+        up = next_message(
+            up, made[chips - distance], slopes if hops == 1 else None, True, wait_for
+        )
+        down = next_message(down, made[distance], None, False, wait_for)
+        before = (up, down)
+        up, down = ring_send(up, 1), ring_send(down, -1)
+        passed[hops], passed[chips - 1 - hops] = up, down
+        if hops == 1:
+            parts = [
+                weight_parts(kept, hidden[1], delta[1], half=half_of, wait_for=before)
+                for half_of in range(2)
+            ]
+            got = [from_partner(value, "expert", 0) for part_of in parts for value in part_of[:-1]]
+    grads = weight_parts(kept, hidden[0], delta[0], received=tuple(got), wait_for=before)
+    gate_grad, up_grad, down_grad = grads[:-1]
+
+    router_delta, keep, send = router_parts(
+        where,
+        columns,
+        [passed[k] for k in range(1, chips)],
+        slopes,
+        sides,
+        layout,
+        order,
+        experts,
+        grads[-1],
+    )
+    router_grad = keep + from_partner(send, "expert", 0)
+    mixed, token_grad = last_sums(up, down, made[0], router_delta, router_wide)
     return (mixed, token_grad, gate_grad, up_grad, down_grad, router_grad)
 
 

time: 180 us -> 118 us (0.66)
  blocking collectives: 41.2 us -> 0 us
  Pallas kernels: 0 us -> 40.7 us
  matrix products: 25.5 us -> 1.11 us
  starting transfers between devices: 35.4 us -> 19.1 us
  waiting for transfers between devices: 58 us -> 49.1 us
  local copies, waits for them, and re-layouts: 12 us -> 5.92 us
  other arithmetic: 6.43 us -> 0.91 us
    all_gather x2 -> x0, blocking collectives: 41.2 us -> none  [the longest x1 22.4 us: all_tokens_pass(): lax.all_gather(shares, 'expert').reshape(chips, 2, rows_own, 2 * experts)]
    pallas_call x0 -> x17, Pallas kernels: none -> 40.7 us  [the longest x16 38 us: kernel_call(): pl.pallas_call(body, name=name, out_shape=outs, scratch_shapes=scratch, c...]
    dot_general x8 -> x0, matrix products: 18 us -> none  [the longest x3 9.1 us: dot_nt(): lax.dot_general(left, right, (((1,), (1,)), ((), ())), preferred_element_...]
    ppermute x32 -> x16, starting transfers between devices: 34 us -> 17.4 us  [ring_send(): return lax.ppermute(value, 'expert', pairs)]
    ppermute x32 -> x16, waiting for transfers between devices: 58 us -> 49 us  [ring_send(): return lax.ppermute(value, 'expert', pairs)]
    dot_general x3 -> x1, matrix products: 7.55 us -> 1.11 us  [dot(): return jnp.dot(left, right, preferred_element_type=F32)]
    unnamed x48 -> x14, local copies, waits for them, and re-layouts: 10.1 us -> 5.65 us
    broadcast_in_dim x1 -> x0, other arithmetic: 2.28 us -> none  [all_tokens_pass(): up_grad = (in_own[:, width:] + in_other[:, width:]).astype(BF16)[None]]
  transfers between devices with their start and end apart: 38 -> 26, of which waited for: 17 -> 11; matrix products, arithmetic and copies ran while one was open for 19% -> 1% of each run, Pallas kernels for 0% -> 26%
where the time goes in v2:
time: 118 us
  waiting for transfers between devices  49.1 us (42%)
  Pallas kernels  40.7 us (34%)
  starting transfers between devices  19.1 us (16%)
  local copies, waits for them, and re-layouts  5.92 us (5%)
    ppermute x16, waiting for transfers between devices, ring_send(): return lax.ppermute(value, 'expert', pairs)  49 us
    pallas_call x16, Pallas kernels, kernel_call(): pl.pallas_call(body, name=name, out_shape=outs, scratch_shapes=scratch, c...  38 us
    ppermute x16, starting transfers between devices, ring_send(): return lax.ppermute(value, 'expert', pairs)  17.4 us
    unnamed x14, local copies, waits for them, and re-layouts  5.65 us
    pallas_call x1, Pallas kernels, router_parts(): pl.pallas_call(body, name='router_parts', out_shape=outs, grid_spec=pltpu...  2.63 us
  transfers between devices with their start and end apart: 26, of which 11 were waited for; matrix products, arithmetic and copies ran while one was open for 1% of the time, Pallas kernels for 26%

profile of v2, /device:TPU:0, one launch (start us, length us, event | category | flops | bytes accessed | tf_op | source)
XLA Modules:
  0.0 117.7 jit_solution(12720733815616031230)
XLA Ops:
  0.6 0.8 convert_element_type.18
  1.6 0.9 copy-done.3
  2.5 0.9 copy-done.4
  3.5 0.8 pack_block.1.refs_0_
  4.3 0.5 collective-permute-start.4
  4.8 0.5 collective-permute-start.6
  5.3 2.6 %collective-permute-start = (bf16[64,4224]{1,0:T(8,128)(2,1)}, bf16[64,4224]{1,0:T(8,128)(2,1)}, u32[]{:S(2)}, u32[]{:S(2)}) collective-permute-start(bf16[64,4224]{1,0:T(8,128)(2,1)} %pack_block.1.refs_0_), channel_id=1, source_target_pairs={{0,4},{1,5},{4,8},{5,9},{8,12},{9,13},{12,14},{13,15},{14,10},{15,... | collective-permute-start | bytes 1622024 | tf_op jit(solution)/shard_map/ppermute | solution.py:43
  8.0 13.1 %collective-permute-done.refs_1_ = bf16[64,4224]{1,0:T(8,128)(2,1)} collective-permute-done((bf16[64,4224]{1,0:T(8,128)(2,1)}, bf16[64,4224]{1,0:T(8,128)(2,1)}, u32[]{:S(2)}, u32[]{:S(2)}) %collective-permute-start) | collective-permute-done | bytes 540704 | tf_op jit(solution)/shard_map/ppermute | solution.py:43
  21.1 1.8 %collective-permute-start.1 = (bf16[64,4224]{1,0:T(8,128)(2,1)}, bf16[64,4224]{1,0:T(8,128)(2,1)S(1)}, u32[]{:S(2)}, u32[]{:S(2)}) collective-permute-start(bf16[64,4224]{1,0:T(8,128)(2,1)} %collective-permute-done.refs_1_), channel_id=1, source_target_pairs={{0,4},{1,5},{4,8},{5,9},{8,12},{9,13},{12,14},{13,15},{14,10},{15,... | collective-permute-start | bytes 1622024 | tf_op jit(solution)/shard_map/ppermute | solution.py:43
  22.9 0.2 collective-permute-start.3
  23.1 1.1 fusion.refs_5_.refs_4_.refs_6_
  24.3 1.4 %copy-done.1 = bf16[1,2048,384]{2,1,0:T(8,128)(2,1)S(1)} copy-done((bf16[1,2048,384]{2,1,0:T(8,128)(2,1)S(1)}, bf16[1,2048,384]{2,1,0:T(8,128)(2,1)}, u32[]{:S(2)}) %copy-start.1) | copy-done | bytes 1572888
  25.7 1.4 %copy-done.2 = bf16[1,384,2048]{2,1,0:T(8,128)(2,1)S(1)} copy-done((bf16[1,384,2048]{2,1,0:T(8,128)(2,1)S(1)}, bf16[1,384,2048]{2,1,0:T(8,128)(2,1)}, u32[]{:S(2)}) %copy-start.2) | copy-done | bytes 1572888
  27.1 3.2 %pack_weights.1 = (bf16[2048,1536]{1,0:T(8,128)(2,1)S(1)}, bf16[768,2048]{1,0:T(8,128)(2,1)S(1)}) custom-call(bf16[2048,384]{1,0:T(8,128)(2,1)S(1)} %bitcast.11, bf16[2048,384]{1,0:T(8,128)(2,1)S(1)} %bitcast.13, bf16[384,2048]{1,0:T(8,128)(2,1)S(1)} %bitcast.15, bf16[2048,384]{1,0:T(8,128)(2,1)S(1)} %collective-permute-done.4.gate_other_ref, ...), custom_call_target="tpu_custom_call" | custom-call | bytes 18874368 | tf_op jit(solution)/shard_map/pack_weights/pallas_call | solution.py:52
  30.2 6.7 %expert_chunk.3 = (bf16[64,4096]{1,0:T(8,128)(2,1)S(1)}, bf16[64,4096]{1,0:T(8,128)(2,1)S(1)}, bf16[64,4096]{1,0:T(8,128)(2,1)S(1)}, bf16[192,384]{1,0:T(8,128)(...) custom-call(bf16[64,4224]{1,0:T(8,128)(2,1)} %pack_block.1.refs_0_, ...), custom_call_target="tpu_custom_call" | custom-call | flops 3623878656 | bytes 16056872 | tf_op jit(solution)/shard_map/expert_chunk/pallas_call | solution.py:52
  37.0 1.9 %collective-permute-start.7 = (bf16[64,4224]{1,0:T(8,128)(2,1)S(1)}, bf16[64,4224]{1,0:T(8,128)(2,1)S(1)}, u32[]{:S(2)}, u32[]{:S(2)}) collective-permute-start(bf16[64,4224]{1,0:T(8,128)(2,1)S(1)} %collective-permute-done.1.refs_0_), channel_id=1, source_target_pairs={{0,4},{1,5},{4,8},{5,9},{8,12},{9,13},{12,14},{13,15},{14,10},{15,... | collective-permute-start | bytes 1622024 | tf_op jit(solution)/shard_map/ppermute | solution.py:43
  38.8 0.2 collective-permute-start.8
  39.1 5.1 %expert_chunk.4 = (bf16[64,4096]{1,0:T(8,128)(2,1)S(1)}, bf16[64,4096]{1,0:T(8,128)(2,1)S(1)}, bf16[128,384]{1,0:T(8,128)(2,1)S(1)}, bf16[128,384]{1,0:T(8,128)(...) custom-call(bf16[64,4224]{1,0:T(8,128)(2,1)S(1)} %collective-permute, ...), custom_call_target="tpu_custom_call" | custom-call | flops 2415919104 | bytes 14025256 | tf_op jit(solution)/shard_map/expert_chunk/pallas_call | solution.py:52
  44.2 6.4 %collective-permute-done.7.refs_0_ = bf16[64,4224]{1,0:T(8,128)(2,1)S(1)} collective-permute-done((bf16[64,4224]{1,0:T(8,128)(2,1)S(1)}, bf16[64,4224]{1,0:T(8,128)(2,1)S(1)}, u32[]{:S(2)}, u32[]{:S(2)}) %collective-permute-start.7) | collective-permute-done | bytes 540704 | tf_op jit(solution)/shard_map/ppermute | solution.py:43
  50.6 1.3 %collective-permute-done.8.refs_1_ = bf16[64,4224]{1,0:T(8,128)(2,1)S(1)} collective-permute-done((bf16[64,4224]{1,0:T(8,128)(2,1)S(1)}, bf16[64,4224]{1,0:T(8,128)(2,1)S(1)}, u32[]{:S(2)}, u32[]{:S(2)}) %collective-permute-start.8) | collective-permute-done | bytes 540704 | tf_op jit(solution)/shard_map/ppermute | solution.py:43
  51.9 0.5 collective-permute-start.10
  52.4 1.8 %collective-permute-start.9 = (bf16[32,4224]{1,0:T(8,128)(2,1)S(1)}, bf16[32,4224]{1,0:T(8,128)(2,1)S(1)}, u32[]{:S(2)}, u32[]{:S(2)}) collective-permute-start(bf16[32,4224]{1,0:T(8,128)(2,1)S(1)} %slice.6), channel_id=1, source_target_pairs={{0,4},{1,5},{4,8},{5,9},{8,12},{9,13},{12,14},{13,15},{14,10},{15,... | collective-permute-start | bytes 811016 | tf_op jit(solution)/shard_map/ppermute | solution.py:43
  54.3 4.2 %collective-permute-done.10.refs_3_ = bf16[32,4224]{1,0:T(8,128)(2,1)S(1)} collective-permute-done((bf16[32,4224]{1,0:T(8,128)(2,1)S(1)}, bf16[32,4224]{1,0:T(8,128)(2,1)S(1)}, u32[]{:S(2)}, u32[]{:S(2)}) %collective-permute-start.10) | collective-permute-done | bytes 270368 | tf_op jit(solution)/shard_map/ppermute | solution.py:43
  58.4 0.7 collective-permute-done.9.refs_2_
  59.1 5.9 %expert_chunk.5 = (bf16[64,4096]{1,0:T(8,128)(2,1)S(1)}, bf16[64,4096]{1,0:T(8,128)(2,1)S(1)}, bf16[32,4096]{1,0:T(8,128)(2,1)S(1)}, bf16[32,4096]{1,0:T(8,128)(...) custom-call(bf16[64,4224]{1,0:T(8,128)(2,1)S(1)} %collective-permute, ...), custom_call_target="tpu_custom_call" | custom-call | flops 3623878656 | bytes 16056872 | tf_op jit(solution)/shard_map/expert_chunk/pallas_call | solution.py:52
  65.0 0.2 first_messages.1
  65.2 1.5 %collective-permute-start.14 = (bf16[32,4224]{1,0:T(8,128)(2,1)S(1)}, bf16[32,4224]{1,0:T(8,128)(2,1)S(1)}, u32[]{:S(2)}, u32[]{:S(2)}) collective-permute-start(bf16[32,4224]{1,0:T(8,128)(2,1)S(1)} %get-tuple-element.93), channel_id=1, source_target_pairs={{0,2},{1,3},{4,0},{5,1},{8,4},{9,5},{12,8},{13,9},{14,12},{15,13},... | collective-permute-start | bytes 811016 | tf_op jit(solution)/shard_map/ppermute | solution.py:43
  66.7 0.5 collective-permute-start.11
  67.2 5.8 %collective-permute-done.14.got_ref.refs_9_ = bf16[32,4224]{1,0:T(8,128)(2,1)S(1)} collective-permute-done((bf16[32,4224]{1,0:T(8,128)(2,1)S(1)}, bf16[32,4224]{1,0:T(8,128)(2,1)S(1)}, u32[]{:S(2)}, u32[]{:S(2)}) %collective-permute-start.14) | collective-permute-done | bytes 270368 | tf_op jit(solution)/shard_map/ppermute | solution.py:43
  73.1 1.6 %collective-permute-start.16 = (bf16[64,4224]{1,0:T(8,128)(2,1)S(1)}, bf16[64,4224]{1,0:T(8,128)(2,1)S(1)}, u32[]{:S(2)}, u32[]{:S(2)}) collective-permute-start(bf16[64,4224]{1,0:T(8,128)(2,1)S(1)} %next_message.8.refs_13_), channel_id=1, source_target_pairs={{0,2},{1,3},{4,0},{5,1},{8,4},{9,5},{12,8},{13,9},{14,12},{15,13},... | collective-permute-start | bytes 1622024 | tf_op jit(solution)/shard_map/ppermute | solution.py:43
  74.8 0.5 collective-permute-start.12
  75.3 3.3 %weight_parts.4 = (bf16[1024,384]{1,0:T(8,128)(2,1)S(1)}, bf16[1024,384]{1,0:T(8,128)(2,1)S(1)}, bf16[384,1024]{1,0:T(8,128)(2,1)S(1)}, f32[8,128]{1,0:T(8,128)S(1)}) custom-call(bf16[192,4224]{1,0:T(8,128)(2,1)S(1)} %get-tuple-element.84.refs_0_.refs_3_, bf16[128,4224]{1,0:T(8,128)(2,1)S(1)} %get-tuple-element.85.refs_1_.refs_4_, ...), custom_call_target="tpu_custom_call" | custom-call | flops 1207959552 | bytes 13275136 | tf_op jit(solution)/shard_map/weight_parts/pallas_call | solution.py:52
  78.7 5.6 %collective-permute-done.16.got_ref.refs_8_ = bf16[64,4224]{1,0:T(8,128)(2,1)S(1)} collective-permute-done((bf16[64,4224]{1,0:T(8,128)(2,1)S(1)}, bf16[64,4224]{1,0:T(8,128)(2,1)S(1)}, u32[]{:S(2)}, u32[]{:S(2)}) %collective-permute-start.16) | collective-permute-done | bytes 540704 | tf_op jit(solution)/shard_map/ppermute | solution.py:43
  84.5 1.7 %collective-permute-start.17 = (bf16[64,4224]{1,0:T(8,128)(2,1)S(1)}, bf16[64,4224]{1,0:T(8,128)(2,1)S(1)}, u32[]{:S(2)}, u32[]{:S(2)}) collective-permute-start(bf16[64,4224]{1,0:T(8,128)(2,1)S(1)} %next_message.10), channel_id=1, source_target_pairs={{0,2},{1,3},{4,0},{5,1},{8,4},{9,5},{12,8},{13,9},{14,12},{15,13},... | collective-permute-start | bytes 1622024 | tf_op jit(solution)/shard_map/ppermute | solution.py:43
  86.3 0.5 collective-permute-start.13
  86.8 0.5 collective-permute-start.24
  87.3 3.3 %weight_parts.3 = (bf16[1024,384]{1,0:T(8,128)(2,1)S(1)}, bf16[1024,384]{1,0:T(8,128)(2,1)S(1)}, bf16[384,1024]{1,0:T(8,128)(2,1)S(1)}, f32[8,128]{1,0:T(8,128)S(1)}) custom-call(bf16[192,4224]{1,0:T(8,128)(2,1)S(1)} %get-tuple-element.84.refs_0_.refs_3_, bf16[128,4224]{1,0:T(8,128)(2,1)S(1)} %get-tuple-element.85.refs_1_.refs_4_, ...), custom_call_target="tpu_custom_call" | custom-call | flops 1207959552 | bytes 13275136 | tf_op jit(solution)/shard_map/weight_parts/pallas_call | solution.py:52
  90.7 4.2 %collective-permute-done.17.got_ref.refs_7_ = bf16[64,4224]{1,0:T(8,128)(2,1)S(1)} collective-permute-done((bf16[64,4224]{1,0:T(8,128)(2,1)S(1)}, bf16[64,4224]{1,0:T(8,128)(2,1)S(1)}, u32[]{:S(2)}, u32[]{:S(2)}) %collective-permute-start.17) | collective-permute-done | bytes 540704 | tf_op jit(solution)/shard_map/ppermute | solution.py:43
  94.8 1.5 %collective-permute-done.13.got_ref.refs_4_ = bf16[64,4224]{1,0:T(8,128)(2,1)S(1)} collective-permute-done((bf16[64,4224]{1,0:T(8,128)(2,1)S(1)}, bf16[64,4224]{1,0:T(8,128)(2,1)S(1)}, u32[]{:S(2)}, u32[]{:S(2)}) %collective-permute-start.13) | collective-permute-done | bytes 540704 | tf_op jit(solution)/shard_map/ppermute | solution.py:43
  96.7 1.7 %collective-permute-start.18 = (bf16[64,4224]{1,0:T(8,128)(2,1)S(1)}, bf16[64,4224]{1,0:T(8,128)(2,1)S(1)}, u32[]{:S(2)}, u32[]{:S(2)}) collective-permute-start(bf16[64,4224]{1,0:T(8,128)(2,1)S(1)} %next_message.11.refs_13_), channel_id=1, source_target_pairs={{0,2},{1,3},{4,0},{5,1},{8,4},{9,5},{12,8},{13,9},{14,12},{15,13},... | collective-permute-start | bytes 1622024 | tf_op jit(solution)/shard_map/ppermute | solution.py:43
  98.3 0.4 collective-permute-start.15
  98.8 7.6 %weight_parts.5 = (bf16[1,2048,384]{2,1,0:T(8,128)(2,1)}, bf16[1,2048,384]{2,1,0:T(8,128)(2,1)}, bf16[1,384,2048]{2,1,0:T(8,128)(2,1)}, f32[8,128]{1,0:T(8,128)S(1)}) custom-call(bf16[192,4224]{1,0:T(8,128)(2,1)S(1)} %get-tuple-element.84.refs_0_.refs_3_, bf16[128,4224]{1,0:T(8,128)(2,1)S(1)} %get-tuple-element.85.refs_1_.refs_4_, ...), custom_call_target="tpu_custom_call" | custom-call | flops 2415919104 | bytes 20353024 | tf_op jit(solution)/shard_map/weight_parts/pallas_call | solution.py:52
  106.4 5.0 %collective-permute-done.18.refs_6_.down_ref = bf16[64,4224]{1,0:T(8,128)(2,1)S(1)} collective-permute-done((bf16[64,4224]{1,0:T(8,128)(2,1)S(1)}, bf16[64,4224]{1,0:T(8,128)(2,1)S(1)}, u32[]{:S(2)}, u32[]{:S(2)}) %collective-permute-start.18) | collective-permute-done | bytes 540704 | tf_op jit(solution)/shard_map/ppermute | solution.py:43
  111.4 1.3 %collective-permute-done.15.refs_5_.up_ref = bf16[64,4224]{1,0:T(8,128)(2,1)S(1)} collective-permute-done((bf16[64,4224]{1,0:T(8,128)(2,1)S(1)}, bf16[64,4224]{1,0:T(8,128)(2,1)S(1)}, u32[]{:S(2)}, u32[]{:S(2)}) %collective-permute-start.15) | collective-permute-done | bytes 540704 | tf_op jit(solution)/shard_map/ppermute | solution.py:43
  112.7 2.6 %router_parts.1 = (bf16[64,128]{1,0:T(8,128)(2,1)S(1)}, f32[128,8]{1,0:T(8,128)S(1)}, f32[128,8]{1,0:T(8,128)S(1)}) custom-call(s32[10]{0:T(128)S(1)} %pad_add_fusion.refs_7_.refs_6_.refs_8_.where_ref, bf16[192,256]{1,0:T(8,128)(2,1)S(1)} %get-tuple-element.100.refs_0_, bf16[128,256]{1,0:T(8,128)(2,1)S(1)} %get-tuple-element.101.refs_1_, ...), custom_call_target="tpu_custom_call" | custom-call | flops 10000000 | bytes 1000000 | tf_op jit(solution)/shard_map/router_parts/pallas_call | solution.py:413
  115.5 0.3 copy.19
  115.9 1.1 last_sums.1
  117.0 0.7 copy.20
  (47 shorter events, 1.4 us)
Async XLA Ops:
  0.6 23.6 %copy-start = (bf16[1,2048,384]{2,1,0:T(8,128)(2,1)S(1)}, bf16[1,2048,384]{2,1,0:T(8,128)(2,1)}, u32[]{:S(2)}) copy-start(bf16[1,2048,384]{2,1,0:T(8,128)(2,1)} %param.11) | copy-start | bytes 4718596
  1.6 1.0 copy-start.3
  2.5 0.9 copy-start.4
  4.3 19.9 %collective-permute-start.4 = (bf16[2048,384]{1,0:T(8,128)(2,1)}, bf16[2048,384]{1,0:T(8,128)(2,1)S(1)}, u32[]{:S(2)}, u32[]{:S(2)}) collective-permute-start(bf16[2048,384]{1,0:T(8,128)(2,1)} %bitcast.10), channel_id=1, source_target_pairs={{0,1},{1,0},{2,3},{3,2},{4,5},{5,4},{6,7},{7,6},{8,9},{9,8},{10,11... | collective-permute-start | bytes 4718600 | tf_op jit(solution)/shard_map/ppermute | solution.py:15
  4.8 19.5 %collective-permute-start.5 = (bf16[2048,384]{1,0:T(8,128)(2,1)}, bf16[2048,384]{1,0:T(8,128)(2,1)}, u32[]{:S(2)}, u32[]{:S(2)}) collective-permute-start(bf16[2048,384]{1,0:T(8,128)(2,1)} %bitcast.12), channel_id=1, source_target_pairs={{0,1},{1,0},{2,3},{3,2},{4,5},{5,4},{6,7},{7,6},{8,9},{9,8},{10,11... | collective-permute-start | bytes 4718600 | tf_op jit(solution)/shard_map/ppermute | solution.py:15
  4.8 19.4 %collective-permute-start.6 = (bf16[384,2048]{1,0:T(8,128)(2,1)}, bf16[384,2048]{1,0:T(8,128)(2,1)}, u32[]{:S(2)}, u32[]{:S(2)}) collective-permute-start(bf16[384,2048]{1,0:T(8,128)(2,1)} %bitcast.14), channel_id=1, source_target_pairs={{0,1},{1,0},{2,3},{3,2},{4,5},{5,4},{6,7},{7,6},{8,9},{9,8},{10,11... | collective-permute-start | bytes 4718600 | tf_op jit(solution)/shard_map/ppermute | solution.py:15
  5.3 15.8 %collective-permute-start = (bf16[64,4224]{1,0:T(8,128)(2,1)}, bf16[64,4224]{1,0:T(8,128)(2,1)}, u32[]{:S(2)}, u32[]{:S(2)}) collective-permute-start(bf16[64,4224]{1,0:T(8,128)(2,1)} %pack_block.1.refs_0_), channel_id=1, source_target_pairs={{0,4},{1,5},{4,8},{5,9},{8,12},{9,13},{12,14},{13,15},{14,10},{15,... | collective-permute-start | bytes 1622024 | tf_op jit(solution)/shard_map/ppermute | solution.py:43
  7.8 15.0 %collective-permute-start.2 = (bf16[64,4224]{1,0:T(8,128)(2,1)}, bf16[64,4224]{1,0:T(8,128)(2,1)}, u32[]{:S(2)}, u32[]{:S(2)}) collective-permute-start(bf16[64,4224]{1,0:T(8,128)(2,1)} %pack_block.1.refs_0_), channel_id=1, source_target_pairs={{0,2},{1,3},{4,0},{5,1},{8,4},{9,5},{12,8},{13,9},{14,12},{15,13},... | collective-permute-start | bytes 1622024 | tf_op jit(solution)/shard_map/ppermute | solution.py:43
  21.1 15.9 %collective-permute-start.1 = (bf16[64,4224]{1,0:T(8,128)(2,1)}, bf16[64,4224]{1,0:T(8,128)(2,1)S(1)}, u32[]{:S(2)}, u32[]{:S(2)}) collective-permute-start(bf16[64,4224]{1,0:T(8,128)(2,1)} %collective-permute-done.refs_1_), channel_id=1, source_target_pairs={{0,4},{1,5},{4,8},{5,9},{8,12},{9,13},{12,14},{13,15},{14,10},{15,... | collective-permute-start | bytes 1622024 | tf_op jit(solution)/shard_map/ppermute | solution.py:43
  22.9 14.1 %collective-permute-start.3 = (bf16[64,4224]{1,0:T(8,128)(2,1)}, bf16[64,4224]{1,0:T(8,128)(2,1)S(1)}, u32[]{:S(2)}, u32[]{:S(2)}) collective-permute-start(bf16[64,4224]{1,0:T(8,128)(2,1)} %collective-permute-done.2.refs_2_), channel_id=1, source_target_pairs={{0,2},{1,3},{4,0},{5,1},{8,4},{9,5},{12,8},{13,9},{14,12},{15,13},... | collective-permute-start | bytes 1622024 | tf_op jit(solution)/shard_map/ppermute | solution.py:43
  24.2 1.4 %copy-start.1 = (bf16[1,2048,384]{2,1,0:T(8,128)(2,1)S(1)}, bf16[1,2048,384]{2,1,0:T(8,128)(2,1)}, u32[]{:S(2)}) copy-start(bf16[1,2048,384]{2,1,0:T(8,128)(2,1)} %param.12) | copy-start | bytes 4718596
  25.7 1.4 %copy-start.2 = (bf16[1,384,2048]{2,1,0:T(8,128)(2,1)S(1)}, bf16[1,384,2048]{2,1,0:T(8,128)(2,1)}, u32[]{:S(2)}) copy-start(bf16[1,384,2048]{2,1,0:T(8,128)(2,1)} %param.13) | copy-start | bytes 4718596
  37.0 13.6 %collective-permute-start.7 = (bf16[64,4224]{1,0:T(8,128)(2,1)S(1)}, bf16[64,4224]{1,0:T(8,128)(2,1)S(1)}, u32[]{:S(2)}, u32[]{:S(2)}) collective-permute-start(bf16[64,4224]{1,0:T(8,128)(2,1)S(1)} %collective-permute-done.1.refs_0_), channel_id=1, source_target_pairs={{0,4},{1,5},{4,8},{5,9},{8,12},{9,13},{12,14},{13,15},{14,10},{15,... | collective-permute-start | bytes 1622024 | tf_op jit(solution)/shard_map/ppermute | solution.py:43
  38.8 13.1 %collective-permute-start.8 = (bf16[64,4224]{1,0:T(8,128)(2,1)S(1)}, bf16[64,4224]{1,0:T(8,128)(2,1)S(1)}, u32[]{:S(2)}, u32[]{:S(2)}) collective-permute-start(bf16[64,4224]{1,0:T(8,128)(2,1)S(1)} %collective-permute-done.3.refs_1_), channel_id=1, source_target_pairs={{0,2},{1,3},{4,0},{5,1},{8,4},{9,5},{12,8},{13,9},{14,12},{15,13},... | collective-permute-start | bytes 1622024 | tf_op jit(solution)/shard_map/ppermute | solution.py:43
  51.9 6.5 %collective-permute-start.10 = (bf16[32,4224]{1,0:T(8,128)(2,1)S(1)}, bf16[32,4224]{1,0:T(8,128)(2,1)S(1)}, u32[]{:S(2)}, u32[]{:S(2)}) collective-permute-start(bf16[32,4224]{1,0:T(8,128)(2,1)S(1)} %slice.7), channel_id=1, source_target_pairs={{0,2},{1,3},{4,0},{5,1},{8,4},{9,5},{12,8},{13,9},{14,12},{15,13},... | collective-permute-start | bytes 811016 | tf_op jit(solution)/shard_map/ppermute | solution.py:43
  52.4 6.7 %collective-permute-start.9 = (bf16[32,4224]{1,0:T(8,128)(2,1)S(1)}, bf16[32,4224]{1,0:T(8,128)(2,1)S(1)}, u32[]{:S(2)}, u32[]{:S(2)}) collective-permute-start(bf16[32,4224]{1,0:T(8,128)(2,1)S(1)} %slice.6), channel_id=1, source_target_pairs={{0,4},{1,5},{4,8},{5,9},{8,12},{9,13},{12,14},{13,15},{14,10},{15,... | collective-permute-start | bytes 811016 | tf_op jit(solution)/shard_map/ppermute | solution.py:43
  65.2 7.8 %collective-permute-start.14 = (bf16[32,4224]{1,0:T(8,128)(2,1)S(1)}, bf16[32,4224]{1,0:T(8,128)(2,1)S(1)}, u32[]{:S(2)}, u32[]{:S(2)}) collective-permute-start(bf16[32,4224]{1,0:T(8,128)(2,1)S(1)} %get-tuple-element.93), channel_id=1, source_target_pairs={{0,2},{1,3},{4,0},{5,1},{8,4},{9,5},{12,8},{13,9},{14,12},{15,13},... | collective-permute-start | bytes 811016 | tf_op jit(solution)/shard_map/ppermute | solution.py:43
  66.7 8.0 %collective-permute-start.11 = (bf16[32,4224]{1,0:T(8,128)(2,1)S(1)}, bf16[32,4224]{1,0:T(8,128)(2,1)S(1)}, u32[]{:S(2)}, u32[]{:S(2)}) collective-permute-start(bf16[32,4224]{1,0:T(8,128)(2,1)S(1)} %get-tuple-element.79), channel_id=1, source_target_pairs={{0,4},{1,5},{4,8},{5,9},{8,12},{9,13},{12,14},{13,15},{14,10},{15,... | collective-permute-start | bytes 811016 | tf_op jit(solution)/shard_map/ppermute | solution.py:43
  73.1 11.3 %collective-permute-start.16 = (bf16[64,4224]{1,0:T(8,128)(2,1)S(1)}, bf16[64,4224]{1,0:T(8,128)(2,1)S(1)}, u32[]{:S(2)}, u32[]{:S(2)}) collective-permute-start(bf16[64,4224]{1,0:T(8,128)(2,1)S(1)} %next_message.8.refs_13_), channel_id=1, source_target_pairs={{0,2},{1,3},{4,0},{5,1},{8,4},{9,5},{12,8},{13,9},{14,12},{15,13},... | collective-permute-start | bytes 1622024 | tf_op jit(solution)/shard_map/ppermute | solution.py:43
  74.8 11.3 %collective-permute-start.12 = (bf16[64,4224]{1,0:T(8,128)(2,1)S(1)}, bf16[64,4224]{1,0:T(8,128)(2,1)S(1)}, u32[]{:S(2)}, u32[]{:S(2)}) collective-permute-start(bf16[64,4224]{1,0:T(8,128)(2,1)S(1)} %next_message.6.refs_12_), channel_id=1, source_target_pairs={{0,4},{1,5},{4,8},{5,9},{8,12},{9,13},{12,14},{13,15},{14,10},{15,... | collective-permute-start | bytes 1622024 | tf_op jit(solution)/shard_map/ppermute | solution.py:43
  78.6 11.9 %collective-permute-start.22 = (bf16[1024,384]{1,0:T(8,128)(2,1)S(1)}, bf16[1024,384]{1,0:T(8,128)(2,1)S(1)}, u32[]{:S(2)}, u32[]{:S(2)}) collective-permute-start(bf16[1024,384]{1,0:T(8,128)(2,1)S(1)} %get-tuple-element.112), channel_id=1, source_target_pairs={{0,1},{1,0},{2,3},{3,2},{4,5},{5,4},{6,7},{7,6},{8,9},{9,8},{10,11... | collective-permute-start | bytes 2359304 | tf_op jit(solution)/shard_map/ppermute | solution.py:15
  84.5 10.4 %collective-permute-start.17 = (bf16[64,4224]{1,0:T(8,128)(2,1)S(1)}, bf16[64,4224]{1,0:T(8,128)(2,1)S(1)}, u32[]{:S(2)}, u32[]{:S(2)}) collective-permute-start(bf16[64,4224]{1,0:T(8,128)(2,1)S(1)} %next_message.10), channel_id=1, source_target_pairs={{0,2},{1,3},{4,0},{5,1},{8,4},{9,5},{12,8},{13,9},{14,12},{15,13},... | collective-permute-start | bytes 1622024 | tf_op jit(solution)/shard_map/ppermute | solution.py:43
  86.3 10.1 %collective-permute-start.13 = (bf16[64,4224]{1,0:T(8,128)(2,1)S(1)}, bf16[64,4224]{1,0:T(8,128)(2,1)S(1)}, u32[]{:S(2)}, u32[]{:S(2)}) collective-permute-start(bf16[64,4224]{1,0:T(8,128)(2,1)S(1)} %next_message.7), channel_id=1, source_target_pairs={{0,4},{1,5},{4,8},{5,9},{8,12},{9,13},{12,14},{13,15},{14,10},{15,... | collective-permute-start | bytes 1622024 | tf_op jit(solution)/shard_map/ppermute | solution.py:43
  86.7 9.9 %collective-permute-start.23 = (bf16[1024,384]{1,0:T(8,128)(2,1)S(1)}, bf16[1024,384]{1,0:T(8,128)(2,1)S(1)}, u32[]{:S(2)}, u32[]{:S(2)}) collective-permute-start(bf16[1024,384]{1,0:T(8,128)(2,1)S(1)} %get-tuple-element.113), channel_id=1, source_target_pairs={{0,1},{1,0},{2,3},{3,2},{4,5},{5,4},{6,7},{7,6},{8,9},{9,8},{10,11... | collective-permute-start | bytes 2359304 | tf_op jit(solution)/shard_map/ppermute | solution.py:15
  86.8 11.6 %collective-permute-start.24 = (bf16[384,1024]{1,0:T(8,128)(2,1)S(1)}, bf16[384,1024]{1,0:T(8,128)(2,1)S(1)}, u32[]{:S(2)}, u32[]{:S(2)}) collective-permute-start(bf16[384,1024]{1,0:T(8,128)(2,1)S(1)} %get-tuple-element.114), channel_id=1, source_target_pairs={{0,1},{1,0},{2,3},{3,2},{4,5},{5,4},{6,7},{7,6},{8,9},{9,8},{10,11... | collective-permute-start | bytes 2359304 | tf_op jit(solution)/shard_map/ppermute | solution.py:15
  90.6 8.2 %collective-permute-start.19 = (bf16[1024,384]{1,0:T(8,128)(2,1)S(1)}, bf16[1024,384]{1,0:T(8,128)(2,1)S(1)}, u32[]{:S(2)}, u32[]{:S(2)}) collective-permute-start(bf16[1024,384]{1,0:T(8,128)(2,1)S(1)} %get-tuple-element.109), channel_id=1, source_target_pairs={{0,1},{1,0},{2,3},{3,2},{4,5},{5,4},{6,7},{7,6},{8,9},{9,8},{10,11... | collective-permute-start | bytes 2359304 | tf_op jit(solution)/shard_map/ppermute | solution.py:15
  94.8 3.9 %collective-permute-start.20 = (bf16[1024,384]{1,0:T(8,128)(2,1)S(1)}, bf16[1024,384]{1,0:T(8,128)(2,1)S(1)}, u32[]{:S(2)}, u32[]{:S(2)}) collective-permute-start(bf16[1024,384]{1,0:T(8,128)(2,1)S(1)} %get-tuple-element.110), channel_id=1, source_target_pairs={{0,1},{1,0},{2,3},{3,2},{4,5},{5,4},{6,7},{7,6},{8,9},{9,8},{10,11... | collective-permute-start | bytes 2359304 | tf_op jit(solution)/shard_map/ppermute | solution.py:15
  96.4 2.4 %collective-permute-start.21 = (bf16[384,1024]{1,0:T(8,128)(2,1)S(1)}, bf16[384,1024]{1,0:T(8,128)(2,1)S(1)}, u32[]{:S(2)}, u32[]{:S(2)}) collective-permute-start(bf16[384,1024]{1,0:T(8,128)(2,1)S(1)} %get-tuple-element.111), channel_id=1, source_target_pairs={{0,1},{1,0},{2,3},{3,2},{4,5},{5,4},{6,7},{7,6},{8,9},{9,8},{10,11... | collective-permute-start | bytes 2359304 | tf_op jit(solution)/shard_map/ppermute | solution.py:15
  96.7 14.7 %collective-permute-start.18 = (bf16[64,4224]{1,0:T(8,128)(2,1)S(1)}, bf16[64,4224]{1,0:T(8,128)(2,1)S(1)}, u32[]{:S(2)}, u32[]{:S(2)}) collective-permute-start(bf16[64,4224]{1,0:T(8,128)(2,1)S(1)} %next_message.11.refs_13_), channel_id=1, source_target_pairs={{0,2},{1,3},{4,0},{5,1},{8,4},{9,5},{12,8},{13,9},{14,12},{15,13},... | collective-permute-start | bytes 1622024 | tf_op jit(solution)/shard_map/ppermute | solution.py:43
  98.3 14.4 %collective-permute-start.15 = (bf16[64,4224]{1,0:T(8,128)(2,1)S(1)}, bf16[64,4224]{1,0:T(8,128)(2,1)S(1)}, u32[]{:S(2)}, u32[]{:S(2)}) collective-permute-start(bf16[64,4224]{1,0:T(8,128)(2,1)S(1)} %next_message.9.refs_12_), channel_id=1, source_target_pairs={{0,4},{1,5},{4,8},{5,9},{8,12},{9,13},{12,14},{13,15},{14,10},{15,... | collective-permute-start | bytes 1622024 | tf_op jit(solution)/shard_map/ppermute | solution.py:43
  112.7 2.7 %copy-start.5 = (bf16[2048,8]{0,1:T(8,128)(2,1)S(1)}, bf16[2048,8]{0,1:T(8,128)(2,1)}, u32[]{:S(2)}) copy-start(bf16[2048,8]{0,1:T(8,128)(2,1)} %param.10) | copy-start | bytes 98308
  115.4 1.6 %collective-permute-start.25 = (f32[128,8]{1,0:T(8,128)S(1)}, f32[128,8]{1,0:T(8,128)S(1)}, u32[]{:S(2)}, u32[]{:S(2)}) collective-permute-start(f32[128,8]{1,0:T(8,128)S(1)} %get-tuple-element.123), channel_id=1, source_target_pairs={{0,1},{1,0},{2,3},{3,2},{4,5},{5,4},{6,7},{7,6},{8,9},{9,8},{10,11... | collective-permute-start | bytes 12296 | tf_op jit(solution)/shard_map/ppermute | solution.py:15

commit v3 on v2

--- a/solution.py
+++ b/solution.py
@@ -64,20 +64,47 @@
 ANY = pl.BlockSpec(memory_space=pl.ANY)
 
 
+def in_hbm(array):
+    return pltpu.with_memory_space_constraint(array, pltpu.HBM)
+
+
 def lane_ids(rows):
     return lax.broadcasted_iota(jnp.int32, (rows, LANES), 1)
 
 
 def pack_block(tokens, grad_out, ids):
     count, width = tokens.shape
-
-    def body(tokens_ref, grads_ref, ids_ref, block_ref):
-        block_ref[:, :width] = tokens_ref[...]
-        block_ref[:, width : 2 * width] = grads_ref[...]
-        block_ref[:, 2 * width :] = ids_ref[...]
+    per_token = ids.shape[1]
+
+    def body(tokens_ref, grads_ref, ids_hbm, block_ref, ids_ref, sems):
+        copies = [
+            pltpu.make_async_copy(
+                ref, block_ref.at[:, pl.ds(i * width, width)], sems.at[i]
+            )
+            for i, ref in enumerate((tokens_ref, grads_ref))
+        ]
+        numbers = pltpu.make_async_copy(ids_hbm, ids_ref, sems.at[2])
+        numbers.start()
+        for copy in copies:
+            copy.start()
+        numbers.wait()
+        row = lax.broadcasted_iota(jnp.int32, (per_token, LANES), 0)
+        spread = (row == lane_ids(per_token)).astype(F32).astype(BF16)
+        numbers = ids_ref[...].astype(F32).astype(BF16)
+        block_ref[:, 2 * width :] = dot_tn(numbers, spread).astype(BF16)
+        for copy in copies:
+            copy.wait()
 
     out = jax.ShapeDtypeStruct((count, 2 * width + LANES), BF16)
-    return kernel_call(body, "pack_block", (out,), (tokens, grad_out, ids))[0]
+    return kernel_call(
+        body,
+        "pack_block",
+        (out,),
+        (in_hbm(tokens), in_hbm(grad_out), in_hbm(ids.T)),
+        scratch=[pltpu.VMEM((per_token, count), jnp.int32), pltpu.SemaphoreType.DMA((3,))],
+        in_specs=[ANY] * 3,
+        out_specs=[VMEM],
+    )[0]
 
 
 def pack_weights(own, other):
@@ -111,7 +138,7 @@
     )
 
 
-def expert_chunk(blocks, weights, router, behind, where, per_token, part):
+def expert_chunk(blocks, weights, router, behind, where, per_token, part, wait_for=()):
     number = len(blocks)
     stride = blocks[0].shape[1]
     spans, total = [], 0
@@ -123,7 +150,8 @@
     def body(*refs):
         block_refs, refs = refs[:number], refs[number:]
         in_ref, down_ref, router_ref, behind_ref, where_ref = refs[:5]
-        made_refs, refs = refs[5 : 5 + number], refs[5 + number :]
+        refs = refs[5 + len(wait_for) :]
+        made_refs, refs = refs[:number], refs[number:]
         hidden_refs, delta_refs = refs[:2], refs[2:4]
         side_ref, column_ref, both_ref, delta_ref = refs[4:]
         for i in range(number):
@@ -180,11 +208,13 @@
         body,
         "expert_chunk",
         outs,
-        (*blocks, *weights, router, behind, where),
+        (*blocks, *weights, router, behind, where, *wait_for),
         scratch=[pltpu.VMEM((total, 4 * width), BF16)],
         limit=24,
         flops=24 * total * model_width * width,
-        in_specs=[VMEM] * (number + 4) + [pl.BlockSpec(memory_space=pltpu.SMEM)],
+        in_specs=[VMEM] * (number + 4)
+        + [pl.BlockSpec(memory_space=pltpu.SMEM)]
+        + [ANY] * len(wait_for),
         out_specs=[VMEM] * len(outs),
     )
     return made[:number], made[number : number + 2], made[number + 2 : number + 4], made[-3:]
@@ -231,7 +261,7 @@
     )
 
 
-def next_message(got, made, slopes=None, upper=None, wait_for=()):
+def next_message(got, made, upper, wait_for=()):
     count, stride = made.shape
     half = count // 2
     small = got.shape[0] == half
@@ -248,18 +278,17 @@
             message_ref[:, :stride] = (
                 made_ref[...].astype(F32) + got_ref[:, :stride].astype(F32)
             ).astype(BF16)
-        message_ref[:half, stride:] = refs[0][...] if slopes is not None else got_ref[:half, stride:]
+        message_ref[:half, stride:] = got_ref[:half, stride:]
         message_ref[half:, stride:] = jnp.zeros((count - half, LANES), BF16)
 
-    ins = (got, made) if slopes is None else (got, made, slopes)
     out = jax.ShapeDtypeStruct((count, stride + LANES), BF16)
     return kernel_call(
         body,
         "next_message",
         (out,),
-        (*ins, *wait_for),
+        (got, made, *wait_for),
         flops=count * stride,
-        in_specs=[VMEM] * len(ins) + [ANY] * len(wait_for),
+        in_specs=[VMEM] * 2 + [ANY] * len(wait_for),
         out_specs=[VMEM],
     )[0]
 
@@ -352,8 +381,8 @@
 def router_parts(where, pieces, passed, slopes, sides, layout, order, experts, mark):
     chips = len(layout)
     number = len(pieces)
-    half, stride = passed[0].shape[0] // 2, passed[0].shape[1]
-    count, part = 2 * half, pieces[0].shape[1] // 2
+    half, part = slopes.shape[0], pieces[0].shape[1] // 2
+    count = 2 * half
 
     def body(where_ref, *refs):
         column_refs, refs = refs[:number], refs[number:]
@@ -388,25 +417,27 @@
             gates = side_refs[index][offset : offset + count, :LANES]
             factor = side_refs[index][offset : offset + count, LANES : 2 * LANES]
             middle = jnp.sum(gates * slope, axis=1, keepdims=True)
-            delta = (factor * (slope - middle)).astype(BF16)
-            deltas.append(dot(delta, turn).astype(BF16))
+            deltas.append((factor * (slope - middle)).astype(BF16))
         delta_ref[...] = deltas[0]
+        deltas = [dot(delta, turn).astype(BF16) for delta in deltas]
         columns = jnp.concatenate([ref[...] for ref in column_refs], axis=0)
-        total_ref[...] = dot_tn(columns, jnp.concatenate([deltas[q] for q in order], axis=0))
+        total_ref[...] = dot_tn(jnp.concatenate([deltas[q] for q in order], axis=0), columns)
         core = where_ref[1]
         own, other = pl.multiple_of(core * part, part), pl.multiple_of((1 - core) * part, part)
-        keep_ref[...] = total_ref[pl.ds(own, part), :experts]
-        send_ref[...] = total_ref[pl.ds(other, part), :experts]
-
-    info = stride // LANES - 1
+        keep_ref[...] = total_ref[:experts, pl.ds(own, part)]
+        send_ref[...] = total_ref[:experts, pl.ds(other, part)]
+
     in_specs = [pl.BlockSpec(a.shape, lambda i, w: (0, 0)) for a in pieces]
-    in_specs += [pl.BlockSpec((half, LANES), lambda i, w: (0, info)) for _ in range(chips - 1)]
+    in_specs += [
+        pl.BlockSpec((half, LANES), lambda i, w, last=a.shape[1] // LANES - 1: (0, last))
+        for a in passed
+    ]
     in_specs += [pl.BlockSpec(slopes.shape, lambda i, w: (0, 0))]
     in_specs += [pl.BlockSpec((side.shape[0], 2 * LANES), lambda i, w: (0, 0)) for side in sides]
     outs = (
         jax.ShapeDtypeStruct((count, LANES), BF16),
-        jax.ShapeDtypeStruct((part, experts), F32),
-        jax.ShapeDtypeStruct((part, experts), F32),
+        jax.ShapeDtypeStruct((experts, part), F32),
+        jax.ShapeDtypeStruct((experts, part), F32),
     )
     in_specs += [ANY]
     ins = (where, *pieces, *passed, slopes, *sides, mark)
@@ -419,7 +450,7 @@
             grid=(1,),
             in_specs=in_specs,
             out_specs=[pl.BlockSpec(o.shape, lambda i, w: (0, 0)) for o in outs],
-            scratch_shapes=[pltpu.VMEM((2 * part, LANES), F32)],
+            scratch_shapes=[pltpu.VMEM((LANES, 2 * part), F32)],
         ),
         compiler_params=pltpu.CompilerParams(vmem_limit_bytes=8 * MIB),
         cost_estimate=pl.CostEstimate(flops=10**7, bytes_accessed=10**6, transcendentals=0),
@@ -463,11 +494,9 @@
     turn = (jnp.arange(experts, dtype=jnp.int32)[:, None] == behind[None, :]).astype(BF16)
     turn = jnp.pad(turn, ((0, 0), (0, LANES - chips)))
     router_turned = dot(router_weight, turn).astype(BF16)
-    router_wide = jnp.pad(router_weight, ((0, 0), (0, LANES - experts)))
     behind = jnp.pad(behind.astype(F32), (0, LANES - chips), constant_values=-1.0)[None]
 
-    ids = jnp.pad(expert_ids.astype(BF16), ((0, 0), (0, LANES - per_token)))
-    block = pack_block(tokens, grad_out, ids)
+    block = pack_block(tokens, grad_out, expert_ids)
     own = after((gate_weight[0], up_weight[0], down_weight[0]), block)
     weights = pack_weights(own, from_partner(own, "expert", 0))
 
@@ -485,6 +514,7 @@
             where,
             per_token,
             part,
+            tuple(sides[-1:]),
         )
         offset = 0
         for name, term in zip(names, terms):
@@ -503,34 +533,36 @@
         arrived[k] = ring_send(arrived[k - 1], 1)
         arrived[chips - k] = ring_send(arrived[(chips - k + 1) % chips], -1)
         waiting += [k, chips - k]
-        if k < far - 1:
+        if k == far - 2:
             work(waiting)
             waiting = []
-            if k > 1:
-                arrived[k], arrived[chips - k] = after(
-                    (arrived[k], arrived[chips - k]), *sides[: k - 1]
-                )
-    ends = after((arrived[far - 1], arrived[far + 1]), *sides)
+            for name in (k, chips - k):
+                arrived[name] = after(arrived[name], *weights)
+    ends = [after(arrived[name], *sides) for name in (far - 1, far + 1)]
     arrived["upper"] = ring_send(ends[0][:half], 1)
     arrived["lower"] = ring_send(ends[1][half:], -1)
-    work(waiting + ["upper", "lower"])
+    work(waiting)
+    work(["upper", "lower"])
     layout[far] = layout["upper"]
     layout = [layout[k] for k in range(chips)]
     order = [far if name == "upper" else name for name in order if name != "lower"]
 
     up, down, slopes = first_messages(made["upper"], made["lower"], sides, layout)
     up, down = ring_send(up, 1), ring_send(down, -1)
-    passed = {chips - 1: down}
+    passed = {1: up, chips - 1: down, far: ring_send(slopes, far)}
     for distance in range(far - 1, 0, -1):
         hops = far - distance
-        wait_for = tuple(part[-1] for part in parts) if distance == 1 else ()
-        up = next_message(
-            up, made[chips - distance], slopes if hops == 1 else None, True, wait_for
-        )
-        down = next_message(down, made[distance], None, False, wait_for)
+        wait_for = ()
+        if distance == 1:
+            wait_for = tuple(part[-1] for part in parts)
+        elif distance == far - 1:
+            wait_for = (passed[far],)
+        up = next_message(up, made[chips - distance], True, wait_for)
+        down = next_message(down, made[distance], False, wait_for)
         before = (up, down)
         up, down = ring_send(up, 1), ring_send(down, -1)
-        passed[hops], passed[chips - 1 - hops] = up, down
+        if distance > 1:
+            passed[hops + 1], passed[chips - 1 - hops] = up, down
         if hops == 1:
             parts = [
                 weight_parts(kept, hidden[1], delta[1], half=half_of, wait_for=before)
@@ -551,8 +583,8 @@
         experts,
         grads[-1],
     )
-    router_grad = keep + from_partner(send, "expert", 0)
-    mixed, token_grad = last_sums(up, down, made[0], router_delta, router_wide)
+    router_grad = (keep + from_partner(send, "expert", 0)).T
+    mixed, token_grad = last_sums(up, down, made[0], router_delta, router_turned)
     return (mixed, token_grad, gate_grad, up_grad, down_grad, router_grad)
 
 

time: 118 us -> 112 us (0.949)
  waiting for transfers between devices: 49.1 us -> 41 us
  starting transfers between devices: 19.1 us -> 23.3 us
  local copies, waits for them, and re-layouts: 5.92 us -> 2.87 us
  Pallas kernels: 40.7 us -> 42.2 us
    ppermute x16 -> x17, waiting for transfers between devices: 49 us -> 39.5 us  [ring_send(): return lax.ppermute(value, 'expert', pairs)]
    ppermute x16 -> x17, starting transfers between devices: 17.4 us -> 21 us  [ring_send(): return lax.ppermute(value, 'expert', pairs)]
    unnamed x14 -> x8, local copies, waits for them, and re-layouts: 5.65 us -> 2.83 us
    pallas_call x16, Pallas kernels: 38 us -> 39.9 us  [kernel_call(): pl.pallas_call(body, name=name, out_shape=outs, scratch_shapes=scratch, c...]
    ppermute x10, waiting for transfers between devices: 0.03 us -> 1.55 us  [from_partner(): return lax.ppermute(value, axis, pairs)]
  transfers between devices with their start and end apart: 26 -> 27, of which waited for: 11 -> 13; matrix products, arithmetic and copies ran while one was open for 1% -> 1% of each run, Pallas kernels for 26% -> 30%
where the time goes in v3:
time: 112 us; the launch traced here: 111 us
  Pallas kernels  42.2 us (38%)
  waiting for transfers between devices  41 us (37%)
  starting transfers between devices  23.3 us (21%)
  local copies, waits for them, and re-layouts  2.87 us (3%)
    pallas_call x16, Pallas kernels, kernel_call(): pl.pallas_call(body, name=name, out_shape=outs, scratch_shapes=scratch, c...  39.9 us
    ppermute x17, waiting for transfers between devices, ring_send(): return lax.ppermute(value, 'expert', pairs)  39.5 us
    ppermute x17, starting transfers between devices, ring_send(): return lax.ppermute(value, 'expert', pairs)  21 us
    unnamed x8, local copies, waits for them, and re-layouts  2.83 us
    pallas_call x1, Pallas kernels, router_parts(): pl.pallas_call(body, name='router_parts', out_shape=outs, grid_spec=pltpu...  2.33 us
    ppermute x10, starting transfers between devices, from_partner(): return lax.ppermute(value, axis, pairs)  2.25 us
  transfers between devices with their start and end apart: 27, of which 13 were waited for; matrix products, arithmetic and copies ran while one was open for 1% of the time, Pallas kernels for 30%

profile of v3, /device:TPU:0, one launch (start us, length us, event | category | flops | bytes accessed | tf_op | source)
XLA Modules:
  0.0 111.3 jit_solution(16215278696622383728)
XLA Ops:
  0.7 2.0 %pack_block.1.refs_0_ = bf16[64,4224]{1,0:T(8,128)(2,1)} custom-call(bf16[64,2048]{1,0:T(8,128)(2,1)} %tokens_ref.1, bf16[64,2048]{1,0:T(8,128)(2,1)} %grads_ref.1, s32[4,64]{1,0:T(4,128)} %bitcast.19), custom_call_target="tpu_custom_call" | custom-call | bytes 1065984 | tf_op jit(solution)/shard_map/pack_block/pallas_call | solution.py:52
  2.7 0.5 collective-permute-start.2
  3.3 0.4 collective-permute-start.4
  3.7 2.6 %collective-permute-start.6 = (bf16[64,4224]{1,0:T(8,128)(2,1)}, bf16[64,4224]{1,0:T(8,128)(2,1)}, u32[]{:S(2)}, u32[]{:S(2)}) collective-permute-start(bf16[64,4224]{1,0:T(8,128)(2,1)} %pack_block.1.refs_0_), channel_id=1, source_target_pairs={{0,2},{1,3},{4,0},{5,1},{8,4},{9,5},{12,8},{13,9},{14,12},{15,13},... | collective-permute-start | bytes 1622024 | tf_op jit(solution)/shard_map/ppermute | solution.py:43
  6.4 13.2 %collective-permute-done.6.refs_2_ = bf16[64,4224]{1,0:T(8,128)(2,1)} collective-permute-done((bf16[64,4224]{1,0:T(8,128)(2,1)}, bf16[64,4224]{1,0:T(8,128)(2,1)}, u32[]{:S(2)}, u32[]{:S(2)}) %collective-permute-start.6) | collective-permute-done | bytes 540704 | tf_op jit(solution)/shard_map/ppermute | solution.py:43
  19.5 1.7 %collective-permute-start.7 = (bf16[64,4224]{1,0:T(8,128)(2,1)}, bf16[64,4224]{1,0:T(8,128)(2,1)S(1)}, u32[]{:S(2)}, u32[]{:S(2)}) collective-permute-start(bf16[64,4224]{1,0:T(8,128)(2,1)} %collective-permute-done.6.refs_2_), channel_id=1, source_target_pairs={{0,2},{1,3},{4,0},{5,1},{8,4},{9,5},{12,8},{13,9},{14,12},{15,13},... | collective-permute-start | bytes 1622024 | tf_op jit(solution)/shard_map/ppermute | solution.py:43
  21.2 0.3 collective-permute-start.1
  21.6 0.4 fusion.refs_7_.refs_4_.router_ref
  22.1 1.4 %copy-done.2 = bf16[1,2048,384]{2,1,0:T(8,128)(2,1)S(1)} copy-done((bf16[1,2048,384]{2,1,0:T(8,128)(2,1)S(1)}, bf16[1,2048,384]{2,1,0:T(8,128)(2,1)}, u32[]{:S(2)}) %copy-start.2) | copy-done | bytes 1572888
  23.5 1.4 %copy-done.3 = bf16[1,384,2048]{2,1,0:T(8,128)(2,1)S(1)} copy-done((bf16[1,384,2048]{2,1,0:T(8,128)(2,1)S(1)}, bf16[1,384,2048]{2,1,0:T(8,128)(2,1)}, u32[]{:S(2)}) %copy-start.3) | copy-done | bytes 1572888
  24.9 3.2 %pack_weights.1 = (bf16[2048,1536]{1,0:T(8,128)(2,1)S(1)}, bf16[768,2048]{1,0:T(8,128)(2,1)S(1)}) custom-call(bf16[2048,384]{1,0:T(8,128)(2,1)S(1)} %bitcast.14, bf16[2048,384]{1,0:T(8,128)(2,1)S(1)} %bitcast.16, bf16[384,2048]{1,0:T(8,128)(2,1)S(1)} %bitcast.18, bf16[2048,384]{1,0:T(8,128)(2,1)S(1)} %collective-permute-done.2.gate_other_ref, ...), custom_call_target="tpu_custom_call" | custom-call | bytes 18874368 | tf_op jit(solution)/shard_map/pack_weights/pallas_call | solution.py:52
  28.0 5.7 %collective-permute-done.7.refs_4_ = bf16[64,4224]{1,0:T(8,128)(2,1)S(1)} collective-permute-done((bf16[64,4224]{1,0:T(8,128)(2,1)}, bf16[64,4224]{1,0:T(8,128)(2,1)S(1)}, u32[]{:S(2)}, u32[]{:S(2)}) %collective-permute-start.7) | collective-permute-done | bytes 540704 | tf_op jit(solution)/shard_map/ppermute | solution.py:43
  33.8 1.2 %collective-permute-done.1.refs_3_ = bf16[64,4224]{1,0:T(8,128)(2,1)S(1)} collective-permute-done((bf16[64,4224]{1,0:T(8,128)(2,1)}, bf16[64,4224]{1,0:T(8,128)(2,1)S(1)}, u32[]{:S(2)}, u32[]{:S(2)}) %collective-permute-start.1) | collective-permute-done | bytes 540704 | tf_op jit(solution)/shard_map/ppermute | solution.py:43
  35.0 0.5 collective-permute-start.5
  35.5 1.5 %collective-permute-start.9 = (bf16[64,4224]{1,0:T(8,128)(2,1)S(1)}, bf16[64,4224]{1,0:T(8,128)(2,1)S(1)}, u32[]{:S(2)}, u32[]{:S(2)}) collective-permute-start(bf16[64,4224]{1,0:T(8,128)(2,1)S(1)} %collective-permute-done.7.refs_4_), channel_id=1, source_target_pairs={{0,2},{1,3},{4,0},{5,1},{8,4},{9,5},{12,8},{13,9},{14,12},{15,13},... | collective-permute-start | bytes 1622024 | tf_op jit(solution)/shard_map/ppermute | solution.py:43
  37.0 8.5 %expert_chunk.3 = (bf16[64,4096]{1,0:T(8,128)(2,1)S(1)}, bf16[64,4096]{1,0:T(8,128)(2,1)S(1)}, bf16[64,4096]{1,0:T(8,128)(2,1)S(1)}, bf16[64,4096]{1,0:T(8,128)(...) custom-call(bf16[64,4224]{1,0:T(8,128)(2,1)} %pack_block.1.refs_0_, ...), custom_call_target="tpu_custom_call" | custom-call | flops 6039797760 | bytes 20120104 | tf_op jit(solution)/shard_map/expert_chunk/pallas_call | solution.py:52
  45.5 2.6 %collective-permute-done.9.refs_1_ = bf16[64,4224]{1,0:T(8,128)(2,1)S(1)} collective-permute-done((bf16[64,4224]{1,0:T(8,128)(2,1)S(1)}, bf16[64,4224]{1,0:T(8,128)(2,1)S(1)}, u32[]{:S(2)}, u32[]{:S(2)}) %collective-permute-start.9) | collective-permute-done | bytes 540704 | tf_op jit(solution)/shard_map/ppermute | solution.py:43
  48.1 1.4 %collective-permute-start.10 = (bf16[32,4224]{1,0:T(8,128)(2,1)S(1)}, bf16[32,4224]{1,0:T(8,128)(2,1)S(1)}, u32[]{:S(2)}, u32[]{:S(2)}) collective-permute-start(bf16[32,4224]{1,0:T(8,128)(2,1)S(1)} %slice.7), channel_id=1, source_target_pairs={{0,2},{1,3},{4,0},{5,1},{8,4},{9,5},{12,8},{13,9},{14,12},{15,13},... | collective-permute-start | bytes 811016 | tf_op jit(solution)/shard_map/ppermute | solution.py:43
  49.5 0.7 collective-permute-start.8
  50.2 5.1 %expert_chunk.4 = (bf16[64,4096]{1,0:T(8,128)(2,1)S(1)}, bf16[64,4096]{1,0:T(8,128)(2,1)S(1)}, bf16[128,384]{1,0:T(8,128)(2,1)S(1)}, bf16[128,384]{1,0:T(8,128)(...) custom-call(bf16[64,4224]{1,0:T(8,128)(2,1)S(1)} %collective-permute, ...), custom_call_target="tpu_custom_call" | custom-call | flops 2415919104 | bytes 14516776 | tf_op jit(solution)/shard_map/expert_chunk/pallas_call | solution.py:52
  55.4 0.6 collective-permute-done.8.refs_0_
  55.9 5.2 %expert_chunk.5 = (bf16[32,4096]{1,0:T(8,128)(2,1)S(1)}, bf16[32,4096]{1,0:T(8,128)(2,1)S(1)}, bf16[64,384]{1,0:T(8,128)(2,1)S(1)}, bf16[64,384]{1,0:T(8,128)(2,...) custom-call(bf16[32,4224]{1,0:T(8,128)(2,1)S(1)} %collective-permute, ...), custom_call_target="tpu_custom_call" | custom-call | flops 1207959552 | bytes 12190248 | tf_op jit(solution)/shard_map/expert_chunk/pallas_call | solution.py:52
  61.2 0.2 first_messages.1
  61.3 1.6 %collective-permute-start.15 = (bf16[32,4224]{1,0:T(8,128)(2,1)S(1)}, bf16[32,4224]{1,0:T(8,128)(2,1)S(1)}, u32[]{:S(2)}, u32[]{:S(2)}) collective-permute-start(bf16[32,4224]{1,0:T(8,128)(2,1)S(1)} %get-tuple-element.93), channel_id=1, source_target_pairs={{0,2},{1,3},{4,0},{5,1},{8,4},{9,5},{12,8},{13,9},{14,12},{15,13},... | collective-permute-start | bytes 811016 | tf_op jit(solution)/shard_map/ppermute | solution.py:43
  62.9 0.5 collective-permute-start.11
  63.4 3.8 %collective-permute-start.12 = (bf16[32,128]{1,0:T(8,128)(2,1)S(1)}, bf16[32,128]{1,0:T(8,128)(2,1)S(1)}, u32[]{:S(2)}, u32[]{:S(2)}) collective-permute-start(bf16[32,128]{1,0:T(8,128)(2,1)S(1)} %get-tuple-element.81.refs_10_), channel_id=1, source_target_pairs={{0,14},{1,15},{4,10},{5,11},{8,6},{9,7},{12,2},{13,3},{14,0},{15,1... | collective-permute-start | bytes 24584 | tf_op jit(solution)/shard_map/ppermute | solution.py:43
  67.1 5.1 %collective-permute-done.12.refs_0_.refs_6_ = bf16[32,128]{1,0:T(8,128)(2,1)S(1)} collective-permute-done((bf16[32,128]{1,0:T(8,128)(2,1)S(1)}, bf16[32,128]{1,0:T(8,128)(2,1)S(1)}, u32[]{:S(2)}, u32[]{:S(2)}) %collective-permute-start.12) | collective-permute-done | bytes 8224 | tf_op jit(solution)/shard_map/ppermute | solution.py:43
  72.4 2.1 %collective-permute-start.13 = (bf16[64,4224]{1,0:T(8,128)(2,1)S(1)}, bf16[64,4224]{1,0:T(8,128)(2,1)S(1)}, u32[]{:S(2)}, u32[]{:S(2)}) collective-permute-start(bf16[64,4224]{1,0:T(8,128)(2,1)S(1)} %next_message.6.refs_12_), channel_id=1, source_target_pairs={{0,4},{1,5},{4,8},{5,9},{8,12},{9,13},{12,14},{13,15},{14,10},{15,... | collective-permute-start | bytes 1622024 | tf_op jit(solution)/shard_map/ppermute | solution.py:43
  74.5 3.3 %weight_parts.3 = (bf16[1024,384]{1,0:T(8,128)(2,1)S(1)}, bf16[1024,384]{1,0:T(8,128)(2,1)S(1)}, bf16[384,1024]{1,0:T(8,128)(2,1)S(1)}, f32[8,128]{1,0:T(8,128)S(1)}) custom-call(bf16[320,4224]{1,0:T(8,128)(2,1)S(1)} %get-tuple-element.84.refs_0_.refs_3_, bf16[128,4224]{1,0:T(8,128)(2,1)S(1)} %get-tuple-element.85.refs_1_.refs_4_, ...), custom_call_target="tpu_custom_call" | custom-call | flops 1207959552 | bytes 13275136 | tf_op jit(solution)/shard_map/weight_parts/pallas_call | solution.py:52
  77.8 4.4 %collective-permute-done.17.got_ref.refs_8_ = bf16[64,4224]{1,0:T(8,128)(2,1)S(1)} collective-permute-done((bf16[64,4224]{1,0:T(8,128)(2,1)S(1)}, bf16[64,4224]{1,0:T(8,128)(2,1)S(1)}, u32[]{:S(2)}, u32[]{:S(2)}) %collective-permute-start.17) | collective-permute-done | bytes 540704 | tf_op jit(solution)/shard_map/ppermute | solution.py:43
  82.6 2.2 %collective-permute-start.14 = (bf16[64,4224]{1,0:T(8,128)(2,1)S(1)}, bf16[64,4224]{1,0:T(8,128)(2,1)S(1)}, u32[]{:S(2)}, u32[]{:S(2)}) collective-permute-start(bf16[64,4224]{1,0:T(8,128)(2,1)S(1)} %next_message.7), channel_id=1, source_target_pairs={{0,4},{1,5},{4,8},{5,9},{8,12},{9,13},{12,14},{13,15},{14,10},{15,... | collective-permute-start | bytes 1622024 | tf_op jit(solution)/shard_map/ppermute | solution.py:43
  84.8 0.5 collective-permute-start.22
  85.3 3.3 %weight_parts.4 = (bf16[1024,384]{1,0:T(8,128)(2,1)S(1)}, bf16[1024,384]{1,0:T(8,128)(2,1)S(1)}, bf16[384,1024]{1,0:T(8,128)(2,1)S(1)}, f32[8,128]{1,0:T(8,128)S(1)}) custom-call(bf16[320,4224]{1,0:T(8,128)(2,1)S(1)} %get-tuple-element.84.refs_0_.refs_3_, bf16[128,4224]{1,0:T(8,128)(2,1)S(1)} %get-tuple-element.85.refs_1_.refs_4_, ...), custom_call_target="tpu_custom_call" | custom-call | flops 1207959552 | bytes 13275136 | tf_op jit(solution)/shard_map/weight_parts/pallas_call | solution.py:52
  88.7 4.6 %collective-permute-done.18.got_ref.refs_7_ = bf16[64,4224]{1,0:T(8,128)(2,1)S(1)} collective-permute-done((bf16[64,4224]{1,0:T(8,128)(2,1)S(1)}, bf16[64,4224]{1,0:T(8,128)(2,1)S(1)}, u32[]{:S(2)}, u32[]{:S(2)}) %collective-permute-start.18) | collective-permute-done | bytes 540704 | tf_op jit(solution)/shard_map/ppermute | solution.py:43
  93.3 0.1 collective-permute-done.14.got_ref.refs_5_
  93.4 0.4 collective-permute-start.25
  93.9 0.1 next_message.9.refs_12_
  94.1 1.7 %collective-permute-start.16 = (bf16[64,4224]{1,0:T(8,128)(2,1)S(1)}, bf16[64,4224]{1,0:T(8,128)(2,1)S(1)}, u32[]{:S(2)}, u32[]{:S(2)}) collective-permute-start(bf16[64,4224]{1,0:T(8,128)(2,1)S(1)} %next_message.9.refs_12_), channel_id=1, source_target_pairs={{0,4},{1,5},{4,8},{5,9},{8,12},{9,13},{12,14},{13,15},{14,10},{15,... | collective-permute-start | bytes 1622024 | tf_op jit(solution)/shard_map/ppermute | solution.py:43
  95.8 0.4 collective-permute-start.19
  96.2 0.5 collective-permute-done.25.refs_19_
  96.7 7.4 %weight_parts.5 = (bf16[1,2048,384]{2,1,0:T(8,128)(2,1)}, bf16[1,2048,384]{2,1,0:T(8,128)(2,1)}, bf16[1,384,2048]{2,1,0:T(8,128)(2,1)}, f32[8,128]{1,0:T(8,128)S(1)}) custom-call(bf16[320,4224]{1,0:T(8,128)(2,1)S(1)} %get-tuple-element.84.refs_0_.refs_3_, bf16[128,4224]{1,0:T(8,128)(2,1)S(1)} %get-tuple-element.85.refs_1_.refs_4_, ...), custom_call_target="tpu_custom_call" | custom-call | flops 2415919104 | bytes 20353024 | tf_op jit(solution)/shard_map/weight_parts/pallas_call | solution.py:52
  104.1 2.3 %router_parts.1 = (bf16[64,128]{1,0:T(8,128)(2,1)S(1)}, f32[8,128]{1,0:T(8,128)S(1)}, f32[8,128]{1,0:T(8,128)S(1)}) custom-call(s32[10]{0:T(128)S(1)} %pad_add_fusion.refs_9_.refs_6_.where_ref, bf16[320,256]{1,0:T(8,128)(2,1)S(1)} %get-tuple-element.100.refs_0_, bf16[128,256]{1,0:T(8,128)(2,1)S(1)} %get-tuple-element.101.refs_1_, ...), custom_call_target="tpu_custom_call" | custom-call | flops 10000000 | bytes 1000000 | tf_op jit(solution)/shard_map/router_parts/pallas_call | solution.py:444
  106.5 0.2 collective-permute-start.26
  106.7 1.0 collective-permute-done.26
  107.7 0.6 add_bitcast_fusion
  108.3 0.2 collective-permute-done.16.up_ref
  108.5 1.7 %collective-permute-done.19.down_ref = bf16[64,4224]{1,0:T(8,128)(2,1)S(1)} collective-permute-done((bf16[64,4224]{1,0:T(8,128)(2,1)S(1)}, bf16[64,4224]{1,0:T(8,128)(2,1)S(1)}, u32[]{:S(2)}, u32[]{:S(2)}) %collective-permute-start.19) | collective-permute-done | bytes 540704 | tf_op jit(solution)/shard_map/ppermute | solution.py:43
  110.2 1.1 %last_sums.1 = (bf16[64,2048]{1,0:T(8,128)(2,1)}, bf16[64,2048]{1,0:T(8,128)(2,1)}) custom-call(bf16[64,4224]{1,0:T(8,128)(2,1)S(1)} %collective-permute-done.16.up_ref, bf16[64,4224]{1,0:T(8,128)(2,1)S(1)} %collective-permute-done.19.down_ref, bf16[64,4096]{1,0:T(8,128)(2,1)S(1)} %get-tuple-element.99.made_ref, ...), custom_call_target="tpu_custom_call" | custom-call | bytes 2670592 | tf_op jit(solution)/shard_map/last_sums/pallas_call | solution.py:52
  (39 shorter events, 1.1 us)
Async XLA Ops:
  0.6 21.0 %copy-start = (bf16[2048,8]{0,1:T(8,128)(2,1)S(1)}, bf16[2048,8]{0,1:T(8,128)(2,1)}, u32[]{:S(2)}) copy-start(bf16[2048,8]{0,1:T(8,128)(2,1)} %param.10) | copy-start | bytes 98308
  0.6 21.4 %copy-start.1 = (bf16[1,2048,384]{2,1,0:T(8,128)(2,1)S(1)}, bf16[1,2048,384]{2,1,0:T(8,128)(2,1)}, u32[]{:S(2)}) copy-start(bf16[1,2048,384]{2,1,0:T(8,128)(2,1)} %param.11) | copy-start | bytes 4718596
  2.7 19.3 %collective-permute-start.2 = (bf16[2048,384]{1,0:T(8,128)(2,1)}, bf16[2048,384]{1,0:T(8,128)(2,1)S(1)}, u32[]{:S(2)}, u32[]{:S(2)}) collective-permute-start(bf16[2048,384]{1,0:T(8,128)(2,1)} %bitcast.13), channel_id=1, source_target_pairs={{0,1},{1,0},{2,3},{3,2},{4,5},{5,4},{6,7},{7,6},{8,9},{9,8},{10,11... | collective-permute-start | bytes 4718600 | tf_op jit(solution)/shard_map/ppermute | solution.py:15
  3.2 18.8 %collective-permute-start.3 = (bf16[2048,384]{1,0:T(8,128)(2,1)}, bf16[2048,384]{1,0:T(8,128)(2,1)}, u32[]{:S(2)}, u32[]{:S(2)}) collective-permute-start(bf16[2048,384]{1,0:T(8,128)(2,1)} %bitcast.15), channel_id=1, source_target_pairs={{0,1},{1,0},{2,3},{3,2},{4,5},{5,4},{6,7},{7,6},{8,9},{9,8},{10,11... | collective-permute-start | bytes 4718600 | tf_op jit(solution)/shard_map/ppermute | solution.py:15
  3.3 18.8 %collective-permute-start.4 = (bf16[384,2048]{1,0:T(8,128)(2,1)}, bf16[384,2048]{1,0:T(8,128)(2,1)}, u32[]{:S(2)}, u32[]{:S(2)}) collective-permute-start(bf16[384,2048]{1,0:T(8,128)(2,1)} %bitcast.17), channel_id=1, source_target_pairs={{0,1},{1,0},{2,3},{3,2},{4,5},{5,4},{6,7},{7,6},{8,9},{9,8},{10,11... | collective-permute-start | bytes 4718600 | tf_op jit(solution)/shard_map/ppermute | solution.py:15
  3.7 15.8 %collective-permute-start.6 = (bf16[64,4224]{1,0:T(8,128)(2,1)}, bf16[64,4224]{1,0:T(8,128)(2,1)}, u32[]{:S(2)}, u32[]{:S(2)}) collective-permute-start(bf16[64,4224]{1,0:T(8,128)(2,1)} %pack_block.1.refs_0_), channel_id=1, source_target_pairs={{0,2},{1,3},{4,0},{5,1},{8,4},{9,5},{12,8},{13,9},{14,12},{15,13},... | collective-permute-start | bytes 1622024 | tf_op jit(solution)/shard_map/ppermute | solution.py:43
  6.3 14.9 %collective-permute-start = (bf16[64,4224]{1,0:T(8,128)(2,1)}, bf16[64,4224]{1,0:T(8,128)(2,1)}, u32[]{:S(2)}, u32[]{:S(2)}) collective-permute-start(bf16[64,4224]{1,0:T(8,128)(2,1)} %pack_block.1.refs_0_), channel_id=1, source_target_pairs={{0,4},{1,5},{4,8},{5,9},{8,12},{9,13},{12,14},{13,15},{14,10},{15,... | collective-permute-start | bytes 1622024 | tf_op jit(solution)/shard_map/ppermute | solution.py:43
  19.5 14.2 %collective-permute-start.7 = (bf16[64,4224]{1,0:T(8,128)(2,1)}, bf16[64,4224]{1,0:T(8,128)(2,1)S(1)}, u32[]{:S(2)}, u32[]{:S(2)}) collective-permute-start(bf16[64,4224]{1,0:T(8,128)(2,1)} %collective-permute-done.6.refs_2_), channel_id=1, source_target_pairs={{0,2},{1,3},{4,0},{5,1},{8,4},{9,5},{12,8},{13,9},{14,12},{15,13},... | collective-permute-start | bytes 1622024 | tf_op jit(solution)/shard_map/ppermute | solution.py:43
  21.2 13.8 %collective-permute-start.1 = (bf16[64,4224]{1,0:T(8,128)(2,1)}, bf16[64,4224]{1,0:T(8,128)(2,1)S(1)}, u32[]{:S(2)}, u32[]{:S(2)}) collective-permute-start(bf16[64,4224]{1,0:T(8,128)(2,1)} %collective-permute-done.refs_1_), channel_id=1, source_target_pairs={{0,4},{1,5},{4,8},{5,9},{8,12},{9,13},{12,14},{13,15},{14,10},{15,... | collective-permute-start | bytes 1622024 | tf_op jit(solution)/shard_map/ppermute | solution.py:43
  22.0 1.4 %copy-start.2 = (bf16[1,2048,384]{2,1,0:T(8,128)(2,1)S(1)}, bf16[1,2048,384]{2,1,0:T(8,128)(2,1)}, u32[]{:S(2)}) copy-start(bf16[1,2048,384]{2,1,0:T(8,128)(2,1)} %param.12) | copy-start | bytes 4718596
  23.4 1.4 %copy-start.3 = (bf16[1,384,2048]{2,1,0:T(8,128)(2,1)S(1)}, bf16[1,384,2048]{2,1,0:T(8,128)(2,1)}, u32[]{:S(2)}) copy-start(bf16[1,384,2048]{2,1,0:T(8,128)(2,1)} %param.13) | copy-start | bytes 4718596
  35.0 13.1 %collective-permute-start.5 = (bf16[64,4224]{1,0:T(8,128)(2,1)S(1)}, bf16[64,4224]{1,0:T(8,128)(2,1)S(1)}, u32[]{:S(2)}, u32[]{:S(2)}) collective-permute-start(bf16[64,4224]{1,0:T(8,128)(2,1)S(1)} %collective-permute-done.1.refs_3_), channel_id=1, source_target_pairs={{0,4},{1,5},{4,8},{5,9},{8,12},{9,13},{12,14},{13,15},{14,10},{15,... | collective-permute-start | bytes 1622024 | tf_op jit(solution)/shard_map/ppermute | solution.py:43
  35.5 12.6 %collective-permute-start.9 = (bf16[64,4224]{1,0:T(8,128)(2,1)S(1)}, bf16[64,4224]{1,0:T(8,128)(2,1)S(1)}, u32[]{:S(2)}, u32[]{:S(2)}) collective-permute-start(bf16[64,4224]{1,0:T(8,128)(2,1)S(1)} %collective-permute-done.7.refs_4_), channel_id=1, source_target_pairs={{0,2},{1,3},{4,0},{5,1},{8,4},{9,5},{12,8},{13,9},{14,12},{15,13},... | collective-permute-start | bytes 1622024 | tf_op jit(solution)/shard_map/ppermute | solution.py:43
  48.1 7.2 %collective-permute-start.10 = (bf16[32,4224]{1,0:T(8,128)(2,1)S(1)}, bf16[32,4224]{1,0:T(8,128)(2,1)S(1)}, u32[]{:S(2)}, u32[]{:S(2)}) collective-permute-start(bf16[32,4224]{1,0:T(8,128)(2,1)S(1)} %slice.7), channel_id=1, source_target_pairs={{0,2},{1,3},{4,0},{5,1},{8,4},{9,5},{12,8},{13,9},{14,12},{15,13},... | collective-permute-start | bytes 811016 | tf_op jit(solution)/shard_map/ppermute | solution.py:43
  49.5 6.5 %collective-permute-start.8 = (bf16[32,4224]{1,0:T(8,128)(2,1)S(1)}, bf16[32,4224]{1,0:T(8,128)(2,1)S(1)}, u32[]{:S(2)}, u32[]{:S(2)}) collective-permute-start(bf16[32,4224]{1,0:T(8,128)(2,1)S(1)} %slice.6), channel_id=1, source_target_pairs={{0,4},{1,5},{4,8},{5,9},{8,12},{9,13},{12,14},{13,15},{14,10},{15,... | collective-permute-start | bytes 811016 | tf_op jit(solution)/shard_map/ppermute | solution.py:43
  61.3 10.9 %collective-permute-start.15 = (bf16[32,4224]{1,0:T(8,128)(2,1)S(1)}, bf16[32,4224]{1,0:T(8,128)(2,1)S(1)}, u32[]{:S(2)}, u32[]{:S(2)}) collective-permute-start(bf16[32,4224]{1,0:T(8,128)(2,1)S(1)} %get-tuple-element.93), channel_id=1, source_target_pairs={{0,2},{1,3},{4,0},{5,1},{8,4},{9,5},{12,8},{13,9},{14,12},{15,13},... | collective-permute-start | bytes 811016 | tf_op jit(solution)/shard_map/ppermute | solution.py:43
  62.9 9.5 %collective-permute-start.11 = (bf16[32,4224]{1,0:T(8,128)(2,1)S(1)}, bf16[32,4224]{1,0:T(8,128)(2,1)S(1)}, u32[]{:S(2)}, u32[]{:S(2)}) collective-permute-start(bf16[32,4224]{1,0:T(8,128)(2,1)S(1)} %get-tuple-element.79), channel_id=1, source_target_pairs={{0,4},{1,5},{4,8},{5,9},{8,12},{9,13},{12,14},{13,15},{14,10},{15,... | collective-permute-start | bytes 811016 | tf_op jit(solution)/shard_map/ppermute | solution.py:43
  63.4 8.9 %collective-permute-start.12 = (bf16[32,128]{1,0:T(8,128)(2,1)S(1)}, bf16[32,128]{1,0:T(8,128)(2,1)S(1)}, u32[]{:S(2)}, u32[]{:S(2)}) collective-permute-start(bf16[32,128]{1,0:T(8,128)(2,1)S(1)} %get-tuple-element.81.refs_10_), channel_id=1, source_target_pairs={{0,14},{1,15},{4,10},{5,11},{8,6},{9,7},{12,2},{13,3},{14,0},{15,1... | collective-permute-start | bytes 24584 | tf_op jit(solution)/shard_map/ppermute | solution.py:43
  72.3 9.9 %collective-permute-start.17 = (bf16[64,4224]{1,0:T(8,128)(2,1)S(1)}, bf16[64,4224]{1,0:T(8,128)(2,1)S(1)}, u32[]{:S(2)}, u32[]{:S(2)}) collective-permute-start(bf16[64,4224]{1,0:T(8,128)(2,1)S(1)} %next_message.8.refs_13_), channel_id=1, source_target_pairs={{0,2},{1,3},{4,0},{5,1},{8,4},{9,5},{12,8},{13,9},{14,12},{15,13},... | collective-permute-start | bytes 1622024 | tf_op jit(solution)/shard_map/ppermute | solution.py:43
  72.4 10.0 %collective-permute-start.13 = (bf16[64,4224]{1,0:T(8,128)(2,1)S(1)}, bf16[64,4224]{1,0:T(8,128)(2,1)S(1)}, u32[]{:S(2)}, u32[]{:S(2)}) collective-permute-start(bf16[64,4224]{1,0:T(8,128)(2,1)S(1)} %next_message.6.refs_12_), channel_id=1, source_target_pairs={{0,4},{1,5},{4,8},{5,9},{8,12},{9,13},{12,14},{13,15},{14,10},{15,... | collective-permute-start | bytes 1622024 | tf_op jit(solution)/shard_map/ppermute | solution.py:43
  77.8 10.8 %collective-permute-start.20 = (bf16[1024,384]{1,0:T(8,128)(2,1)S(1)}, bf16[1024,384]{1,0:T(8,128)(2,1)S(1)}, u32[]{:S(2)}, u32[]{:S(2)}) collective-permute-start(bf16[1024,384]{1,0:T(8,128)(2,1)S(1)} %get-tuple-element.109), channel_id=1, source_target_pairs={{0,1},{1,0},{2,3},{3,2},{4,5},{5,4},{6,7},{7,6},{8,9},{9,8},{10,11... | collective-permute-start | bytes 2359304 | tf_op jit(solution)/shard_map/ppermute | solution.py:15
  82.3 10.9 %collective-permute-start.18 = (bf16[64,4224]{1,0:T(8,128)(2,1)S(1)}, bf16[64,4224]{1,0:T(8,128)(2,1)S(1)}, u32[]{:S(2)}, u32[]{:S(2)}) collective-permute-start(bf16[64,4224]{1,0:T(8,128)(2,1)S(1)} %next_message.10), channel_id=1, source_target_pairs={{0,2},{1,3},{4,0},{5,1},{8,4},{9,5},{12,8},{13,9},{14,12},{15,13},... | collective-permute-start | bytes 1622024 | tf_op jit(solution)/shard_map/ppermute | solution.py:43
  82.6 10.9 %collective-permute-start.14 = (bf16[64,4224]{1,0:T(8,128)(2,1)S(1)}, bf16[64,4224]{1,0:T(8,128)(2,1)S(1)}, u32[]{:S(2)}, u32[]{:S(2)}) collective-permute-start(bf16[64,4224]{1,0:T(8,128)(2,1)S(1)} %next_message.7), channel_id=1, source_target_pairs={{0,4},{1,5},{4,8},{5,9},{8,12},{9,13},{12,14},{13,15},{14,10},{15,... | collective-permute-start | bytes 1622024 | tf_op jit(solution)/shard_map/ppermute | solution.py:43
  84.8 9.3 %collective-permute-start.21 = (bf16[1024,384]{1,0:T(8,128)(2,1)S(1)}, bf16[1024,384]{1,0:T(8,128)(2,1)S(1)}, u32[]{:S(2)}, u32[]{:S(2)}) collective-permute-start(bf16[1024,384]{1,0:T(8,128)(2,1)S(1)} %get-tuple-element.110), channel_id=1, source_target_pairs={{0,1},{1,0},{2,3},{3,2},{4,5},{5,4},{6,7},{7,6},{8,9},{9,8},{10,11... | collective-permute-start | bytes 2359304 | tf_op jit(solution)/shard_map/ppermute | solution.py:15
  84.8 11.0 %collective-permute-start.22 = (bf16[384,1024]{1,0:T(8,128)(2,1)S(1)}, bf16[384,1024]{1,0:T(8,128)(2,1)S(1)}, u32[]{:S(2)}, u32[]{:S(2)}) collective-permute-start(bf16[384,1024]{1,0:T(8,128)(2,1)S(1)} %get-tuple-element.111), channel_id=1, source_target_pairs={{0,1},{1,0},{2,3},{3,2},{4,5},{5,4},{6,7},{7,6},{8,9},{9,8},{10,11... | collective-permute-start | bytes 2359304 | tf_op jit(solution)/shard_map/ppermute | solution.py:15
  88.6 7.6 %collective-permute-start.23 = (bf16[1024,384]{1,0:T(8,128)(2,1)S(1)}, bf16[1024,384]{1,0:T(8,128)(2,1)S(1)}, u32[]{:S(2)}, u32[]{:S(2)}) collective-permute-start(bf16[1024,384]{1,0:T(8,128)(2,1)S(1)} %get-tuple-element.112), channel_id=1, source_target_pairs={{0,1},{1,0},{2,3},{3,2},{4,5},{5,4},{6,7},{7,6},{8,9},{9,8},{10,11... | collective-permute-start | bytes 2359304 | tf_op jit(solution)/shard_map/ppermute | solution.py:15
  93.3 2.9 %collective-permute-start.24 = (bf16[1024,384]{1,0:T(8,128)(2,1)S(1)}, bf16[1024,384]{1,0:T(8,128)(2,1)S(1)}, u32[]{:S(2)}, u32[]{:S(2)}) collective-permute-start(bf16[1024,384]{1,0:T(8,128)(2,1)S(1)} %get-tuple-element.113), channel_id=1, source_target_pairs={{0,1},{1,0},{2,3},{3,2},{4,5},{5,4},{6,7},{7,6},{8,9},{9,8},{10,11... | collective-permute-start | bytes 2359304 | tf_op jit(solution)/shard_map/ppermute | solution.py:15
  93.4 3.3 %collective-permute-start.25 = (bf16[384,1024]{1,0:T(8,128)(2,1)S(1)}, bf16[384,1024]{1,0:T(8,128)(2,1)S(1)}, u32[]{:S(2)}, u32[]{:S(2)}) collective-permute-start(bf16[384,1024]{1,0:T(8,128)(2,1)S(1)} %get-tuple-element.114), channel_id=1, source_target_pairs={{0,1},{1,0},{2,3},{3,2},{4,5},{5,4},{6,7},{7,6},{8,9},{9,8},{10,11... | collective-permute-start | bytes 2359304 | tf_op jit(solution)/shard_map/ppermute | solution.py:15
  94.1 14.4 %collective-permute-start.16 = (bf16[64,4224]{1,0:T(8,128)(2,1)S(1)}, bf16[64,4224]{1,0:T(8,128)(2,1)S(1)}, u32[]{:S(2)}, u32[]{:S(2)}) collective-permute-start(bf16[64,4224]{1,0:T(8,128)(2,1)S(1)} %next_message.9.refs_12_), channel_id=1, source_target_pairs={{0,4},{1,5},{4,8},{5,9},{8,12},{9,13},{12,14},{13,15},{14,10},{15,... | collective-permute-start | bytes 1622024 | tf_op jit(solution)/shard_map/ppermute | solution.py:43
  95.8 14.4 %collective-permute-start.19 = (bf16[64,4224]{1,0:T(8,128)(2,1)S(1)}, bf16[64,4224]{1,0:T(8,128)(2,1)S(1)}, u32[]{:S(2)}, u32[]{:S(2)}) collective-permute-start(bf16[64,4224]{1,0:T(8,128)(2,1)S(1)} %next_message.11.refs_13_), channel_id=1, source_target_pairs={{0,2},{1,3},{4,0},{5,1},{8,4},{9,5},{12,8},{13,9},{14,12},{15,13},... | collective-permute-start | bytes 1622024 | tf_op jit(solution)/shard_map/ppermute | solution.py:43
  106.5 1.2 %collective-permute-start.26 = (f32[8,128]{1,0:T(8,128)S(1)}, f32[8,128]{1,0:T(8,128)S(1)}, u32[]{:S(2)}, u32[]{:S(2)}) collective-permute-start(f32[8,128]{1,0:T(8,128)S(1)} %get-tuple-element.123), channel_id=1, source_target_pairs={{0,1},{1,0},{2,3},{3,2},{4,5},{5,4},{6,7},{7,6},{8,9},{9,8},{10,11... | collective-permute-start | bytes 12296 | tf_op jit(solution)/shard_map/ppermute | solution.py:15

commit v4 on v3

--- a/solution.py
+++ b/solution.py
@@ -112,11 +112,14 @@
     steps = 4
     tile = depth // steps
 
-    def body(gate_ref, up_ref, down_ref, gate_other_ref, up_other_ref, down_other_ref, in_ref, out_ref):
+    def body(gate_ref, up_ref, down_ref, gate_other_ref, up_other_ref, down_other_ref, *made):
+        in_ref, out_ref, in_turned_ref, out_turned_ref = made
         for i, ref in enumerate((gate_ref, gate_other_ref, up_ref, up_other_ref)):
             in_ref[:, i * width : (i + 1) * width] = ref[...]
-        out_ref[:width] = down_ref[...]
-        out_ref[width:] = down_other_ref[...]
+            in_turned_ref[i * width : (i + 1) * width, :] = ref[...].T
+        for i, ref in enumerate((down_ref, down_other_ref)):
+            out_ref[i * width : (i + 1) * width, :] = ref[...]
+            out_turned_ref[:, i * width : (i + 1) * width] = ref[...].T
 
     in_spec = pl.BlockSpec((tile, width), lambda d: (d, 0))
     down_spec = pl.BlockSpec((width, tile), lambda d: (0, d))
@@ -126,6 +129,8 @@
         (
             jax.ShapeDtypeStruct((depth, 4 * width), BF16),
             jax.ShapeDtypeStruct((2 * width, depth), BF16),
+            jax.ShapeDtypeStruct((4 * width, depth), BF16),
+            jax.ShapeDtypeStruct((depth, 2 * width), BF16),
         ),
         (*own, *other),
         grid=(steps,),
@@ -133,6 +138,8 @@
         out_specs=[
             pl.BlockSpec((tile, 4 * width), lambda d: (d, 0)),
             pl.BlockSpec((2 * width, tile), lambda d: (0, d)),
+            pl.BlockSpec((4 * width, tile), lambda d: (0, d)),
+            pl.BlockSpec((tile, 2 * width), lambda d: (d, 0)),
         ],
         limit=16,
     )
@@ -149,8 +156,9 @@
 
     def body(*refs):
         block_refs, refs = refs[:number], refs[number:]
-        in_ref, down_ref, router_ref, behind_ref, where_ref = refs[:5]
-        refs = refs[5 + len(wait_for) :]
+        in_ref, down_ref, in_turned_ref, down_turned_ref = refs[:4]
+        router_ref, behind_ref, where_ref = refs[4:7]
+        refs = refs[7 + len(wait_for) :]
         made_refs, refs = refs[:number], refs[number:]
         hidden_refs, delta_refs = refs[:2], refs[2:4]
         side_ref, column_ref, both_ref, delta_ref = refs[4:]
@@ -177,7 +185,7 @@
         activated = pre_gate * squash
         hidden = activated * pre_up
         hidden_gated = (gate * hidden).astype(BF16)
-        back_hidden = dot_nt(grads, down_ref[...])
+        back_hidden = dot(grads, down_turned_ref[...])
         slope = jnp.sum(hidden * back_hidden, axis=1, keepdims=True)
         side_ref[:, 2 * LANES :] = jnp.broadcast_to(slope, (total, LANES))
         back_hidden = gate * back_hidden
@@ -191,7 +199,7 @@
             delta_refs[h][:, :width] = gate_delta[:, half]
             delta_refs[h][:, width:] = up_delta[:, half]
         out = dot(hidden_gated, down_ref[...]).astype(BF16)
-        back = dot_nt(delta_ref[...], in_ref[...]).astype(BF16)
+        back = dot(delta_ref[...], in_turned_ref[...]).astype(BF16)
         for i in range(number):
             made_refs[i][:, :model_width] = out[spans[i]]
             made_refs[i][:, model_width:] = back[spans[i]]
@@ -210,9 +218,9 @@
         outs,
         (*blocks, *weights, router, behind, where, *wait_for),
         scratch=[pltpu.VMEM((total, 4 * width), BF16)],
-        limit=24,
+        limit=20,
         flops=24 * total * model_width * width,
-        in_specs=[VMEM] * (number + 4)
+        in_specs=[VMEM] * (number + 6)
         + [pl.BlockSpec(memory_space=pltpu.SMEM)]
         + [ANY] * len(wait_for),
         out_specs=[VMEM] * len(outs),

time: 112 us -> 111 us (level)
    unnamed x8 -> x10, local copies, waits for them, and re-layouts: 2.83 us -> 2.83 us
  transfers between devices with their start and end apart: 27 -> 27, of which waited for: 13 -> 15; matrix products, arithmetic and copies ran while one was open for 1% -> 1% of each run, Pallas kernels for 30% -> 31%
where the time goes in v4:
time: 111 us
  Pallas kernels  41.7 us (38%)
  waiting for transfers between devices  41.4 us (37%)
  starting transfers between devices  23.1 us (21%)
  local copies, waits for them, and re-layouts  2.88 us (3%)
    ppermute x17, waiting for transfers between devices, ring_send(): return lax.ppermute(value, 'expert', pairs)  39.9 us
    pallas_call x16, Pallas kernels, kernel_call(): pl.pallas_call(body, name=name, out_shape=outs, scratch_shapes=scratch, c...  39.3 us
    ppermute x17, starting transfers between devices, ring_send(): return lax.ppermute(value, 'expert', pairs)  20.8 us
    unnamed x10, local copies, waits for them, and re-layouts  2.83 us
    pallas_call x1, Pallas kernels, router_parts(): pl.pallas_call(body, name='router_parts', out_shape=outs, grid_spec=pltpu...  2.33 us
    ppermute x10, starting transfers between devices, from_partner(): return lax.ppermute(value, axis, pairs)  2.27 us
  transfers between devices with their start and end apart: 27, of which 15 were waited for; matrix products, arithmetic and copies ran while one was open for 1% of the time, Pallas kernels for 31%

profile of v4, /device:TPU:0, one launch (start us, length us, event | category | flops | bytes accessed | tf_op | source)
XLA Modules:
  0.0 111.0 jit_solution(18052127944781975219)
XLA Ops:
  0.7 2.0 %pack_block.1.refs_0_ = bf16[64,4224]{1,0:T(8,128)(2,1)} custom-call(bf16[64,2048]{1,0:T(8,128)(2,1)} %tokens_ref.1, bf16[64,2048]{1,0:T(8,128)(2,1)} %grads_ref.1, s32[4,64]{1,0:T(4,128)} %bitcast.19), custom_call_target="tpu_custom_call" | custom-call | bytes 1065984 | tf_op jit(solution)/shard_map/pack_block/pallas_call | solution.py:52
  2.7 0.5 collective-permute-start.2
  3.3 0.4 collective-permute-start.4
  3.7 2.6 %collective-permute-start.6 = (bf16[64,4224]{1,0:T(8,128)(2,1)}, bf16[64,4224]{1,0:T(8,128)(2,1)}, u32[]{:S(2)}, u32[]{:S(2)}) collective-permute-start(bf16[64,4224]{1,0:T(8,128)(2,1)} %pack_block.1.refs_0_), channel_id=1, source_target_pairs={{0,2},{1,3},{4,0},{5,1},{8,4},{9,5},{12,8},{13,9},{14,12},{15,13},... | collective-permute-start | bytes 1622024 | tf_op jit(solution)/shard_map/ppermute | solution.py:43
  6.4 13.2 %collective-permute-done.6.refs_2_ = bf16[64,4224]{1,0:T(8,128)(2,1)} collective-permute-done((bf16[64,4224]{1,0:T(8,128)(2,1)}, bf16[64,4224]{1,0:T(8,128)(2,1)}, u32[]{:S(2)}, u32[]{:S(2)}) %collective-permute-start.6) | collective-permute-done | bytes 540704 | tf_op jit(solution)/shard_map/ppermute | solution.py:43
  19.5 1.7 %collective-permute-start.7 = (bf16[64,4224]{1,0:T(8,128)(2,1)}, bf16[64,4224]{1,0:T(8,128)(2,1)S(1)}, u32[]{:S(2)}, u32[]{:S(2)}) collective-permute-start(bf16[64,4224]{1,0:T(8,128)(2,1)} %collective-permute-done.6.refs_2_), channel_id=1, source_target_pairs={{0,2},{1,3},{4,0},{5,1},{8,4},{9,5},{12,8},{13,9},{14,12},{15,13},... | collective-permute-start | bytes 1622024 | tf_op jit(solution)/shard_map/ppermute | solution.py:43
  21.2 0.3 collective-permute-start.1
  21.6 0.4 fusion.refs_9_.refs_6_.router_ref
  22.1 1.4 %copy-done.3 = bf16[1,2048,384]{2,1,0:T(8,128)(2,1)S(1)} copy-done((bf16[1,2048,384]{2,1,0:T(8,128)(2,1)S(1)}, bf16[1,2048,384]{2,1,0:T(8,128)(2,1)}, u32[]{:S(2)}) %copy-start.3) | copy-done | bytes 1572888
  23.5 1.4 %copy-done.4 = bf16[1,384,2048]{2,1,0:T(8,128)(2,1)S(1)} copy-done((bf16[1,384,2048]{2,1,0:T(8,128)(2,1)S(1)}, bf16[1,384,2048]{2,1,0:T(8,128)(2,1)}, u32[]{:S(2)}) %copy-start.4) | copy-done | bytes 1572888
  24.9 5.5 %pack_weights.1 = (bf16[2048,1536]{1,0:T(8,128)(2,1)S(1)}, bf16[768,2048]{1,0:T(8,128)(2,1)S(1)}, bf16[1536,2048]{1,0:T(8,128)(2,1)S(1)}, bf16[2048,768]{1,0:T(8,128)(2,1)S(1)}) custom-call(bf16[2048,384]{1,0:T(8,128)(2,1)S(1)} %bitcast.14, bf16[2048,384]{1,0:T(8,128)(2,1)S(1)} %bitcast.16, bf16[384,2048]{1,0:T(8,128)(2,1)S(1)} %bitcast.18, ...), custom_call_target="tpu_custom_call" | custom-call | bytes 28311552 | tf_op jit(solution)/shard_map/pack_weights/pallas_call | solution.py:52
  30.3 3.4 %collective-permute-done.7.refs_4_ = bf16[64,4224]{1,0:T(8,128)(2,1)S(1)} collective-permute-done((bf16[64,4224]{1,0:T(8,128)(2,1)}, bf16[64,4224]{1,0:T(8,128)(2,1)S(1)}, u32[]{:S(2)}, u32[]{:S(2)}) %collective-permute-start.7) | collective-permute-done | bytes 540704 | tf_op jit(solution)/shard_map/ppermute | solution.py:43
  33.8 1.2 %collective-permute-done.1.refs_3_ = bf16[64,4224]{1,0:T(8,128)(2,1)S(1)} collective-permute-done((bf16[64,4224]{1,0:T(8,128)(2,1)}, bf16[64,4224]{1,0:T(8,128)(2,1)S(1)}, u32[]{:S(2)}, u32[]{:S(2)}) %collective-permute-start.1) | collective-permute-done | bytes 540704 | tf_op jit(solution)/shard_map/ppermute | solution.py:43
  35.0 0.5 collective-permute-start.5
  35.5 1.5 %collective-permute-start.9 = (bf16[64,4224]{1,0:T(8,128)(2,1)S(1)}, bf16[64,4224]{1,0:T(8,128)(2,1)S(1)}, u32[]{:S(2)}, u32[]{:S(2)}) collective-permute-start(bf16[64,4224]{1,0:T(8,128)(2,1)S(1)} %collective-permute-done.7.refs_4_), channel_id=1, source_target_pairs={{0,2},{1,3},{4,0},{5,1},{8,4},{9,5},{12,8},{13,9},{14,12},{15,13},... | collective-permute-start | bytes 1622024 | tf_op jit(solution)/shard_map/ppermute | solution.py:43
  37.0 8.5 %expert_chunk.3 = (bf16[64,4096]{1,0:T(8,128)(2,1)S(1)}, bf16[64,4096]{1,0:T(8,128)(2,1)S(1)}, bf16[64,4096]{1,0:T(8,128)(2,1)S(1)}, bf16[64,4096]{1,0:T(8,128)(...) custom-call(bf16[64,4224]{1,0:T(8,128)(2,1)} %pack_block.1.refs_0_, ...), custom_call_target="tpu_custom_call" | custom-call | flops 6039797760 | bytes 29557288 | tf_op jit(solution)/shard_map/expert_chunk/pallas_call | solution.py:52
  45.5 2.6 %collective-permute-done.9.refs_1_ = bf16[64,4224]{1,0:T(8,128)(2,1)S(1)} collective-permute-done((bf16[64,4224]{1,0:T(8,128)(2,1)S(1)}, bf16[64,4224]{1,0:T(8,128)(2,1)S(1)}, u32[]{:S(2)}, u32[]{:S(2)}) %collective-permute-start.9) | collective-permute-done | bytes 540704 | tf_op jit(solution)/shard_map/ppermute | solution.py:43
  48.1 1.4 %collective-permute-start.10 = (bf16[32,4224]{1,0:T(8,128)(2,1)S(1)}, bf16[32,4224]{1,0:T(8,128)(2,1)S(1)}, u32[]{:S(2)}, u32[]{:S(2)}) collective-permute-start(bf16[32,4224]{1,0:T(8,128)(2,1)S(1)} %slice.7), channel_id=1, source_target_pairs={{0,2},{1,3},{4,0},{5,1},{8,4},{9,5},{12,8},{13,9},{14,12},{15,13},... | collective-permute-start | bytes 811016 | tf_op jit(solution)/shard_map/ppermute | solution.py:43
  49.5 0.7 collective-permute-start.8
  50.2 3.4 %expert_chunk.4 = (bf16[64,4096]{1,0:T(8,128)(2,1)S(1)}, bf16[64,4096]{1,0:T(8,128)(2,1)S(1)}, bf16[128,384]{1,0:T(8,128)(2,1)S(1)}, bf16[128,384]{1,0:T(8,128)(...) custom-call(bf16[64,4224]{1,0:T(8,128)(2,1)S(1)} %collective-permute, ...), custom_call_target="tpu_custom_call" | custom-call | flops 2415919104 | bytes 23953960 | tf_op jit(solution)/shard_map/expert_chunk/pallas_call | solution.py:52
  53.7 1.0 collective-permute-done.10.refs_1_
  54.6 1.3 %collective-permute-done.8.refs_0_ = bf16[32,4224]{1,0:T(8,128)(2,1)S(1)} collective-permute-done((bf16[32,4224]{1,0:T(8,128)(2,1)S(1)}, bf16[32,4224]{1,0:T(8,128)(2,1)S(1)}, u32[]{:S(2)}, u32[]{:S(2)}) %collective-permute-start.8) | collective-permute-done | bytes 270368 | tf_op jit(solution)/shard_map/ppermute | solution.py:43
  55.9 4.1 %expert_chunk.5 = (bf16[32,4096]{1,0:T(8,128)(2,1)S(1)}, bf16[32,4096]{1,0:T(8,128)(2,1)S(1)}, bf16[64,384]{1,0:T(8,128)(2,1)S(1)}, bf16[64,384]{1,0:T(8,128)(2,...) custom-call(bf16[32,4224]{1,0:T(8,128)(2,1)S(1)} %collective-permute, ...), custom_call_target="tpu_custom_call" | custom-call | flops 1207959552 | bytes 21627432 | tf_op jit(solution)/shard_map/expert_chunk/pallas_call | solution.py:52
  60.0 0.2 first_messages.1
  60.2 1.6 %collective-permute-start.15 = (bf16[32,4224]{1,0:T(8,128)(2,1)S(1)}, bf16[32,4224]{1,0:T(8,128)(2,1)S(1)}, u32[]{:S(2)}, u32[]{:S(2)}) collective-permute-start(bf16[32,4224]{1,0:T(8,128)(2,1)S(1)} %get-tuple-element.97), channel_id=1, source_target_pairs={{0,2},{1,3},{4,0},{5,1},{8,4},{9,5},{12,8},{13,9},{14,12},{15,13},... | collective-permute-start | bytes 811016 | tf_op jit(solution)/shard_map/ppermute | solution.py:43
  61.8 0.4 collective-permute-start.11
  62.2 3.6 %collective-permute-start.12 = (bf16[32,128]{1,0:T(8,128)(2,1)S(1)}, bf16[32,128]{1,0:T(8,128)(2,1)S(1)}, u32[]{:S(2)}, u32[]{:S(2)}) collective-permute-start(bf16[32,128]{1,0:T(8,128)(2,1)S(1)} %get-tuple-element.85.refs_10_), channel_id=1, source_target_pairs={{0,14},{1,15},{4,10},{5,11},{8,6},{9,7},{12,2},{13,3},{14,0},{15,1... | collective-permute-start | bytes 24584 | tf_op jit(solution)/shard_map/ppermute | solution.py:43
  65.9 5.9 %collective-permute-done.12.refs_0_.refs_6_ = bf16[32,128]{1,0:T(8,128)(2,1)S(1)} collective-permute-done((bf16[32,128]{1,0:T(8,128)(2,1)S(1)}, bf16[32,128]{1,0:T(8,128)(2,1)S(1)}, u32[]{:S(2)}, u32[]{:S(2)}) %collective-permute-start.12) | collective-permute-done | bytes 8224 | tf_op jit(solution)/shard_map/ppermute | solution.py:43
  71.9 2.1 %collective-permute-start.13 = (bf16[64,4224]{1,0:T(8,128)(2,1)S(1)}, bf16[64,4224]{1,0:T(8,128)(2,1)S(1)}, u32[]{:S(2)}, u32[]{:S(2)}) collective-permute-start(bf16[64,4224]{1,0:T(8,128)(2,1)S(1)} %next_message.6.refs_12_), channel_id=1, source_target_pairs={{0,4},{1,5},{4,8},{5,9},{8,12},{9,13},{12,14},{13,15},{14,10},{15,... | collective-permute-start | bytes 1622024 | tf_op jit(solution)/shard_map/ppermute | solution.py:43
  74.0 3.3 %weight_parts.3 = (bf16[1024,384]{1,0:T(8,128)(2,1)S(1)}, bf16[1024,384]{1,0:T(8,128)(2,1)S(1)}, bf16[384,1024]{1,0:T(8,128)(2,1)S(1)}, f32[8,128]{1,0:T(8,128)S(1)}) custom-call(bf16[320,4224]{1,0:T(8,128)(2,1)S(1)} %get-tuple-element.88.refs_0_.refs_3_, bf16[128,4224]{1,0:T(8,128)(2,1)S(1)} %get-tuple-element.89.refs_1_.refs_4_, ...), custom_call_target="tpu_custom_call" | custom-call | flops 1207959552 | bytes 13275136 | tf_op jit(solution)/shard_map/weight_parts/pallas_call | solution.py:52
  77.3 4.2 %collective-permute-done.17.got_ref.refs_8_ = bf16[64,4224]{1,0:T(8,128)(2,1)S(1)} collective-permute-done((bf16[64,4224]{1,0:T(8,128)(2,1)S(1)}, bf16[64,4224]{1,0:T(8,128)(2,1)S(1)}, u32[]{:S(2)}, u32[]{:S(2)}) %collective-permute-start.17) | collective-permute-done | bytes 540704 | tf_op jit(solution)/shard_map/ppermute | solution.py:43
  82.0 2.1 %collective-permute-start.14 = (bf16[64,4224]{1,0:T(8,128)(2,1)S(1)}, bf16[64,4224]{1,0:T(8,128)(2,1)S(1)}, u32[]{:S(2)}, u32[]{:S(2)}) collective-permute-start(bf16[64,4224]{1,0:T(8,128)(2,1)S(1)} %next_message.7), channel_id=1, source_target_pairs={{0,4},{1,5},{4,8},{5,9},{8,12},{9,13},{12,14},{13,15},{14,10},{15,... | collective-permute-start | bytes 1622024 | tf_op jit(solution)/shard_map/ppermute | solution.py:43
  84.1 0.5 collective-permute-start.22
  84.6 3.3 %weight_parts.4 = (bf16[1024,384]{1,0:T(8,128)(2,1)S(1)}, bf16[1024,384]{1,0:T(8,128)(2,1)S(1)}, bf16[384,1024]{1,0:T(8,128)(2,1)S(1)}, f32[8,128]{1,0:T(8,128)S(1)}) custom-call(bf16[320,4224]{1,0:T(8,128)(2,1)S(1)} %get-tuple-element.88.refs_0_.refs_3_, bf16[128,4224]{1,0:T(8,128)(2,1)S(1)} %get-tuple-element.89.refs_1_.refs_4_, ...), custom_call_target="tpu_custom_call" | custom-call | flops 1207959552 | bytes 13275136 | tf_op jit(solution)/shard_map/weight_parts/pallas_call | solution.py:52
  88.0 4.8 %collective-permute-done.18.got_ref.refs_7_ = bf16[64,4224]{1,0:T(8,128)(2,1)S(1)} collective-permute-done((bf16[64,4224]{1,0:T(8,128)(2,1)S(1)}, bf16[64,4224]{1,0:T(8,128)(2,1)S(1)}, u32[]{:S(2)}, u32[]{:S(2)}) %collective-permute-start.18) | collective-permute-done | bytes 540704 | tf_op jit(solution)/shard_map/ppermute | solution.py:43
  92.8 0.1 collective-permute-done.14.got_ref.refs_5_
  92.9 0.4 collective-permute-start.25
  93.4 0.1 next_message.9.refs_12_
  93.6 2.0 %collective-permute-start.16 = (bf16[64,4224]{1,0:T(8,128)(2,1)S(1)}, bf16[64,4224]{1,0:T(8,128)(2,1)S(1)}, u32[]{:S(2)}, u32[]{:S(2)}) collective-permute-start(bf16[64,4224]{1,0:T(8,128)(2,1)S(1)} %next_message.9.refs_12_), channel_id=1, source_target_pairs={{0,4},{1,5},{4,8},{5,9},{8,12},{9,13},{12,14},{13,15},{14,10},{15,... | collective-permute-start | bytes 1622024 | tf_op jit(solution)/shard_map/ppermute | solution.py:43
  95.7 0.5 collective-permute-done.25.refs_19_
  96.2 7.4 %weight_parts.5 = (bf16[1,2048,384]{2,1,0:T(8,128)(2,1)}, bf16[1,2048,384]{2,1,0:T(8,128)(2,1)}, bf16[1,384,2048]{2,1,0:T(8,128)(2,1)}, f32[8,128]{1,0:T(8,128)S(1)}) custom-call(bf16[320,4224]{1,0:T(8,128)(2,1)S(1)} %get-tuple-element.88.refs_0_.refs_3_, bf16[128,4224]{1,0:T(8,128)(2,1)S(1)} %get-tuple-element.89.refs_1_.refs_4_, ...), custom_call_target="tpu_custom_call" | custom-call | flops 2415919104 | bytes 20353024 | tf_op jit(solution)/shard_map/weight_parts/pallas_call | solution.py:52
  103.6 2.3 %router_parts.1 = (bf16[64,128]{1,0:T(8,128)(2,1)S(1)}, f32[8,128]{1,0:T(8,128)S(1)}, f32[8,128]{1,0:T(8,128)S(1)}) custom-call(s32[10]{0:T(128)S(1)} %pad_add_fusion.refs_11_.refs_8_.where_ref, bf16[320,256]{1,0:T(8,128)(2,1)S(1)} %get-tuple-element.104.refs_0_, bf16[128,256]{1,0:T(8,128)(2,1)S(1)} %get-tuple-element.105.refs_1_, ...), custom_call_target="tpu_custom_call" | custom-call | flops 10000000 | bytes 1000000 | tf_op jit(solution)/shard_map/router_parts/pallas_call | solution.py:452
  106.0 0.2 collective-permute-start.26
  106.2 1.0 collective-permute-done.26
  107.2 0.6 add_bitcast_fusion
  107.8 0.2 collective-permute-done.16.up_ref
  108.0 1.9 %collective-permute-done.19.down_ref = bf16[64,4224]{1,0:T(8,128)(2,1)S(1)} collective-permute-done((bf16[64,4224]{1,0:T(8,128)(2,1)S(1)}, bf16[64,4224]{1,0:T(8,128)(2,1)S(1)}, u32[]{:S(2)}, u32[]{:S(2)}) %collective-permute-start.19) | collective-permute-done | bytes 540704 | tf_op jit(solution)/shard_map/ppermute | solution.py:43
  109.9 1.1 %last_sums.1 = (bf16[64,2048]{1,0:T(8,128)(2,1)}, bf16[64,2048]{1,0:T(8,128)(2,1)}) custom-call(bf16[64,4224]{1,0:T(8,128)(2,1)S(1)} %collective-permute-done.16.up_ref, bf16[64,4224]{1,0:T(8,128)(2,1)S(1)} %collective-permute-done.19.down_ref, bf16[64,4096]{1,0:T(8,128)(2,1)S(1)} %get-tuple-element.103.made_ref, ...), custom_call_target="tpu_custom_call" | custom-call | bytes 2670592 | tf_op jit(solution)/shard_map/last_sums/pallas_call | solution.py:52
  (41 shorter events, 1.3 us)
Async XLA Ops:
  0.6 21.0 %copy-start = (bf16[2048,8]{0,1:T(8,128)(2,1)S(1)}, bf16[2048,8]{0,1:T(8,128)(2,1)}, u32[]{:S(2)}) copy-start(bf16[2048,8]{0,1:T(8,128)(2,1)} %param.10) | copy-start | bytes 98308
  0.6 21.4 %copy-start.2 = (bf16[1,2048,384]{2,1,0:T(8,128)(2,1)S(1)}, bf16[1,2048,384]{2,1,0:T(8,128)(2,1)}, u32[]{:S(2)}) copy-start(bf16[1,2048,384]{2,1,0:T(8,128)(2,1)} %param.11) | copy-start | bytes 4718596
  2.7 19.3 %collective-permute-start.2 = (bf16[2048,384]{1,0:T(8,128)(2,1)}, bf16[2048,384]{1,0:T(8,128)(2,1)S(1)}, u32[]{:S(2)}, u32[]{:S(2)}) collective-permute-start(bf16[2048,384]{1,0:T(8,128)(2,1)} %bitcast.13), channel_id=1, source_target_pairs={{0,1},{1,0},{2,3},{3,2},{4,5},{5,4},{6,7},{7,6},{8,9},{9,8},{10,11... | collective-permute-start | bytes 4718600 | tf_op jit(solution)/shard_map/ppermute | solution.py:15
  3.2 18.8 %collective-permute-start.3 = (bf16[2048,384]{1,0:T(8,128)(2,1)}, bf16[2048,384]{1,0:T(8,128)(2,1)}, u32[]{:S(2)}, u32[]{:S(2)}) collective-permute-start(bf16[2048,384]{1,0:T(8,128)(2,1)} %bitcast.15), channel_id=1, source_target_pairs={{0,1},{1,0},{2,3},{3,2},{4,5},{5,4},{6,7},{7,6},{8,9},{9,8},{10,11... | collective-permute-start | bytes 4718600 | tf_op jit(solution)/shard_map/ppermute | solution.py:15
  3.3 18.8 %collective-permute-start.4 = (bf16[384,2048]{1,0:T(8,128)(2,1)}, bf16[384,2048]{1,0:T(8,128)(2,1)}, u32[]{:S(2)}, u32[]{:S(2)}) collective-permute-start(bf16[384,2048]{1,0:T(8,128)(2,1)} %bitcast.17), channel_id=1, source_target_pairs={{0,1},{1,0},{2,3},{3,2},{4,5},{5,4},{6,7},{7,6},{8,9},{9,8},{10,11... | collective-permute-start | bytes 4718600 | tf_op jit(solution)/shard_map/ppermute | solution.py:15
  3.7 15.8 %collective-permute-start.6 = (bf16[64,4224]{1,0:T(8,128)(2,1)}, bf16[64,4224]{1,0:T(8,128)(2,1)}, u32[]{:S(2)}, u32[]{:S(2)}) collective-permute-start(bf16[64,4224]{1,0:T(8,128)(2,1)} %pack_block.1.refs_0_), channel_id=1, source_target_pairs={{0,2},{1,3},{4,0},{5,1},{8,4},{9,5},{12,8},{13,9},{14,12},{15,13},... | collective-permute-start | bytes 1622024 | tf_op jit(solution)/shard_map/ppermute | solution.py:43
  6.3 14.9 %collective-permute-start = (bf16[64,4224]{1,0:T(8,128)(2,1)}, bf16[64,4224]{1,0:T(8,128)(2,1)}, u32[]{:S(2)}, u32[]{:S(2)}) collective-permute-start(bf16[64,4224]{1,0:T(8,128)(2,1)} %pack_block.1.refs_0_), channel_id=1, source_target_pairs={{0,4},{1,5},{4,8},{5,9},{8,12},{9,13},{12,14},{13,15},{14,10},{15,... | collective-permute-start | bytes 1622024 | tf_op jit(solution)/shard_map/ppermute | solution.py:43
  19.5 14.2 %collective-permute-start.7 = (bf16[64,4224]{1,0:T(8,128)(2,1)}, bf16[64,4224]{1,0:T(8,128)(2,1)S(1)}, u32[]{:S(2)}, u32[]{:S(2)}) collective-permute-start(bf16[64,4224]{1,0:T(8,128)(2,1)} %collective-permute-done.6.refs_2_), channel_id=1, source_target_pairs={{0,2},{1,3},{4,0},{5,1},{8,4},{9,5},{12,8},{13,9},{14,12},{15,13},... | collective-permute-start | bytes 1622024 | tf_op jit(solution)/shard_map/ppermute | solution.py:43
  21.2 13.8 %collective-permute-start.1 = (bf16[64,4224]{1,0:T(8,128)(2,1)}, bf16[64,4224]{1,0:T(8,128)(2,1)S(1)}, u32[]{:S(2)}, u32[]{:S(2)}) collective-permute-start(bf16[64,4224]{1,0:T(8,128)(2,1)} %collective-permute-done.refs_1_), channel_id=1, source_target_pairs={{0,4},{1,5},{4,8},{5,9},{8,12},{9,13},{12,14},{13,15},{14,10},{15,... | collective-permute-start | bytes 1622024 | tf_op jit(solution)/shard_map/ppermute | solution.py:43
  22.0 1.4 %copy-start.3 = (bf16[1,2048,384]{2,1,0:T(8,128)(2,1)S(1)}, bf16[1,2048,384]{2,1,0:T(8,128)(2,1)}, u32[]{:S(2)}) copy-start(bf16[1,2048,384]{2,1,0:T(8,128)(2,1)} %param.12) | copy-start | bytes 4718596
  23.5 1.4 %copy-start.4 = (bf16[1,384,2048]{2,1,0:T(8,128)(2,1)S(1)}, bf16[1,384,2048]{2,1,0:T(8,128)(2,1)}, u32[]{:S(2)}) copy-start(bf16[1,384,2048]{2,1,0:T(8,128)(2,1)} %param.13) | copy-start | bytes 4718596
  35.0 13.1 %collective-permute-start.5 = (bf16[64,4224]{1,0:T(8,128)(2,1)S(1)}, bf16[64,4224]{1,0:T(8,128)(2,1)S(1)}, u32[]{:S(2)}, u32[]{:S(2)}) collective-permute-start(bf16[64,4224]{1,0:T(8,128)(2,1)S(1)} %collective-permute-done.1.refs_3_), channel_id=1, source_target_pairs={{0,4},{1,5},{4,8},{5,9},{8,12},{9,13},{12,14},{13,15},{14,10},{15,... | collective-permute-start | bytes 1622024 | tf_op jit(solution)/shard_map/ppermute | solution.py:43
  35.5 12.6 %collective-permute-start.9 = (bf16[64,4224]{1,0:T(8,128)(2,1)S(1)}, bf16[64,4224]{1,0:T(8,128)(2,1)S(1)}, u32[]{:S(2)}, u32[]{:S(2)}) collective-permute-start(bf16[64,4224]{1,0:T(8,128)(2,1)S(1)} %collective-permute-done.7.refs_4_), channel_id=1, source_target_pairs={{0,2},{1,3},{4,0},{5,1},{8,4},{9,5},{12,8},{13,9},{14,12},{15,13},... | collective-permute-start | bytes 1622024 | tf_op jit(solution)/shard_map/ppermute | solution.py:43
  48.1 6.5 %collective-permute-start.10 = (bf16[32,4224]{1,0:T(8,128)(2,1)S(1)}, bf16[32,4224]{1,0:T(8,128)(2,1)S(1)}, u32[]{:S(2)}, u32[]{:S(2)}) collective-permute-start(bf16[32,4224]{1,0:T(8,128)(2,1)S(1)} %slice.7), channel_id=1, source_target_pairs={{0,2},{1,3},{4,0},{5,1},{8,4},{9,5},{12,8},{13,9},{14,12},{15,13},... | collective-permute-start | bytes 811016 | tf_op jit(solution)/shard_map/ppermute | solution.py:43
  49.5 6.5 %collective-permute-start.8 = (bf16[32,4224]{1,0:T(8,128)(2,1)S(1)}, bf16[32,4224]{1,0:T(8,128)(2,1)S(1)}, u32[]{:S(2)}, u32[]{:S(2)}) collective-permute-start(bf16[32,4224]{1,0:T(8,128)(2,1)S(1)} %slice.6), channel_id=1, source_target_pairs={{0,4},{1,5},{4,8},{5,9},{8,12},{9,13},{12,14},{13,15},{14,10},{15,... | collective-permute-start | bytes 811016 | tf_op jit(solution)/shard_map/ppermute | solution.py:43
  60.2 11.5 %collective-permute-start.15 = (bf16[32,4224]{1,0:T(8,128)(2,1)S(1)}, bf16[32,4224]{1,0:T(8,128)(2,1)S(1)}, u32[]{:S(2)}, u32[]{:S(2)}) collective-permute-start(bf16[32,4224]{1,0:T(8,128)(2,1)S(1)} %get-tuple-element.97), channel_id=1, source_target_pairs={{0,2},{1,3},{4,0},{5,1},{8,4},{9,5},{12,8},{13,9},{14,12},{15,13},... | collective-permute-start | bytes 811016 | tf_op jit(solution)/shard_map/ppermute | solution.py:43
  61.8 10.1 %collective-permute-start.11 = (bf16[32,4224]{1,0:T(8,128)(2,1)S(1)}, bf16[32,4224]{1,0:T(8,128)(2,1)S(1)}, u32[]{:S(2)}, u32[]{:S(2)}) collective-permute-start(bf16[32,4224]{1,0:T(8,128)(2,1)S(1)} %get-tuple-element.83), channel_id=1, source_target_pairs={{0,4},{1,5},{4,8},{5,9},{8,12},{9,13},{12,14},{13,15},{14,10},{15,... | collective-permute-start | bytes 811016 | tf_op jit(solution)/shard_map/ppermute | solution.py:43
  62.2 9.5 %collective-permute-start.12 = (bf16[32,128]{1,0:T(8,128)(2,1)S(1)}, bf16[32,128]{1,0:T(8,128)(2,1)S(1)}, u32[]{:S(2)}, u32[]{:S(2)}) collective-permute-start(bf16[32,128]{1,0:T(8,128)(2,1)S(1)} %get-tuple-element.85.refs_10_), channel_id=1, source_target_pairs={{0,14},{1,15},{4,10},{5,11},{8,6},{9,7},{12,2},{13,3},{14,0},{15,1... | collective-permute-start | bytes 24584 | tf_op jit(solution)/shard_map/ppermute | solution.py:43
  71.8 9.7 %collective-permute-start.17 = (bf16[64,4224]{1,0:T(8,128)(2,1)S(1)}, bf16[64,4224]{1,0:T(8,128)(2,1)S(1)}, u32[]{:S(2)}, u32[]{:S(2)}) collective-permute-start(bf16[64,4224]{1,0:T(8,128)(2,1)S(1)} %next_message.8.refs_13_), channel_id=1, source_target_pairs={{0,2},{1,3},{4,0},{5,1},{8,4},{9,5},{12,8},{13,9},{14,12},{15,13},... | collective-permute-start | bytes 1622024 | tf_op jit(solution)/shard_map/ppermute | solution.py:43
  71.9 9.9 %collective-permute-start.13 = (bf16[64,4224]{1,0:T(8,128)(2,1)S(1)}, bf16[64,4224]{1,0:T(8,128)(2,1)S(1)}, u32[]{:S(2)}, u32[]{:S(2)}) collective-permute-start(bf16[64,4224]{1,0:T(8,128)(2,1)S(1)} %next_message.6.refs_12_), channel_id=1, source_target_pairs={{0,4},{1,5},{4,8},{5,9},{8,12},{9,13},{12,14},{13,15},{14,10},{15,... | collective-permute-start | bytes 1622024 | tf_op jit(solution)/shard_map/ppermute | solution.py:43
  77.3 10.6 %collective-permute-start.20 = (bf16[1024,384]{1,0:T(8,128)(2,1)S(1)}, bf16[1024,384]{1,0:T(8,128)(2,1)S(1)}, u32[]{:S(2)}, u32[]{:S(2)}) collective-permute-start(bf16[1024,384]{1,0:T(8,128)(2,1)S(1)} %get-tuple-element.113), channel_id=1, source_target_pairs={{0,1},{1,0},{2,3},{3,2},{4,5},{5,4},{6,7},{7,6},{8,9},{9,8},{10,11... | collective-permute-start | bytes 2359304 | tf_op jit(solution)/shard_map/ppermute | solution.py:15
  81.7 11.1 %collective-permute-start.18 = (bf16[64,4224]{1,0:T(8,128)(2,1)S(1)}, bf16[64,4224]{1,0:T(8,128)(2,1)S(1)}, u32[]{:S(2)}, u32[]{:S(2)}) collective-permute-start(bf16[64,4224]{1,0:T(8,128)(2,1)S(1)} %next_message.10), channel_id=1, source_target_pairs={{0,2},{1,3},{4,0},{5,1},{8,4},{9,5},{12,8},{13,9},{14,12},{15,13},... | collective-permute-start | bytes 1622024 | tf_op jit(solution)/shard_map/ppermute | solution.py:43
  82.0 11.0 %collective-permute-start.14 = (bf16[64,4224]{1,0:T(8,128)(2,1)S(1)}, bf16[64,4224]{1,0:T(8,128)(2,1)S(1)}, u32[]{:S(2)}, u32[]{:S(2)}) collective-permute-start(bf16[64,4224]{1,0:T(8,128)(2,1)S(1)} %next_message.7), channel_id=1, source_target_pairs={{0,4},{1,5},{4,8},{5,9},{8,12},{9,13},{12,14},{13,15},{14,10},{15,... | collective-permute-start | bytes 1622024 | tf_op jit(solution)/shard_map/ppermute | solution.py:43
  84.1 9.5 %collective-permute-start.21 = (bf16[1024,384]{1,0:T(8,128)(2,1)S(1)}, bf16[1024,384]{1,0:T(8,128)(2,1)S(1)}, u32[]{:S(2)}, u32[]{:S(2)}) collective-permute-start(bf16[1024,384]{1,0:T(8,128)(2,1)S(1)} %get-tuple-element.114), channel_id=1, source_target_pairs={{0,1},{1,0},{2,3},{3,2},{4,5},{5,4},{6,7},{7,6},{8,9},{9,8},{10,11... | collective-permute-start | bytes 2359304 | tf_op jit(solution)/shard_map/ppermute | solution.py:15
  84.1 11.5 %collective-permute-start.22 = (bf16[384,1024]{1,0:T(8,128)(2,1)S(1)}, bf16[384,1024]{1,0:T(8,128)(2,1)S(1)}, u32[]{:S(2)}, u32[]{:S(2)}) collective-permute-start(bf16[384,1024]{1,0:T(8,128)(2,1)S(1)} %get-tuple-element.115), channel_id=1, source_target_pairs={{0,1},{1,0},{2,3},{3,2},{4,5},{5,4},{6,7},{7,6},{8,9},{9,8},{10,11... | collective-permute-start | bytes 2359304 | tf_op jit(solution)/shard_map/ppermute | solution.py:15
  87.9 7.8 %collective-permute-start.23 = (bf16[1024,384]{1,0:T(8,128)(2,1)S(1)}, bf16[1024,384]{1,0:T(8,128)(2,1)S(1)}, u32[]{:S(2)}, u32[]{:S(2)}) collective-permute-start(bf16[1024,384]{1,0:T(8,128)(2,1)S(1)} %get-tuple-element.116), channel_id=1, source_target_pairs={{0,1},{1,0},{2,3},{3,2},{4,5},{5,4},{6,7},{7,6},{8,9},{9,8},{10,11... | collective-permute-start | bytes 2359304 | tf_op jit(solution)/shard_map/ppermute | solution.py:15
  92.8 2.9 %collective-permute-start.24 = (bf16[1024,384]{1,0:T(8,128)(2,1)S(1)}, bf16[1024,384]{1,0:T(8,128)(2,1)S(1)}, u32[]{:S(2)}, u32[]{:S(2)}) collective-permute-start(bf16[1024,384]{1,0:T(8,128)(2,1)S(1)} %get-tuple-element.117), channel_id=1, source_target_pairs={{0,1},{1,0},{2,3},{3,2},{4,5},{5,4},{6,7},{7,6},{8,9},{9,8},{10,11... | collective-permute-start | bytes 2359304 | tf_op jit(solution)/shard_map/ppermute | solution.py:15
  92.9 3.3 %collective-permute-start.25 = (bf16[384,1024]{1,0:T(8,128)(2,1)S(1)}, bf16[384,1024]{1,0:T(8,128)(2,1)S(1)}, u32[]{:S(2)}, u32[]{:S(2)}) collective-permute-start(bf16[384,1024]{1,0:T(8,128)(2,1)S(1)} %get-tuple-element.118), channel_id=1, source_target_pairs={{0,1},{1,0},{2,3},{3,2},{4,5},{5,4},{6,7},{7,6},{8,9},{9,8},{10,11... | collective-permute-start | bytes 2359304 | tf_op jit(solution)/shard_map/ppermute | solution.py:15
  93.6 14.4 %collective-permute-start.16 = (bf16[64,4224]{1,0:T(8,128)(2,1)S(1)}, bf16[64,4224]{1,0:T(8,128)(2,1)S(1)}, u32[]{:S(2)}, u32[]{:S(2)}) collective-permute-start(bf16[64,4224]{1,0:T(8,128)(2,1)S(1)} %next_message.9.refs_12_), channel_id=1, source_target_pairs={{0,4},{1,5},{4,8},{5,9},{8,12},{9,13},{12,14},{13,15},{14,10},{15,... | collective-permute-start | bytes 1622024 | tf_op jit(solution)/shard_map/ppermute | solution.py:43
  95.6 14.3 %collective-permute-start.19 = (bf16[64,4224]{1,0:T(8,128)(2,1)S(1)}, bf16[64,4224]{1,0:T(8,128)(2,1)S(1)}, u32[]{:S(2)}, u32[]{:S(2)}) collective-permute-start(bf16[64,4224]{1,0:T(8,128)(2,1)S(1)} %next_message.11.refs_13_), channel_id=1, source_target_pairs={{0,2},{1,3},{4,0},{5,1},{8,4},{9,5},{12,8},{13,9},{14,12},{15,13},... | collective-permute-start | bytes 1622024 | tf_op jit(solution)/shard_map/ppermute | solution.py:43
  103.6 7.4 %copy-start.1 = (bf16[2048,8]{0,1:T(8,128)(2,1)S(1)}, bf16[2048,8]{0,1:T(8,128)(2,1)}, u32[]{:S(2)}) copy-start(bf16[2048,8]{0,1:T(8,128)(2,1)} %param.10) | copy-start | bytes 98308
  106.0 1.2 %collective-permute-start.26 = (f32[8,128]{1,0:T(8,128)S(1)}, f32[8,128]{1,0:T(8,128)S(1)}, u32[]{:S(2)}, u32[]{:S(2)}) collective-permute-start(f32[8,128]{1,0:T(8,128)S(1)} %get-tuple-element.127), channel_id=1, source_target_pairs={{0,1},{1,0},{2,3},{3,2},{4,5},{5,4},{6,7},{7,6},{8,9},{9,8},{10,11... | collective-permute-start | bytes 12296 | tf_op jit(solution)/shard_map/ppermute | solution.py:15
